TPU v7x, 256 devices: a whole 4x4x8 slice. The times are simulated.
256 devices in a mesh: rec: 16 (over z, core), tm: 16 (over y, x).
Axes of the slice: x: 4, y: 4, z: 8, core: 2. Of those that a mesh axis runs over, the one named last changes fastest.
Arguments:
- frames: bfloat16 [65536, 1280], P(('rec', 'tm')), parts along dimension 0, may hold values from -50 to 50
- w_query: bfloat16 [1280, 1280], replicated, may hold values from -1 to 1
- w_kv: bfloat16 [1280, 2560], replicated, may hold values from -1 to 1
- w_out: bfloat16 [1280, 1280], replicated, may hold values from -0.15625 to 0.15625
- norm_gain: float32 [1280], replicated, may hold values from 0.5 to 1.5
- rand_owner: int32 [512, 3], P(('rec', 'tm')), parts along dimension 0, may hold values from 0 to 15, all different within a row; in each aligned block of 2 rows (0 to 1, 2 to 3, ...) at most 2 rows name the same one
- rand_slot: int32 [512, 3], P(('rec', 'tm')), parts along dimension 0, may hold values from 0 to 1
- global_pos: int32 [2048], P('rec'), parts along dimension 0, may hold values from 0 to 4095
- length: int32 [16], P('rec'), parts along dimension 0, may hold values from 16 to 32
Outputs:
- pooled_out: bfloat16 [16384, 1280], P(('rec', 'tm')), parts along dimension 0
There are 16 independent parts, one for each index of `rec`. A program takes and returns all parts, laid end to end along the dimension named above; an argument that names none is the same for every part. Nothing has to cross between parts.
Inputs may be any that keep to these rules, and one draw needn't show every extreme that they name: `rand_owner`: the 3 owners of one query block differ; over the query blocks of one time shard no owner is named more than 2 times, a bound that some block reaches.
All inputs are finite; a program needn't handle non-finite values.
Results may differ from a plain program's by a relative error of at most 0.012.
The roundings to bfloat16 on the way count: a program that leaves them out, or rounds other values in their place, can miss the bound.
Values may be sent and summed in bfloat16 or wider, within the bound.
No kernel may reach another device: no remote copies, remote signals or barrier semaphores. Data moves between devices by JAX's collectives and lax.ppermute only.
A program may use at most 128 MiB of HBM per device.

v0:
```python
import math

import jax
import jax.numpy as jnp
from jax import lax
from jax.sharding import PartitionSpec as P

HEADS = 20
BLOCK = 128
POOL = 4


def with_halo(value, sides, width):
    for axis, dim in sides:
        size, length = (lax.axis_size(axis), value.shape[dim])
        up = [(i, (i + 1) % size) for i in range(size - 1)]
        down = [(j, i) for i, j in up]
        last = lax.slice_in_dim(value, length - width, length, axis=dim)
        leading = lax.slice_in_dim(value, 0, width, axis=dim)
        before = lax.ppermute(last, axis, up)
        after = lax.ppermute(leading, axis, down)
        value = jnp.concatenate([before, value, after], axis=dim)
    return value


def attend(query_rows, key_rows, key_live, global_keys, global_live, head_count):
    group_size, block_rows, model_width = query_rows.shape
    head_size = model_width // head_count
    score_scale = head_size ** (-0.5)
    query_h = query_rows.reshape(group_size, block_rows, head_count, head_size)
    key_h = key_rows[..., :model_width].reshape(group_size, -1, head_count, head_size)
    value_h = key_rows[..., model_width:].reshape(group_size, -1, head_count, head_size)
    global_key_h = global_keys[:, :model_width].reshape(-1, head_count, head_size)
    global_value_h = global_keys[:, model_width:].reshape(-1, head_count, head_size)
    near_scores = (
        jnp.einsum("bihd,bjhd->bhij", query_h, key_h, preferred_element_type=jnp.float32)
        * score_scale
    )
    far_scores = (
        jnp.einsum("bihd,jhd->bhij", query_h, global_key_h, preferred_element_type=jnp.float32)
        * score_scale
    )
    near_scores = jnp.where(key_live[:, None, None, :], near_scores, -1e30)
    far_scores = jnp.where(global_live[None, None, None, :], far_scores, -1e30)
    row_max = jnp.maximum(jnp.max(near_scores, axis=-1), jnp.max(far_scores, axis=-1))[..., None]
    near_exp = jnp.exp(near_scores - row_max)
    far_exp = jnp.exp(far_scores - row_max)
    row_total = jnp.sum(near_exp, axis=-1, keepdims=True) + jnp.sum(far_exp, axis=-1, keepdims=True)
    near_weight = (near_exp / row_total).astype(jnp.bfloat16)
    far_weight = (far_exp / row_total).astype(jnp.bfloat16)
    context = jnp.einsum(
        "bhij,bjhd->bihd", near_weight, value_h, preferred_element_type=jnp.float32
    )
    context = context + jnp.einsum(
        "bhij,jhd->bihd", far_weight, global_value_h, preferred_element_type=jnp.float32
    )
    return context.reshape(group_size, block_rows, model_width).astype(jnp.bfloat16)


def body(frames, w_query, w_kv, w_out, norm_gain, rand_owner, rand_slot, global_pos, length):
    shards = lax.axis_size("tm")
    rank_here = lax.axis_index("tm")
    local_rows, model_width = frames.shape
    qblocks = local_rows // BLOCK
    pick_count = rand_owner.shape[1]
    first_block = rank_here * qblocks
    live_blocks = length[0]
    query_rows = jnp.dot(frames, w_query, preferred_element_type=jnp.float32).astype(jnp.bfloat16)
    keyval = jnp.dot(frames, w_kv, preferred_element_type=jnp.float32).astype(jnp.bfloat16)
    payload_width = keyval.shape[1]
    padded = with_halo(keyval, (("tm", 0),), BLOCK)
    lower_rim = padded[:BLOCK]
    upper_rim = padded[BLOCK + local_rows :]
    extended = jnp.concatenate([lower_rim, keyval, upper_rim], axis=0).reshape(
        qblocks + 2, BLOCK, 2 * model_width
    )
    window_rows = jnp.stack([extended[offset : offset + qblocks] for offset in range(3)], axis=1)
    window_rows = window_rows.reshape(qblocks, 3 * BLOCK, 2 * model_width)
    local_index = global_pos - first_block * BLOCK
    onehot = (local_index[:, None] == jnp.arange(local_rows, dtype=jnp.int32)[None, :]).astype(
        jnp.bfloat16
    )
    picked = jnp.dot(onehot, keyval, preferred_element_type=jnp.float32)
    summed = lax.psum(picked.astype(jnp.bfloat16), "tm")
    global_live = global_pos < live_blocks * BLOCK
    owners = rand_owner.reshape(-1)
    slot_ids = rand_slot.reshape(-1)
    request_count = owners.shape[0]
    capacity = min(qblocks, (pick_count * qblocks + shards - 1) // shards + 1)
    request_index = jnp.arange(request_count, dtype=jnp.int32)
    same_owner = (owners[:, None] == owners[None, :]) & (
        request_index[None, :] < request_index[:, None]
    )
    owner_rank = jnp.sum(same_owner.astype(jnp.int32), axis=1)
    position = owners * capacity + owner_rank
    slot_index = jnp.arange(shards * capacity, dtype=jnp.int32)
    request_table = (
        jnp.sum(
            jnp.where(position[None, :] == slot_index[:, None], slot_ids[None, :] + 1, 0), axis=1
        )
        - 1
    )
    request_table = request_table.reshape(shards, capacity)
    asked_slots = lax.all_to_all(request_table, "tm", split_axis=0, concat_axis=0, tiled=True)
    chosen = jnp.clip(asked_slots.reshape(-1), 0, qblocks - 1)
    reply_blocks = jnp.take(keyval.reshape(qblocks, BLOCK, payload_width), chosen, axis=0)
    reply_blocks = reply_blocks.reshape(shards, capacity, BLOCK, payload_width)
    answered = lax.all_to_all(reply_blocks, "tm", split_axis=0, concat_axis=0, tiled=True)
    fetched = jnp.take(answered.reshape(shards * capacity, BLOCK, payload_width), position, axis=0)
    random_rows = fetched.reshape(-1, payload_width).reshape(
        qblocks, pick_count * BLOCK, 2 * model_width
    )
    key_rows = jnp.concatenate([window_rows, random_rows], axis=1)
    window_ids = (
        first_block
        + jnp.arange(qblocks, dtype=jnp.int32)[:, None]
        - 1
        + jnp.arange(3, dtype=jnp.int32)[None, :]
    )
    block_ids = jnp.concatenate([window_ids, rand_owner * qblocks + rand_slot], axis=1)
    key_live = jnp.repeat((block_ids >= 0) & (block_ids < live_blocks), BLOCK, axis=1)
    group_size = math.gcd(qblocks, max(1, 512 // BLOCK))
    group_count = qblocks // group_size

    def one_group(inputs):
        return attend(inputs[0], inputs[1], inputs[2], summed, global_live, HEADS)

    context = lax.map(
        one_group,
        (
            query_rows.reshape(group_count, group_size, BLOCK, model_width),
            key_rows.reshape(group_count, group_size, -1, 2 * model_width),
            key_live.reshape(group_count, group_size, -1),
        ),
    )
    context = context.reshape(local_rows, model_width)
    projected = jnp.dot(context, w_out, preferred_element_type=jnp.float32)
    pooled = jnp.mean(projected.reshape(local_rows // POOL, POOL, model_width), axis=1)
    feature_mean = jnp.mean(pooled, axis=1, keepdims=True)
    centered = pooled - feature_mean
    feature_var = jnp.mean(centered * centered, axis=1, keepdims=True)
    normed = centered * lax.rsqrt(feature_var + 1e-05) * norm_gain
    row_block = first_block + jnp.arange(local_rows // POOL, dtype=jnp.int32) * POOL // BLOCK
    return jnp.where((row_block < live_blocks)[:, None], normed, 0.0).astype(jnp.bfloat16)


def solution(mesh):
    placed = (
        P(("rec", "tm"), None),
        P(),
        P(),
        P(),
        P(),
        P(("rec", "tm"), None),
        P(("rec", "tm"), None),
        P("rec"),
        P("rec"),
    )
    return jax.shard_map(
        body, mesh=mesh, in_specs=placed, out_specs=P(("rec", "tm"), None), check_vma=False
    )
```

profile of v0, /device:TPU:2, one launch (start us, length us, event | category | flops | bytes accessed | tf_op | source)
XLA Modules:
  0.0 496.8 jit_solution(9559506666457124655)
XLA Ops:
  6.5 0.9 reshape.225
  7.5 0.8 fusion.26
  9.4 7.5 %all-to-all-start = ((s32[16,1,2]{2,1,0:T(1,128)}), s32[16,1,2]{2,1,0:T(1,128)S(1)}, u32[]{:S(2)}, u32[]{:S(2)}) async-start(s32[16,1,2]{2,1,0:T(1,128)} %bitcast.8), calls=%async_computation | async-start | bytes 16384 | tf_op jit(solution)/shard_map/all_to_all | solution.py:104
  16.8 6.0 %convolution_convert_fusion = bf16[256,2560]{1,0:T(8,128)(2,1)} fusion(bf16[256,1280]{1,0:T(8,128)(2,1)} %param.9, bf16[1280,2560]{1,0:T(8,128)(2,1)} %param.11), kind=kOutput, calls=%fused_computation.15 | convolution fusion | flops 1678376960 | bytes 8519680 | tf_op jit(solution)/shard_map/dot_general | solution.py:69
  23.3 9.7 %gather_fusion = bf16[32,128,2560]{2,1,0:T(8,128)(2,1)} fusion(bf16[2,128,2560]{2,1,0:T(8,128)(2,1)} %bitcast.86, s32[1024]{0:T(1024)S(1)} %pad_clamp_fusion.1), kind=kCustom, calls=%fused_computation | custom fusion | bytes 41943168 | tf_op jit(solution)/shard_map/jit(_take)/gather | solution.py:106
  33.0 17.8 %broadcast_select_fusion = bf16[16,2,128,2560]{3,2,1,0:T(8,128)(2,1)} fusion(bf16[16,2,128,2560]{3,2,1,0:T(8,128)(2,1)} %bitcast.88, pred[16,2]{1,0:T(8,128)(4,1)S(1)} %copy.81), kind=kLoop, calls=%fused_computation.2 | loop fusion | flops 10485760 | bytes 41943072 | tf_op jit(solution)/shard_map/jit(_take)/select_n | solution.py:106
  50.9 7.3 %all-to-all-start.1 = ((bf16[16,2,128,2560]{3,2,1,0:T(8,128)(2,1)}), bf16[16,2,128,2560]{3,2,1,0:T(8,128)(2,1)}, u32[]{:S(2)}, u32[]{:S(2)}) async-start(bf16[16,2,128,2560]{3,2,1,0:T(8,128)(2,1)} %broadcast_select_fusion), calls=%async_computation.1 | async-start | bytes 41943040 | tf_op jit(solution)/shard_map/all_to_all | solution.py:108
  58.2 2.4 fusion.28
  60.6 3.4 collective-permute-start
  64.0 3.3 collective-permute-start.1
  67.3 2.5 convolution_convert_fusion.1
  71.0 3.0 convolution_convert_fusion.2
  74.0 1.3 copy.83
  75.5 347.2 %all-reduce.2.cloned.1.call-done = bf16[128,2560]{1,0:T(8,128)(2,1)} async-done(((bf16[128,2560]{1,0:T(8,128)(2,1)}), bf16[128,2560]{1,0:T(8,128)(2,1)}) %all-reduce.2.cloned.1.call-update) | async-done | bytes 655376 | tf_op jit(solution)/shard_map/psum | solution.py:84
  422.7 1.1 fusion.29
  424.0 0.9 copy.91
  424.9 2.2 bitcast_reduce_fusion
  427.2 1.5 pad_maximum_fusion.3
  428.6 2.3 pad_maximum_fusion.1
  430.9 9.7 %gather_fusion.1 = bf16[6,128,2560]{2,1,0:T(8,128)(2,1)} fusion(bf16[32,128,2560]{2,1,0:T(8,128)(2,1)} %bitcast.13, s32[1024]{0:T(1024)S(1)} %pad_clamp_fusion), kind=kCustom, calls=%fused_computation.1 | custom fusion | bytes 7864344 | tf_op jit(solution)/shard_map/jit(_take)/gather | solution.py:109
  440.6 2.7 bitcast_select_fusion
  443.9 3.3 pad_maximum_fusion
  447.3 6.3 %copy.84 = bf16[2,768,1280]{1,2,0:T(8,128)(2,1)} copy(bf16[2,768,1280]{2,1,0:T(8,128)(2,1)} %get-tuple-element.17) | data formatting | bytes 7864320 | tf_op jit(solution)/shard_map/while/body/eval_jaxpr/slice | solution.py:31
  453.6 4.3 fusion
  457.9 3.9 fusion.1
  461.8 1.6 copy-done.3
  463.4 6.4 %copy.82 = bf16[2,768,1280]{1,2,0:T(8,128)(2,1)} copy(bf16[2,768,1280]{2,1,0:T(8,128)(2,1)} %get-tuple-element.18) | data formatting | bytes 7864320 | tf_op jit(solution)/shard_map/while/body/eval_jaxpr/slice | solution.py:32
  470.5 9.0 %fusion.8 = f32[2,128,20,64]{1,3,2,0:T(8,128)S(1)} fusion(bf16[2,768,20,64]{1,3,2,0:T(8,128)(2,1)} %bitcast.94, f32[2,20,128,768]{3,2,1,0:T(8,128)} %copy-done.3, f32[2,20,128]{2,1,0:T(8,128)S(1)} %copy_add_fusion, f32[2,20,128]{2,1,0:T(8,128)S(1)} %copy_maximum_fusion, pred[2,768]{1,0:T(4,128)(4,1)S(1)} %bitcast.99), kind=kOutput, calls=%fused_computation.26 | convolution fusion | flops 522977280 | bytes 21014016 | tf_op jit(solution)/shard_map/while/body/eval_jaxpr/bhij,bjhd->bihd/dot_general | solution.py:51
  479.5 0.9 fusion.10
  480.5 1.7 copy.94
  482.2 3.4 convert_element_type.40
  485.6 3.2 fusion.12
  (64 shorter events, 4.9 us)
Async XLA Ops:
  6.5 64.5 %copy-start = (bf16[1280,1280]{1,0:T(8,128)(2,1)S(1)}, bf16[1280,1280]{1,0:T(8,128)(2,1)}, u32[]{:S(2)}) copy-start(bf16[1280,1280]{1,0:T(8,128)(2,1)} %param.10) | copy-start | bytes 9830404
  9.4 13.6 %all-to-all-start = ((s32[16,1,2]{2,1,0:T(1,128)}), s32[16,1,2]{2,1,0:T(1,128)S(1)}, u32[]{:S(2)}, u32[]{:S(2)}) async-start(s32[16,1,2]{2,1,0:T(1,128)} %bitcast.8), calls=%async_computation | async-start | bytes 16384 | tf_op jit(solution)/shard_map/all_to_all | solution.py:104
  50.9 16.5 %copy-start.9 = (s32[128]{0:T(128)S(1)}, s32[128]{0:T(128)}, u32[]{:S(2)}) copy-start(s32[128]{0:T(128)} %param.16) | copy-start | bytes 1540
  50.9 380.0 %all-to-all-start.1 = ((bf16[16,2,128,2560]{3,2,1,0:T(8,128)(2,1)}), bf16[16,2,128,2560]{3,2,1,0:T(8,128)(2,1)}, u32[]{:S(2)}, u32[]{:S(2)}) async-start(bf16[16,2,128,2560]{3,2,1,0:T(8,128)(2,1)} %broadcast_select_fusion), calls=%async_computation.1 | async-start | bytes 41943040 | tf_op jit(solution)/shard_map/all_to_all | solution.py:108
  58.1 11.9 %copy-start.8 = (s32[2,3]{1,0:T(2,128)S(1)}, s32[2,3]{1,0:T(2,128)}, u32[]{:S(2)}) copy-start(s32[2,3]{1,0:T(2,128)} %param.14) | copy-start | bytes 76
  58.1 364.6 %all-reduce.2.cloned.1.call-start = ((), (), s32[]{:S(2)}) async-start(), calls=%async_computation.2 | async-start | bytes 1310720 | tf_op jit(solution)/shard_map/psum | solution.py:84
  60.6 366.5 %collective-permute-start = (bf16[128,2560]{1,0:T(8,128)(2,1)}, bf16[128,2560]{1,0:T(8,128)(2,1)}, u32[]{:S(2)}, u32[]{:S(2)}) collective-permute-start(bf16[128,2560]{1,0:T(8,128)(2,1)} %get-tuple-element.28), channel_id=1, source_target_pairs={{0,1},{1,2},{2,3},{3,4},{4,5},{5,6},{6,7},{7,8},{8,9},{9,10},{10,1... | collective-permute-start | bytes 1966088 | tf_op jit(solution)/shard_map/ppermute | solution.py:20
  64.0 363.2 %collective-permute-start.1 = (bf16[128,2560]{1,0:T(8,128)(2,1)}, bf16[128,2560]{1,0:T(8,128)(2,1)}, u32[]{:S(2)}, u32[]{:S(2)}) collective-permute-start(bf16[128,2560]{1,0:T(8,128)(2,1)} %get-tuple-element.30), channel_id=1, source_target_pairs={{1,0},{2,1},{3,2},{4,3},{5,4},{6,5},{7,6},{8,7},{9,8},{10,9},{11,1... | collective-permute-start | bytes 1966088 | tf_op jit(solution)/shard_map/ppermute | solution.py:21
  75.3 351.8 %copy-start.2 = (bf16[256,2560]{1,0:T(8,128)(2,1)S(1)}, bf16[256,2560]{1,0:T(8,128)(2,1)}, u32[]{:S(2)}) copy-start(bf16[256,2560]{1,0:T(8,128)(2,1)} %convolution_convert_fusion) | copy-start | bytes 3932164
  440.6 3.3 copy-start.4
  457.9 5.5 %copy-start.3 = (f32[2,20,128,768]{3,2,1,0:T(8,128)}, f32[2,20,128,768]{3,2,1,0:T(8,128)S(1)}, u32[]{:S(2)}) copy-start(f32[2,20,128,768]{3,2,1,0:T(8,128)S(1)} %get-tuple-element.40) | copy-start | bytes 47185924
  463.4 6.4 %copy-start.5 = (f32[20,128,2,128]{3,1,2,0:T(8,128)S(1)}, f32[20,128,2,128]{3,1,2,0:T(8,128)}, u32[]{:S(2)}) copy-start(f32[20,128,2,128]{3,1,2,0:T(8,128)} %get-tuple-element.42) | copy-start | bytes 7864324
  470.5 9.1 %copy-start.6 = (bf16[128,1280]{0,1:T(8,128)(2,1)S(1)}, bf16[128,1280]{0,1:T(8,128)(2,1)}, u32[]{:S(2)}) copy-start(bf16[128,1280]{0,1:T(8,128)(2,1)} %copy.91) | copy-start | bytes 983044
  482.2 7.8 %copy-start.1 = (bf16[1280,1280]{1,0:T(8,128)(2,1)S(1)}, bf16[1280,1280]{1,0:T(8,128)(2,1)}, u32[]{:S(2)}) copy-start(bf16[1280,1280]{1,0:T(8,128)(2,1)} %param.10) | copy-start | bytes 9830404
  485.6 3.5 copy-start.7
Sparse Core Ops, SparseCore 0:
  70.0 352.6 all-reduce.1
where the time goes:
time: 498 us; the launch traced here: 497 us
  waiting for transfers between devices  347 us (70%)
  local copies, waits for them, and re-layouts  47.9 us (10%)
  other arithmetic  34.6 us (7%)
  matrix products  31.2 us (6%)
  starting transfers between devices  21.5 us (4%)
  between operations  14.3 us (3%)
    psum x1, waiting for transfers between devices, body(): summed = lax.psum(picked.astype(jnp.bfloat16), 'tm')  347 us
    select_n x2, other arithmetic, body(): jnp.take(keyval.reshape(qblocks, BLOCK, payload_width), chosen, axis=0)  17.8 us
  transfers between devices with their start and end apart: 5, of which 2 were waited for; matrix products, arithmetic and copies ran while one was open for 5% of the time, Pallas kernels for 0%

commit v1 on v0

v1 whole, which is shorter than its diff:
```python
import functools

import jax
import jax.numpy as jnp
from jax import lax
from jax.experimental import pallas as pl
from jax.experimental.pallas import tpu as pltpu
from jax.sharding import PartitionSpec as P

HEADS = 20
BLOCK = 128
POOL = 4
PICKS = 3
D = 1280
HD = 64
TILE = 256
STEPS = D // TILE
SHARDS = 16
SUB = BLOCK // SHARDS
ROWS = 256
NEG = -1e30

VM = pltpu.VMEM
SM = pltpu.SMEM


def _pack_kernel(first_ref, frames_ref, gpos_ref, out_ref):
    frames = frames_ref[...]
    for blk in range(2):
        out_ref[:, blk] = frames[blk * BLOCK : (blk + 1) * BLOCK].reshape(SHARDS, SUB, D)
    local = gpos_ref[...] - first_ref[0] * BLOCK
    rows = lax.broadcasted_iota(jnp.int32, (ROWS, BLOCK), 0)
    onehot = jnp.where(rows == local, 1.0, 0.0).T.astype(jnp.bfloat16)
    picked = jnp.dot(onehot, frames, preferred_element_type=jnp.float32)
    out_ref[:, 2] = picked.reshape(SHARDS, SUB, D).astype(jnp.bfloat16)


def pack(first, frames, gpos):
    return pl.pallas_call(
        _pack_kernel,
        out_shape=jax.ShapeDtypeStruct((SHARDS, 3, SUB, D), jnp.bfloat16),
        in_specs=[
            pl.BlockSpec(memory_space=SM),
            pl.BlockSpec(memory_space=VM),
            pl.BlockSpec(memory_space=VM),
        ],
        out_specs=pl.BlockSpec(memory_space=VM),
        name="pack",
    )(first, frames, gpos)


def _select_kernel(ids_ref, rows_ref, a_ref, b_ref):
    total = rows_ref[0, 2].astype(jnp.float32)
    for i in range(1, SHARDS):
        total = total + rows_ref[i, 2].astype(jnp.float32)
    total = total.astype(jnp.bfloat16)
    for r in range(SHARDS):
        for j in range(PICKS):
            c = ids_ref[r, j]
            a_ref[r, j] = rows_ref[c // 2, c % 2]
        a_ref[r, PICKS] = total
        for j in range(PICKS):
            c = ids_ref[r, PICKS + j]
            b_ref[r, j] = rows_ref[c // 2, c % 2]


def select(ids, rows):
    return pl.pallas_call(
        _select_kernel,
        out_shape=(
            jax.ShapeDtypeStruct((SHARDS, PICKS + 1, SUB, D), jnp.bfloat16),
            jax.ShapeDtypeStruct((SHARDS, PICKS, SUB, D), jnp.bfloat16),
        ),
        in_specs=[pl.BlockSpec(memory_space=SM), pl.BlockSpec(memory_space=VM)],
        out_specs=(pl.BlockSpec(memory_space=VM), pl.BlockSpec(memory_space=VM)),
        name="select",
    )(ids, rows)


def _dot(a, b):
    return jnp.dot(a, b, preferred_element_type=jnp.float32)


def _attend(query, keys, values, bias):
    lanes = lax.broadcasted_iota(jnp.int32, (BLOCK, TILE), 1) // HD
    zero = jnp.zeros_like(query)
    stacked = jnp.concatenate([jnp.where(lanes == i, query, zero) for i in range(4)], axis=0)
    scores = lax.dot_general(
        stacked, keys, (((1,), (1,)), ((), ())), preferred_element_type=jnp.float32
    )
    scores = scores + bias
    top = jnp.max(scores, axis=1, keepdims=True)
    weight = jnp.exp(scores - top).astype(jnp.bfloat16)
    ones = jnp.ones((keys.shape[0], 128), jnp.bfloat16)
    low = lax.broadcasted_iota(jnp.int32, (BLOCK, 128), 1) < HD
    outs, sums, tops = [], [], []
    for pair in range(2):
        ext = jnp.concatenate([values[:, pair * 128 : (pair + 1) * 128], ones], axis=1)
        res = _dot(weight[pair * 256 : (pair + 1) * 256], ext)
        outs.append(jnp.where(low, res[:BLOCK, :128], res[BLOCK:, :128]))
        sums.append(jnp.where(low, res[:BLOCK, 128:], res[BLOCK:, 128:]))
        tops.append(
            jnp.where(
                low,
                top[pair * 256 : pair * 256 + BLOCK],
                top[pair * 256 + BLOCK : (pair + 1) * 256],
            )
        )
    return (
        jnp.concatenate(outs, axis=1),
        jnp.concatenate(sums, axis=1),
        jnp.concatenate(tops, axis=1),
    )


def _window_kernel(lo_ref, own_ref, hi_ref, bias_ref, wq_ref, wk_ref, wv_ref, q_ref, o_ref, l_ref, m_ref):
    own = own_ref[...]
    rows = jnp.concatenate([lo_ref[...], own, hi_ref[...]], axis=0)
    query = _dot(own, wq_ref[...]).astype(jnp.bfloat16) * jnp.bfloat16(0.125)
    q_ref[...] = query
    keys = _dot(rows, wk_ref[...]).astype(jnp.bfloat16)
    values = _dot(rows, wv_ref[...]).astype(jnp.bfloat16)
    for b in range(2):
        at = slice(b * BLOCK, b * BLOCK + 3 * BLOCK)
        res = _attend(
            query[b * BLOCK : (b + 1) * BLOCK], keys[at], values[at], bias_ref[b : b + 1, :]
        )
        for ref, val in zip((o_ref, l_ref, m_ref), res):
            ref[b * BLOCK : (b + 1) * BLOCK, :] = val


def _whole(shape):
    return pl.BlockSpec(shape, lambda p: (0,) * len(shape))


def _cols(rows, shift=0):
    return pl.BlockSpec((rows, TILE), lambda p: (0, p + shift))


def window(lo, own, hi, bias, w_query, w_kv):
    f32 = jax.ShapeDtypeStruct((ROWS, D), jnp.float32)
    return pl.pallas_call(
        _window_kernel,
        grid=(STEPS,),
        out_shape=(jax.ShapeDtypeStruct((ROWS, D), jnp.bfloat16), f32, f32, f32),
        in_specs=[
            _whole((BLOCK, D)),
            _whole((ROWS, D)),
            _whole((BLOCK, D)),
            _whole((2, 3 * BLOCK)),
            _cols(D),
            _cols(D),
            _cols(D, STEPS),
        ],
        out_specs=(_cols(ROWS),) * 4,
        name="window",
    )(lo, own, hi, bias, w_query, w_kv, w_kv)


def _finish(acc, out_ref, gain_ref, live):
    tiles = []
    for c in range(D // 128):
        total = acc[c, pl.ds(0, 32, stride=POOL), :]
        for i in range(1, POOL):
            total = total + acc[c, pl.ds(i, 32, stride=POOL), :]
        tiles.append(total)
    pooled = jnp.concatenate(tiles, axis=1) * (1.0 / POOL)
    mean = jnp.mean(pooled, axis=1, keepdims=True)
    centered = pooled - mean
    var = jnp.mean(centered * centered, axis=1, keepdims=True)
    normed = centered * lax.rsqrt(var + 1e-05) * gain_ref[...]
    out_ref[...] = jnp.where(live, normed, 0.0).astype(jnp.bfloat16)


def _merge(query, keys, values, bias, o_ref, l_ref, m_ref):
    out, total, top = _attend(query, keys, values, bias)
    near = m_ref[...]
    both = jnp.maximum(near, top)
    a = jnp.exp(near - both)
    b = jnp.exp(top - both)
    return ((a * o_ref[...] + b * out) / (a * l_ref[...] + b * total)).astype(jnp.bfloat16)


def _accumulate(step, context, wo_ref, acc):
    part = _dot(context, wo_ref[...])
    for c in range(D // 128):
        piece = part[:, c * 128 : (c + 1) * 128]
        acc[c] = jnp.where(step == 0, piece, acc[c] + piece)


def _first_kernel(
    meta_ref, rows_ref, bias_ref, q_ref, o_ref, l_ref, m_ref, wk_ref, wv_ref, wo_ref, gain_ref,
    out_ref, gk_ref, gv_ref, acc,
):
    step = pl.program_id(0)
    rows = rows_ref[...]
    keys = _dot(rows, wk_ref[...])
    gk_ref[...] = keys.reshape(SHARDS, 4, SUB, TILE)[:, 3].reshape(BLOCK, TILE).astype(jnp.bfloat16)
    values = _dot(rows, wv_ref[...])
    gv_ref[...] = values.reshape(SHARDS, 4, SUB, TILE)[:, 3].reshape(BLOCK, TILE).astype(jnp.bfloat16)
    context = _merge(
        q_ref[...], keys.astype(jnp.bfloat16), values.astype(jnp.bfloat16), bias_ref[...], o_ref, l_ref, m_ref
    )
    _accumulate(step, context, wo_ref, acc)

    @pl.when(step == STEPS - 1)
    def _():
        _finish(acc, out_ref, gain_ref, meta_ref[0] < meta_ref[1])


def _second_kernel(
    meta_ref, rows_ref, bias_ref, q_ref, o_ref, l_ref, m_ref, wk_ref, wv_ref, wo_ref, gain_ref, gk_ref, gv_ref,
    prev_ref, out_ref, acc,
):
    step = pl.program_id(0)
    rows = rows_ref[...]
    keys = jnp.concatenate([_dot(rows, wk_ref[...]).astype(jnp.bfloat16), gk_ref[...]], axis=0)
    values = jnp.concatenate([_dot(rows, wv_ref[...]).astype(jnp.bfloat16), gv_ref[...]], axis=0)
    context = _merge(q_ref[...], keys, values, bias_ref[...], o_ref, l_ref, m_ref)
    _accumulate(step, context, wo_ref, acc)

    @pl.when(step == STEPS - 1)
    def _():
        _finish(acc, out_ref, gain_ref, meta_ref[0] + 1 < meta_ref[1])


def _half(b):
    return pl.BlockSpec((BLOCK, TILE), lambda p: (b, p))


def first(meta, rows, bias, q, o, l, m, w_kv, w_out, gain):
    glob = jax.ShapeDtypeStruct((BLOCK, D), jnp.bfloat16)
    return pl.pallas_call(
        _first_kernel,
        grid=(STEPS,),
        out_shape=(jax.ShapeDtypeStruct((64, D), jnp.bfloat16), glob, glob),
        in_specs=[
            pl.BlockSpec(memory_space=SM),
            _whole((4 * BLOCK, D)),
            _whole((1, 4 * BLOCK)),
            *[_half(0)] * 4,
            _cols(D),
            _cols(D, STEPS),
            pl.BlockSpec((TILE, D), lambda p: (p, 0)),
            _whole((1, D)),
        ],
        out_specs=(
            pl.BlockSpec((32, D), lambda p: (0, 0)),
            pl.BlockSpec((BLOCK, TILE), lambda p: (0, p)),
            pl.BlockSpec((BLOCK, TILE), lambda p: (0, p)),
        ),
        scratch_shapes=[pltpu.VMEM((D // 128, BLOCK, 128), jnp.float32)],
        name="first",
    )(meta, rows, bias, q, o, l, m, w_kv, w_kv, w_out, gain)


def second(meta, rows, bias, q, o, l, m, w_kv, w_out, gain, gk, gv, prev):
    return pl.pallas_call(
        _second_kernel,
        grid=(STEPS,),
        out_shape=jax.ShapeDtypeStruct((64, D), jnp.bfloat16),
        in_specs=[
            pl.BlockSpec(memory_space=SM),
            _whole((3 * BLOCK, D)),
            _whole((1, 4 * BLOCK)),
            *[_half(1)] * 4,
            _cols(D),
            _cols(D, STEPS),
            pl.BlockSpec((TILE, D), lambda p: (p, 0)),
            _whole((1, D)),
            pl.BlockSpec((BLOCK, TILE), lambda p: (0, p)),
            pl.BlockSpec((BLOCK, TILE), lambda p: (0, p)),
            pl.BlockSpec(memory_space=pl.ANY),
        ],
        out_specs=pl.BlockSpec((32, D), lambda p: (1, 0)),
        scratch_shapes=[pltpu.VMEM((D // 128, BLOCK, 128), jnp.float32)],
        input_output_aliases={13: 0},
        name="second",
    )(meta, rows, bias, q, o, l, m, w_kv, w_kv, w_out, gain, gk, gv, prev)


def exchange(value):
    return lax.all_to_all(value, "tm", split_axis=0, concat_axis=0, tiled=True)


def body(frames, w_query, w_kv, w_out, norm_gain, rand_owner, rand_slot, global_pos, length):
    shards = lax.axis_size("tm")
    rank = lax.axis_index("tm").astype(jnp.int32)
    first_block = rank * 2
    live = length[0]
    ids = (rand_owner * 2 + rand_slot).astype(jnp.int32)
    meta = jnp.stack([first_block, live])
    asked = exchange(jnp.broadcast_to(jnp.pad(ids.reshape(1, 6), ((0, 0), (0, 2))), (shards, 8)))
    up = [(i, i + 1) for i in range(shards - 1)]
    down = [(j, i) for i, j in up]
    packed = pack(meta, frames, global_pos.reshape(1, BLOCK))
    held = exchange(packed)
    lo = lax.ppermute(frames[BLOCK:], "tm", up)
    hi = lax.ppermute(frames[:BLOCK], "tm", down)
    send_a, send_b = select(asked, held)
    got_a = exchange(send_a).reshape(4 * BLOCK, D)
    got_b = exchange(send_b).reshape(3 * BLOCK, D)

    window_ids = first_block + jnp.arange(2, dtype=jnp.int32)[:, None] - 1 + jnp.arange(3, dtype=jnp.int32)[None, :]
    window_live = (window_ids >= 0) & (window_ids < live)
    window_bias = jnp.where(jnp.repeat(window_live, BLOCK, axis=1), 0.0, NEG)
    rand_bias = jnp.where(ids < live, 0.0, NEG)
    glob_bias = jnp.where(global_pos < live * BLOCK, 0.0, NEG)
    spread = jnp.broadcast_to(rand_bias[:, None, :, None], (2, SHARDS, PICKS, SUB))
    bias_a = jnp.concatenate([spread[0], glob_bias.reshape(SHARDS, 1, SUB)], axis=1).reshape(1, 4 * BLOCK)
    bias_b = jnp.concatenate([spread[1].reshape(-1), glob_bias]).reshape(1, 4 * BLOCK)
    gain = norm_gain.reshape(1, D)

    q, o, l, m = window(lo, frames, hi, window_bias, w_query, w_kv)
    half, gk, gv = first(meta, got_a, bias_a, q, o, l, m, w_kv, w_out, gain)
    return second(meta, got_b, bias_b, q, o, l, m, w_kv, w_out, gain, gk, gv, half)


def solution(mesh):
    placed = (
        P(("rec", "tm"), None),
        P(),
        P(),
        P(),
        P(),
        P(("rec", "tm"), None),
        P(("rec", "tm"), None),
        P("rec"),
        P("rec"),
    )
    return jax.shard_map(
        body, mesh=mesh, in_specs=placed, out_specs=P(("rec", "tm"), None), check_vma=False
    )
```

time: 498 us -> 111 us (0.22)
  waiting for transfers between devices: 347 us -> 17.2 us
  local copies, waits for them, and re-layouts: 47.9 us -> 4.6 us
  Pallas kernels: 0 us -> 42 us
  other arithmetic: 34.6 us -> 2.11 us
  matrix products: 31.2 us -> 0 us
  blocking collectives: 0 us -> 20 us
  between operations: 14.3 us -> 0.75 us
    psum x1 -> x0, waiting for transfers between devices: 347 us -> none  [body(): summed = lax.psum(picked.astype(jnp.bfloat16), 'tm')]
    pallas_call x0 -> x5, Pallas kernels: none -> 42 us  [the longest x1 13 us: window(): pl.pallas_call(_window_kernel, grid=(STEPS,), out_shape=(jax.ShapeDtypeSt...]
    dot_general x8 -> x0, matrix products: 31.2 us -> none  [the longest x1 9.03 us: attend(): jnp.einsum('bhij,bjhd->bihd', near_weight, value_h, preferred_element_typ...]
    all_to_all x0 -> x1, blocking collectives: none -> 20 us  [exchange(): return lax.all_to_all(value, 'tm', split_axis=0, concat_axis=0, tiled=True)]
    select_n x4 -> x2, other arithmetic: 20.5 us -> 0.78 us  [the longest x1 0.77 us: body(): rand_bias = jnp.where(ids < live, 0.0, NEG)]
    gather x2 -> x0, local copies, waits for them, and re-layouts: 19.4 us -> none  [the longest x1 9.75 us: body(): jnp.take(answered.reshape(shards * capacity, BLOCK, payload_width), posit...]
    slice x6 -> x1, local copies, waits for them, and re-layouts: 17.3 us -> 0.04 us  [body(): hi = lax.ppermute(frames[:BLOCK], 'tm', down)]
    all_to_all x2 -> x3, waiting for transfers between devices: 0.13 us -> 17.2 us  [exchange(): return lax.all_to_all(value, 'tm', split_axis=0, concat_axis=0, tiled=True)]
  transfers between devices with their start and end apart: 5 -> 5, of which waited for: 2 -> 2; matrix products, arithmetic and copies ran while one was open for 5% -> 3% of each run, Pallas kernels for 0% -> 25%
where the time goes in v1:
time: 111 us; the launch traced here: 110 us
  Pallas kernels  42 us (38%)
  starting transfers between devices  23.3 us (21%)
  blocking collectives  20 us (18%)
  waiting for transfers between devices  17.2 us (15%)
  local copies, waits for them, and re-layouts  4.6 us (4%)
  other arithmetic  2.11 us (2%)
    all_to_all x1, blocking collectives, exchange(): return lax.all_to_all(value, 'tm', split_axis=0, concat_axis=0, tiled=True)  20 us
    all_to_all x3, starting transfers between devices, exchange(): return lax.all_to_all(value, 'tm', split_axis=0, concat_axis=0, tiled=True)  17.5 us
    all_to_all x3, waiting for transfers between devices, exchange(): return lax.all_to_all(value, 'tm', split_axis=0, concat_axis=0, tiled=True)  17.2 us
    pallas_call x1, Pallas kernels, window(): pl.pallas_call(_window_kernel, grid=(STEPS,), out_shape=(jax.ShapeDtypeSt...  13 us
    pallas_call x1, Pallas kernels, first(): pl.pallas_call(_first_kernel, grid=(STEPS,), out_shape=(jax.ShapeDtypeStr...  12 us
    pallas_call x1, Pallas kernels, second(): pl.pallas_call(_second_kernel, grid=(STEPS,), out_shape=jax.ShapeDtypeStr...  11.3 us
    ppermute x1, starting transfers between devices, body(): lo = lax.ppermute(frames[BLOCK:], 'tm', up)  3.71 us
    pallas_call x1, Pallas kernels, select(): pl.pallas_call(_select_kernel, out_shape=(jax.ShapeDtypeStruct((SHARDS, P...  3.24 us
  transfers between devices with their start and end apart: 5, of which 2 were waited for; matrix products, arithmetic and copies ran while one was open for 3% of the time, Pallas kernels for 25%

profile of v1, /device:TPU:2, one launch (start us, length us, event | category | flops | bytes accessed | tf_op | source)
XLA Modules:
  0.0 110.0 jit_solution(7279099115078339489)
XLA Ops:
  0.7 0.8 compare_select_fusion.1
  1.4 0.1 reshape.46
  1.5 0.6 broadcast_in_dim.42
  2.1 7.5 %all-to-all-start = ((s32[16,1,8]{2,1,0:T(1,128)}), s32[16,1,8]{2,1,0:T(1,128)S(1)}, u32[]{:S(2)}, u32[]{:S(2)}) async-start(s32[16,1,8]{2,1,0:T(1,128)} %broadcast_in_dim.42), calls=%async_computation | async-start | bytes 16384 | tf_op jit(solution)/shard_map/all_to_all | solution.py:283
  9.6 0.7 pad_add_fusion.first_ref.meta_ref
  10.3 2.4 %pack.1 = bf16[16,3,8,1280]{3,2,1,0:T(8,128)(2,1)} custom-call(s32[2]{0:T(128)} %pad_add_fusion.first_ref.meta_ref, bf16[256,1280]{1,0:T(8,128)(2,1)} %own_ref.1, s32[1,128]{1,0:T(1,128)} %bitcast.27), custom_call_target="tpu_custom_call" | custom-call | tf_op jit(solution)/shard_map/pack/pallas_call | solution.py:39
  12.6 3.1 %all-to-all-done = s32[16,1,8]{2,1,0:T(1,128)S(1)} async-done(((s32[16,1,8]{2,1,0:T(1,128)}), s32[16,1,8]{2,1,0:T(1,128)S(1)}, u32[]{:S(2)}, u32[]{:S(2)}) %all-to-all-start) | async-done | bytes 544 | tf_op jit(solution)/shard_map/all_to_all | solution.py:283
  15.8 20.0 %all_to_all.23.rows_ref = bf16[16,3,8,1280]{3,2,1,0:T(8,128)(2,1)} all-to-all(bf16[16,3,8,1280]{3,2,1,0:T(8,128)(2,1)} %pack.1), channel_id=1, replica_groups=mesh['rec'=16,'tm'=16] {'tm'}, dimensions={0} | all-to-all | bytes 1966080 | tf_op jit(solution)/shard_map/all_to_all | solution.py:283
  35.7 3.2 %select.2 = (bf16[16,4,8,1280]{3,2,1,0:T(8,128)(2,1)}, bf16[16,3,8,1280]{3,2,1,0:T(8,128)(2,1)}) custom-call(s32[16,8]{1,0:T(8,128)} %bitcast.23, bf16[16,3,8,1280]{3,2,1,0:T(8,128)(2,1)} %all_to_all.23.rows_ref), custom_call_target="tpu_custom_call" | custom-call | tf_op jit(solution)/shard_map/select/pallas_call | solution.py:68
  39.0 5.1 %all-to-all-start.3 = ((bf16[16,4,8,1280]{3,2,1,0:T(8,128)(2,1)}), bf16[16,4,8,1280]{3,2,1,0:T(8,128)(2,1)S(1)}, u32[]{:S(2)}, u32[]{:S(2)}) async-start(bf16[16,4,8,1280]{3,2,1,0:T(8,128)(2,1)} %get-tuple-element.19), calls=%async_computation.3 | async-start | bytes 2621440 | tf_op jit(solution)/shard_map/all_to_all | solution.py:283
  44.1 0.0 copy-start.5
  44.2 0.0 copy-start.6
  44.2 2.1 %collective-permute-start.1 = (bf16[128,1280]{1,0:T(8,128)(2,1)S(1)}, bf16[128,1280]{1,0:T(8,128)(2,1)S(1)}, u32[]{:S(2)}, u32[]{:S(2)}) collective-permute-start(bf16[128,1280]{1,0:T(8,128)(2,1)S(1)} %get-tuple-element.25), channel_id=1, source_target_pairs={{1,0},{2,1},{3,2},{4,3},{5,4},{6,5},{7,6},{8,7},{9,8},{10,9},{11,1... | collective-permute-start | bytes 983048 | tf_op jit(solution)/shard_map/ppermute | solution.py:299
  46.3 3.7 %collective-permute-start = (bf16[128,1280]{1,0:T(8,128)(2,1)S(1)}, bf16[128,1280]{1,0:T(8,128)(2,1)}, u32[]{:S(2)}, u32[]{:S(2)}) collective-permute-start(bf16[128,1280]{1,0:T(8,128)(2,1)S(1)} %get-tuple-element.26), channel_id=1, source_target_pairs={{0,1},{1,2},{2,3},{3,4},{4,5},{5,6},{6,7},{7,8},{8,9},{9,10},{10,1... | collective-permute-start | bytes 983048 | tf_op jit(solution)/shard_map/ppermute | solution.py:298
  50.0 14.1 %all-to-all-done.3 = bf16[16,4,8,1280]{3,2,1,0:T(8,128)(2,1)S(1)} async-done(((bf16[16,4,8,1280]{3,2,1,0:T(8,128)(2,1)}), bf16[16,4,8,1280]{3,2,1,0:T(8,128)(2,1)S(1)}, u32[]{:S(2)}, u32[]{:S(2)}) %all-to-all-start.3) | async-done | bytes 1310752 | tf_op jit(solution)/shard_map/all_to_all | solution.py:283
  64.1 4.9 %all-to-all-start.2 = ((bf16[16,3,8,1280]{3,2,1,0:T(8,128)(2,1)}), bf16[16,3,8,1280]{3,2,1,0:T(8,128)(2,1)S(1)}, u32[]{:S(2)}, u32[]{:S(2)}) async-start(bf16[16,3,8,1280]{3,2,1,0:T(8,128)(2,1)} %get-tuple-element.14), calls=%async_computation.2 | async-start | bytes 1966080 | tf_op jit(solution)/shard_map/all_to_all | solution.py:283
  69.0 0.1 broadcast_bitcast_fusion
  69.1 0.6 copy.21
  69.7 0.6 reshape.50.gain_ref
  70.3 0.1 reshape.52
  70.4 0.1 pad_maximum_fusion
  70.5 0.7 reshape.53.bias_ref
  71.2 0.1 broadcast_in_dim.45
  71.2 0.1 broadcast_in_dim.46
  71.3 0.6 pad_maximum_fusion.1
  71.9 0.0 collective-permute-done.1.hi_ref
  71.9 0.0 collective-permute-done.lo_ref
  71.9 0.7 copy-done.3
  72.6 13.0 %window.1 = (bf16[256,1280]{1,0:T(8,128)(2,1)}, f32[256,1280]{1,0:T(8,128)}, f32[256,1280]{1,0:T(8,128)}, f32[256,1280]{1,0:T(8,128)}) custom-call(bf16[128,1280]{1,0:T(8,128)(2,1)} %collective-permute-done.lo_ref, bf16[256,1280]{1,0:T(8,128)(2,1)} %own_ref.1, bf16[128,1280]{1,0:T(8,128)(2,1)} %copy-done.3, f32[2,384]{1,0:T(2,128)} %bitcast.25, ...), custom_call_target="tpu_custom_call" | custom-call | tf_op jit(solution)/shard_map/window/pallas_call | solution.py:142
  85.7 12.0 %first.1 = (bf16[64,1280]{1,0:T(8,128)(2,1)}, bf16[128,1280]{1,0:T(8,128)(2,1)}, bf16[128,1280]{1,0:T(8,128)(2,1)}) custom-call(s32[2]{0:T(128)} %pad_add_fusion.first_ref.meta_ref, bf16[512,1280]{1,0:T(8,128)(2,1)} %bitcast.21, f32[1,512]{1,0:T(1,128)} %reshape.53.bias_ref, bf16[256,1280]{1,0:T(8,128)(2,1)} %get-tuple-element.15.q_ref, ...), custom_call_target="tpu_custom_call" | custom-call | tf_op jit(solution)/shard_map/first/pallas_call | solution.py:233
  97.7 0.9 copy-done.2
  98.7 11.3 %second.1 = bf16[64,1280]{1,0:T(8,128)(2,1)} custom-call(s32[2]{0:T(128)} %pad_add_fusion.first_ref.meta_ref, bf16[384,1280]{1,0:T(8,128)(2,1)} %bitcast.22, f32[1,512]{1,0:T(1,128)} %bitcast.26, bf16[256,1280]{1,0:T(8,128)(2,1)} %get-tuple-element.15.q_ref, f32[256,1280]{1,0:T(8,128)} %get-tuple-element.16.o_ref, ...), custom_call_target="tpu_custom_call", output_to_operand_aliasing={{}: (13, {})} | custom-call | tf_op jit(solution)/shard_map/second/pallas_call | solution.py:258
  (17 shorter events, 0.1 us)
Async XLA Ops:
  2.1 13.6 %all-to-all-start = ((s32[16,1,8]{2,1,0:T(1,128)}), s32[16,1,8]{2,1,0:T(1,128)S(1)}, u32[]{:S(2)}, u32[]{:S(2)}) async-start(s32[16,1,8]{2,1,0:T(1,128)} %broadcast_in_dim.42), calls=%async_computation | async-start | bytes 16384 | tf_op jit(solution)/shard_map/all_to_all | solution.py:283
  15.8 20.0 %copy-start.4 = (s32[16,1,8]{2,1,0:T(1,128)}, s32[16,1,8]{2,1,0:T(1,128)S(1)}, u32[]{:S(2)}) copy-start(s32[16,1,8]{2,1,0:T(1,128)S(1)} %all-to-all-done) | copy-start | bytes 1540
  39.0 5.1 %copy-start = (bf16[256,1280]{1,0:T(8,128)(2,1)S(1)}, bf16[256,1280]{1,0:T(8,128)(2,1)}, u32[]{:S(2)}) copy-start(bf16[256,1280]{1,0:T(8,128)(2,1)} %own_ref.1) | copy-start | bytes 1966084
  39.0 25.2 %all-to-all-start.3 = ((bf16[16,4,8,1280]{3,2,1,0:T(8,128)(2,1)}), bf16[16,4,8,1280]{3,2,1,0:T(8,128)(2,1)S(1)}, u32[]{:S(2)}, u32[]{:S(2)}) async-start(bf16[16,4,8,1280]{3,2,1,0:T(8,128)(2,1)} %get-tuple-element.19), calls=%async_computation.3 | async-start | bytes 2621440 | tf_op jit(solution)/shard_map/all_to_all | solution.py:283
  44.1 25.5 %copy-start.5 = (f32[1280]{0:T(1024)S(1)}, f32[1280]{0:T(1024)}, u32[]{:S(2)}) copy-start(f32[1280]{0:T(1024)} %param.13) | copy-start | bytes 15364
  44.2 26.1 %copy-start.6 = (s32[128]{0:T(128)S(1)}, s32[128]{0:T(128)}, u32[]{:S(2)}) copy-start(s32[128]{0:T(128)} %param.16) | copy-start | bytes 1540
  44.2 27.8 %collective-permute-start.1 = (bf16[128,1280]{1,0:T(8,128)(2,1)S(1)}, bf16[128,1280]{1,0:T(8,128)(2,1)S(1)}, u32[]{:S(2)}, u32[]{:S(2)}) collective-permute-start(bf16[128,1280]{1,0:T(8,128)(2,1)S(1)} %get-tuple-element.25), channel_id=1, source_target_pairs={{1,0},{2,1},{3,2},{4,3},{5,4},{6,5},{7,6},{8,7},{9,8},{10,9},{11,1... | collective-permute-start | bytes 983048 | tf_op jit(solution)/shard_map/ppermute | solution.py:299
  46.3 25.6 %collective-permute-start = (bf16[128,1280]{1,0:T(8,128)(2,1)S(1)}, bf16[128,1280]{1,0:T(8,128)(2,1)}, u32[]{:S(2)}, u32[]{:S(2)}) collective-permute-start(bf16[128,1280]{1,0:T(8,128)(2,1)S(1)} %get-tuple-element.26), channel_id=1, source_target_pairs={{0,1},{1,2},{2,3},{3,4},{4,5},{5,6},{6,7},{7,8},{8,9},{9,10},{10,1... | collective-permute-start | bytes 983048 | tf_op jit(solution)/shard_map/ppermute | solution.py:298
  64.1 21.5 %copy-start.1 = (bf16[16,4,8,1280]{3,2,1,0:T(8,128)(2,1)}, bf16[16,4,8,1280]{3,2,1,0:T(8,128)(2,1)S(1)}, u32[]{:S(2)}) copy-start(bf16[16,4,8,1280]{3,2,1,0:T(8,128)(2,1)S(1)} %all-to-all-done.3) | copy-start | bytes 3932164
  64.1 33.6 %all-to-all-start.2 = ((bf16[16,3,8,1280]{3,2,1,0:T(8,128)(2,1)}), bf16[16,3,8,1280]{3,2,1,0:T(8,128)(2,1)S(1)}, u32[]{:S(2)}, u32[]{:S(2)}) async-start(bf16[16,3,8,1280]{3,2,1,0:T(8,128)(2,1)} %get-tuple-element.14), calls=%async_computation.2 | async-start | bytes 1966080 | tf_op jit(solution)/shard_map/all_to_all | solution.py:283
  71.9 0.7 copy-start.3
  97.7 0.9 copy-start.2

commit v2 on v1

--- a/solution.py
+++ b/solution.py
@@ -1,5 +1,3 @@
-import functools
-
 import jax
 import jax.numpy as jnp
 from jax import lax
@@ -7,7 +5,7 @@
 from jax.experimental.pallas import tpu as pltpu
 from jax.sharding import PartitionSpec as P
 
-HEADS = 20
+
 BLOCK = 128
 POOL = 4
 PICKS = 3
@@ -18,63 +16,99 @@
 SHARDS = 16
 SUB = BLOCK // SHARDS
 ROWS = 256
+LT = D // 128
 NEG = -1e30
 
 VM = pltpu.VMEM
 SM = pltpu.SMEM
 
 
-def _pack_kernel(first_ref, frames_ref, gpos_ref, out_ref):
+def _pack_kernel(meta_ref, owner_ref, slot_ref, frames_ref, gpos_ref, out_ref):
     frames = frames_ref[...]
     for blk in range(2):
-        out_ref[:, blk] = frames[blk * BLOCK : (blk + 1) * BLOCK].reshape(SHARDS, SUB, D)
-    local = gpos_ref[...] - first_ref[0] * BLOCK
-    rows = lax.broadcasted_iota(jnp.int32, (ROWS, BLOCK), 0)
-    onehot = jnp.where(rows == local, 1.0, 0.0).T.astype(jnp.bfloat16)
+        for c in range(LT):
+            piece = frames_ref[blk * BLOCK : (blk + 1) * BLOCK, c * 128 : (c + 1) * 128]
+            out_ref[:, blk * LT + c] = piece.reshape(SHARDS, SUB, 128)
+    local = (gpos_ref[...] - meta_ref[0] * BLOCK).astype(jnp.float32)
+    local = jnp.broadcast_to(local, (8, BLOCK)).T[:, :1]
+    cols = lax.broadcasted_iota(jnp.int32, (BLOCK, ROWS), 1).astype(jnp.float32)
+    onehot = jnp.where(cols == local, 1.0, 0.0).astype(jnp.bfloat16)
     picked = jnp.dot(onehot, frames, preferred_element_type=jnp.float32)
-    out_ref[:, 2] = picked.reshape(SHARDS, SUB, D).astype(jnp.bfloat16)
-
-
-def pack(first, frames, gpos):
+    for c in range(LT):
+        piece = picked[:, c * 128 : (c + 1) * 128].reshape(SHARDS, SUB, 128)
+        out_ref[:, 2 * LT + c] = piece.astype(jnp.bfloat16)
+    lane = lax.broadcasted_iota(jnp.int32, (SUB, 128), 1)
+    codes = jnp.zeros((SUB, 128), jnp.int32)
+    for q in range(2):
+        for j in range(PICKS):
+            code = (slot_ref[q, j] * SHARDS + owner_ref[q, j]) * SUB
+            codes = jnp.where(lane == q * PICKS + j, code, codes)
+    codes = codes + lax.broadcasted_iota(jnp.int32, (SUB, 128), 0)
+    codes = codes.astype(jnp.float32).astype(jnp.bfloat16)
+    for s in range(SHARDS):
+        out_ref[s, 3 * LT] = codes
+
+
+def pack(meta, owner, slot, frames, gpos):
     return pl.pallas_call(
         _pack_kernel,
-        out_shape=jax.ShapeDtypeStruct((SHARDS, 3, SUB, D), jnp.bfloat16),
-        in_specs=[
-            pl.BlockSpec(memory_space=SM),
-            pl.BlockSpec(memory_space=VM),
-            pl.BlockSpec(memory_space=VM),
-        ],
+        out_shape=jax.ShapeDtypeStruct((SHARDS, 3 * LT + 1, SUB, 128), jnp.bfloat16),
+        in_specs=[pl.BlockSpec(memory_space=SM)] * 3 + [pl.BlockSpec(memory_space=VM)] * 2,
         out_specs=pl.BlockSpec(memory_space=VM),
         name="pack",
-    )(first, frames, gpos)
-
-
-def _select_kernel(ids_ref, rows_ref, a_ref, b_ref):
-    total = rows_ref[0, 2].astype(jnp.float32)
-    for i in range(1, SHARDS):
-        total = total + rows_ref[i, 2].astype(jnp.float32)
-    total = total.astype(jnp.bfloat16)
-    for r in range(SHARDS):
-        for j in range(PICKS):
-            c = ids_ref[r, j]
-            a_ref[r, j] = rows_ref[c // 2, c % 2]
-        a_ref[r, PICKS] = total
-        for j in range(PICKS):
-            c = ids_ref[r, PICKS + j]
-            b_ref[r, j] = rows_ref[c // 2, c % 2]
-
-
-def select(ids, rows):
+    )(meta, owner, slot, frames, gpos)
+
+
+def _select_kernel(held_ref, a_ref, b_ref, buf, sem):
+    codes = held_ref[:, 3 * LT].astype(jnp.float32).reshape(BLOCK, 128)
+    blocks = []
+    for slot in range(2):
+        tiles = [
+            held_ref[:, slot * LT + c].astype(jnp.float32).reshape(BLOCK, 128).astype(jnp.bfloat16)
+            for c in range(LT)
+        ]
+        blocks.append(jnp.concatenate(tiles, axis=1))
+    rows = jnp.concatenate(blocks, axis=0)
+    cols = lax.broadcasted_iota(jnp.int32, (BLOCK, ROWS), 1).astype(jnp.float32)
+    copies = []
+
+    def send(k, dest):
+        copy = pltpu.make_async_copy(buf.at[k], dest, sem.at[k])
+        copy.start()
+        copies.append(copy)
+
+    for c in range(LT):
+        total = held_ref[0, 2 * LT + c].astype(jnp.float32)
+        for i in range(1, SHARDS):
+            total = total + held_ref[i, 2 * LT + c].astype(jnp.float32)
+        total = total.astype(jnp.bfloat16)
+        for r in range(SHARDS):
+            buf[6, r, :, c * 128 : (c + 1) * 128] = total
+    send(6, a_ref.at[:, PICKS])
+    for k in range(2 * PICKS):
+        onehot = jnp.where(cols == codes[:, k : k + 1], 1.0, 0.0).astype(jnp.bfloat16)
+        got = jnp.dot(onehot, rows, preferred_element_type=jnp.float32)
+        buf[k] = got.reshape(SHARDS, SUB, D).astype(jnp.bfloat16)
+        send(k, a_ref.at[:, k] if k < PICKS else b_ref.at[:, k - PICKS])
+    for copy in copies:
+        copy.wait()
+
+
+def select(held):
     return pl.pallas_call(
         _select_kernel,
         out_shape=(
             jax.ShapeDtypeStruct((SHARDS, PICKS + 1, SUB, D), jnp.bfloat16),
             jax.ShapeDtypeStruct((SHARDS, PICKS, SUB, D), jnp.bfloat16),
         ),
-        in_specs=[pl.BlockSpec(memory_space=SM), pl.BlockSpec(memory_space=VM)],
-        out_specs=(pl.BlockSpec(memory_space=VM), pl.BlockSpec(memory_space=VM)),
+        in_specs=[pl.BlockSpec(memory_space=VM)],
+        out_specs=(pl.BlockSpec(memory_space=pl.ANY), pl.BlockSpec(memory_space=pl.ANY)),
+        scratch_shapes=[
+            pltpu.VMEM((2 * PICKS + 1, SHARDS, SUB, D), jnp.bfloat16),
+            pltpu.SemaphoreType.DMA((2 * PICKS + 1,)),
+        ],
         name="select",
-    )(ids, rows)
+    )(held)
 
 
 def _dot(a, b):
@@ -283,24 +317,23 @@
     return lax.all_to_all(value, "tm", split_axis=0, concat_axis=0, tiled=True)
 
 
-def body(frames, w_query, w_kv, w_out, norm_gain, rand_owner, rand_slot, global_pos, length):
+def program(frames, w_query, w_kv, w_out, norm_gain, rand_owner, rand_slot, global_pos, length):
     shards = lax.axis_size("tm")
     rank = lax.axis_index("tm").astype(jnp.int32)
     first_block = rank * 2
     live = length[0]
-    ids = (rand_owner * 2 + rand_slot).astype(jnp.int32)
     meta = jnp.stack([first_block, live])
-    asked = exchange(jnp.broadcast_to(jnp.pad(ids.reshape(1, 6), ((0, 0), (0, 2))), (shards, 8)))
     up = [(i, i + 1) for i in range(shards - 1)]
     down = [(j, i) for i, j in up]
-    packed = pack(meta, frames, global_pos.reshape(1, BLOCK))
+    packed = pack(meta, rand_owner, rand_slot, frames, global_pos.reshape(1, BLOCK))
     held = exchange(packed)
     lo = lax.ppermute(frames[BLOCK:], "tm", up)
     hi = lax.ppermute(frames[:BLOCK], "tm", down)
-    send_a, send_b = select(asked, held)
+    send_a, send_b = select(held)
     got_a = exchange(send_a).reshape(4 * BLOCK, D)
     got_b = exchange(send_b).reshape(3 * BLOCK, D)
 
+    ids = rand_owner * 2 + rand_slot
     window_ids = first_block + jnp.arange(2, dtype=jnp.int32)[:, None] - 1 + jnp.arange(3, dtype=jnp.int32)[None, :]
     window_live = (window_ids >= 0) & (window_ids < live)
     window_bias = jnp.where(jnp.repeat(window_live, BLOCK, axis=1), 0.0, NEG)
@@ -329,5 +362,5 @@
         P("rec"),
     )
     return jax.shard_map(
-        body, mesh=mesh, in_specs=placed, out_specs=P(("rec", "tm"), None), check_vma=False
-    )
+        program, mesh=mesh, in_specs=placed, out_specs=P(("rec", "tm"), None), check_vma=False
+    )

time: 111 us -> 101 us (0.910)
  starting transfers between devices: 23.3 us -> 15.8 us
  waiting for transfers between devices: 17.2 us -> 14 us
  blocking collectives: 20 us -> 23 us
    all_to_all x3 -> x2, starting transfers between devices: 17.5 us -> 9.98 us  [exchange(): return lax.all_to_all(value, 'tm', split_axis=0, concat_axis=0, tiled=True)]
    all_to_all x3 -> x2, waiting for transfers between devices: 17.2 us -> 14 us  [exchange(): return lax.all_to_all(value, 'tm', split_axis=0, concat_axis=0, tiled=True)]
    all_to_all x1, blocking collectives: 20 us -> 23 us  [exchange(): return lax.all_to_all(value, 'tm', split_axis=0, concat_axis=0, tiled=True)]
    unnamed x16 -> x18, local copies, waits for them, and re-layouts: 2.32 us -> 2.35 us
  transfers between devices with their start and end apart: 5 -> 4, of which waited for: 2 -> 1; matrix products, arithmetic and copies ran while one was open for 3% -> 3% of each run, Pallas kernels for 25% -> 25%
where the time goes in v2:
time: 101 us
  Pallas kernels  41.8 us (41%)
  blocking collectives  23 us (23%)
  starting transfers between devices  15.8 us (16%)
  waiting for transfers between devices  14 us (14%)
  local copies, waits for them, and re-layouts  3.94 us (4%)
  other arithmetic  1.4 us (1%)
    all_to_all x1, blocking collectives, exchange(): return lax.all_to_all(value, 'tm', split_axis=0, concat_axis=0, tiled=True)  23 us
    all_to_all x2, waiting for transfers between devices, exchange(): return lax.all_to_all(value, 'tm', split_axis=0, concat_axis=0, tiled=True)  14 us
    pallas_call x1, Pallas kernels, window(): pl.pallas_call(_window_kernel, grid=(STEPS,), out_shape=(jax.ShapeDtypeSt...  13 us
    pallas_call x1, Pallas kernels, first(): pl.pallas_call(_first_kernel, grid=(STEPS,), out_shape=(jax.ShapeDtypeStr...  12 us
    pallas_call x1, Pallas kernels, second(): pl.pallas_call(_second_kernel, grid=(STEPS,), out_shape=jax.ShapeDtypeStr...  11.3 us
    all_to_all x2, starting transfers between devices, exchange(): return lax.all_to_all(value, 'tm', split_axis=0, concat_axis=0, tiled=True)  9.98 us
    ppermute x1, starting transfers between devices, program(): lo = lax.ppermute(frames[BLOCK:], 'tm', up)  3.71 us
    pallas_call x1, Pallas kernels, select(): pl.pallas_call(_select_kernel, out_shape=(jax.ShapeDtypeStruct((SHARDS, P...  2.95 us
  transfers between devices with their start and end apart: 4, of which 1 were waited for; matrix products, arithmetic and copies ran while one was open for 3% of the time, Pallas kernels for 25%

profile of v2, /device:TPU:2, one launch (start us, length us, event | category | flops | bytes accessed | tf_op | source)
XLA Modules:
  0.0 100.7 jit_solution(7957840816521476386)
XLA Ops:
  0.7 0.7 pad_add_fusion.meta_ref
  1.3 2.4 %pack.1 = bf16[16,31,8,128]{3,2,1,0:T(8,128)(2,1)} custom-call(s32[2]{0:T(128)} %pad_add_fusion.meta_ref, s32[2,3]{1,0:T(2,128)} %owner_ref.1, s32[2,3]{1,0:T(2,128)} %slot_ref.1, bf16[256,1280]{1,0:T(8,128)(2,1)} %own_ref.1, s32[1,128]{1,0:T(1,128)} %bitcast.23), custom_call_target="tpu_custom_call" | custom-call | tf_op jit(solution)/shard_map/pack/pallas_call | solution.py:53
  3.8 23.0 %all_to_all.15.held_ref = bf16[16,31,8,128]{3,2,1,0:T(8,128)(2,1)} all-to-all(bf16[16,31,8,128]{3,2,1,0:T(8,128)(2,1)} %pack.1), channel_id=1, replica_groups=mesh['rec'=16,'tm'=16] {'tm'}, dimensions={0} | all-to-all | bytes 2031616 | tf_op jit(solution)/shard_map/all_to_all | solution.py:317
  26.8 3.0 %select.1 = (bf16[16,4,8,1280]{3,2,1,0:T(8,128)(2,1)}, bf16[16,3,8,1280]{3,2,1,0:T(8,128)(2,1)}) custom-call(bf16[16,31,8,128]{3,2,1,0:T(8,128)(2,1)} %all_to_all.15.held_ref), custom_call_target="tpu_custom_call" | custom-call | tf_op jit(solution)/shard_map/select/pallas_call | solution.py:98
  29.7 0.0 copy-start
  29.7 5.1 %all-to-all-start.2 = ((bf16[16,4,8,1280]{3,2,1,0:T(8,128)(2,1)}), bf16[16,4,8,1280]{3,2,1,0:T(8,128)(2,1)S(1)}, u32[]{:S(2)}, u32[]{:S(2)}) async-start(bf16[16,4,8,1280]{3,2,1,0:T(8,128)(2,1)} %get-tuple-element.19), calls=%async_computation.2 | async-start | bytes 2621440 | tf_op jit(solution)/shard_map/all_to_all | solution.py:317
  34.8 0.0 copy-start.5
  34.9 0.0 copy-start.6
  34.9 0.0 copy-start.4
  34.9 0.0 copy-start.7
  34.9 2.1 %collective-permute-start.1 = (bf16[128,1280]{1,0:T(8,128)(2,1)S(1)}, bf16[128,1280]{1,0:T(8,128)(2,1)S(1)}, u32[]{:S(2)}, u32[]{:S(2)}) collective-permute-start(bf16[128,1280]{1,0:T(8,128)(2,1)S(1)} %get-tuple-element.23), channel_id=1, source_target_pairs={{1,0},{2,1},{3,2},{4,3},{5,4},{6,5},{7,6},{8,7},{9,8},{10,9},{11,1... | collective-permute-start | bytes 983048 | tf_op jit(solution)/shard_map/ppermute | solution.py:331
  37.1 3.7 %collective-permute-start = (bf16[128,1280]{1,0:T(8,128)(2,1)S(1)}, bf16[128,1280]{1,0:T(8,128)(2,1)}, u32[]{:S(2)}, u32[]{:S(2)}) collective-permute-start(bf16[128,1280]{1,0:T(8,128)(2,1)S(1)} %get-tuple-element.24), channel_id=1, source_target_pairs={{0,1},{1,2},{2,3},{3,4},{4,5},{5,6},{6,7},{7,8},{8,9},{9,10},{10,1... | collective-permute-start | bytes 983048 | tf_op jit(solution)/shard_map/ppermute | solution.py:330
  40.8 0.1 and_select_fusion
  40.9 14.0 %all-to-all-done.2 = bf16[16,4,8,1280]{3,2,1,0:T(8,128)(2,1)S(1)} async-done(((bf16[16,4,8,1280]{3,2,1,0:T(8,128)(2,1)}), bf16[16,4,8,1280]{3,2,1,0:T(8,128)(2,1)S(1)}, u32[]{:S(2)}, u32[]{:S(2)}) %all-to-all-start.2) | async-done | bytes 1310752 | tf_op jit(solution)/shard_map/all_to_all | solution.py:317
  54.9 4.9 %all-to-all-start.1 = ((bf16[16,3,8,1280]{3,2,1,0:T(8,128)(2,1)}), bf16[16,3,8,1280]{3,2,1,0:T(8,128)(2,1)S(1)}, u32[]{:S(2)}, u32[]{:S(2)}) async-start(bf16[16,3,8,1280]{3,2,1,0:T(8,128)(2,1)} %get-tuple-element.14), calls=%async_computation.1 | async-start | bytes 1966080 | tf_op jit(solution)/shard_map/all_to_all | solution.py:317
  59.8 0.1 broadcast_bitcast_fusion
  59.9 0.6 copy.15
  60.4 0.6 reshape.40.gain_ref
  61.0 0.1 reshape.42
  61.1 0.1 pad_maximum_fusion
  61.2 0.7 reshape.43.bias_ref
  61.9 0.1 broadcast_in_dim.39
  62.0 0.1 broadcast_in_dim.40
  62.1 0.6 pad_maximum_fusion.1
  62.7 0.0 collective-permute-done.1.hi_ref
  62.7 0.0 collective-permute-done.lo_ref
  62.7 0.7 copy-done.3
  63.4 13.0 %window.1 = (bf16[256,1280]{1,0:T(8,128)(2,1)}, f32[256,1280]{1,0:T(8,128)}, f32[256,1280]{1,0:T(8,128)}, f32[256,1280]{1,0:T(8,128)}) custom-call(bf16[128,1280]{1,0:T(8,128)(2,1)} %collective-permute-done.lo_ref, bf16[256,1280]{1,0:T(8,128)(2,1)} %own_ref.1, bf16[128,1280]{1,0:T(8,128)(2,1)} %copy-done.3, f32[2,384]{1,0:T(2,128)} %bitcast.21, ...), custom_call_target="tpu_custom_call" | custom-call | tf_op jit(solution)/shard_map/window/pallas_call | solution.py:176
  76.4 12.0 %first.1 = (bf16[64,1280]{1,0:T(8,128)(2,1)}, bf16[128,1280]{1,0:T(8,128)(2,1)}, bf16[128,1280]{1,0:T(8,128)(2,1)}) custom-call(s32[2]{0:T(128)} %pad_add_fusion.meta_ref, bf16[512,1280]{1,0:T(8,128)(2,1)} %bitcast.18, f32[1,512]{1,0:T(1,128)} %reshape.43.bias_ref, bf16[256,1280]{1,0:T(8,128)(2,1)} %get-tuple-element.15.q_ref, ...), custom_call_target="tpu_custom_call" | custom-call | tf_op jit(solution)/shard_map/first/pallas_call | solution.py:267
  88.4 0.0 all-to-all-done.1
  88.5 0.9 copy-done.2
  89.4 11.3 %second.1 = bf16[64,1280]{1,0:T(8,128)(2,1)} custom-call(s32[2]{0:T(128)} %pad_add_fusion.meta_ref, bf16[384,1280]{1,0:T(8,128)(2,1)} %bitcast.19, f32[1,512]{1,0:T(1,128)} %bitcast.22, bf16[256,1280]{1,0:T(8,128)(2,1)} %get-tuple-element.15.q_ref, f32[256,1280]{1,0:T(8,128)} %get-tuple-element.16.o_ref, ...), custom_call_target="tpu_custom_call", output_to_operand_aliasing={{}: (13, {})} | custom-call | tf_op jit(solution)/shard_map/second/pallas_call | solution.py:292
  (14 shorter events, 0.1 us)
Async XLA Ops:
  29.7 5.1 %copy-start = (bf16[256,1280]{1,0:T(8,128)(2,1)S(1)}, bf16[256,1280]{1,0:T(8,128)(2,1)}, u32[]{:S(2)}) copy-start(bf16[256,1280]{1,0:T(8,128)(2,1)} %own_ref.1) | copy-start | bytes 1966084
  29.7 25.2 %all-to-all-start.2 = ((bf16[16,4,8,1280]{3,2,1,0:T(8,128)(2,1)}), bf16[16,4,8,1280]{3,2,1,0:T(8,128)(2,1)S(1)}, u32[]{:S(2)}, u32[]{:S(2)}) async-start(bf16[16,4,8,1280]{3,2,1,0:T(8,128)(2,1)} %get-tuple-element.19), calls=%async_computation.2 | async-start | bytes 2621440 | tf_op jit(solution)/shard_map/all_to_all | solution.py:317
  34.8 6.0 %copy-start.5 = (s32[2,3]{1,0:T(2,128)S(1)}, s32[2,3]{1,0:T(2,128)}, u32[]{:S(2)}) copy-start(s32[2,3]{1,0:T(2,128)} %owner_ref.1) | copy-start | bytes 76
  34.9 6.0 %copy-start.6 = (s32[2,3]{1,0:T(2,128)S(1)}, s32[2,3]{1,0:T(2,128)}, u32[]{:S(2)}) copy-start(s32[2,3]{1,0:T(2,128)} %slot_ref.1) | copy-start | bytes 76
  34.9 25.5 %copy-start.4 = (f32[1280]{0:T(1024)S(1)}, f32[1280]{0:T(1024)}, u32[]{:S(2)}) copy-start(f32[1280]{0:T(1024)} %param.13) | copy-start | bytes 15364
  34.9 26.1 %copy-start.7 = (s32[128]{0:T(128)S(1)}, s32[128]{0:T(128)}, u32[]{:S(2)}) copy-start(s32[128]{0:T(128)} %param.16) | copy-start | bytes 1540
  34.9 27.7 %collective-permute-start.1 = (bf16[128,1280]{1,0:T(8,128)(2,1)S(1)}, bf16[128,1280]{1,0:T(8,128)(2,1)S(1)}, u32[]{:S(2)}, u32[]{:S(2)}) collective-permute-start(bf16[128,1280]{1,0:T(8,128)(2,1)S(1)} %get-tuple-element.23), channel_id=1, source_target_pairs={{1,0},{2,1},{3,2},{4,3},{5,4},{6,5},{7,6},{8,7},{9,8},{10,9},{11,1... | collective-permute-start | bytes 983048 | tf_op jit(solution)/shard_map/ppermute | solution.py:331
  37.1 25.6 %collective-permute-start = (bf16[128,1280]{1,0:T(8,128)(2,1)S(1)}, bf16[128,1280]{1,0:T(8,128)(2,1)}, u32[]{:S(2)}, u32[]{:S(2)}) collective-permute-start(bf16[128,1280]{1,0:T(8,128)(2,1)S(1)} %get-tuple-element.24), channel_id=1, source_target_pairs={{0,1},{1,2},{2,3},{3,4},{4,5},{5,6},{6,7},{7,8},{8,9},{9,10},{10,1... | collective-permute-start | bytes 983048 | tf_op jit(solution)/shard_map/ppermute | solution.py:330
  54.9 21.6 %copy-start.1 = (bf16[16,4,8,1280]{3,2,1,0:T(8,128)(2,1)}, bf16[16,4,8,1280]{3,2,1,0:T(8,128)(2,1)S(1)}, u32[]{:S(2)}) copy-start(bf16[16,4,8,1280]{3,2,1,0:T(8,128)(2,1)S(1)} %all-to-all-done.2) | copy-start | bytes 3932164
  54.9 33.6 %all-to-all-start.1 = ((bf16[16,3,8,1280]{3,2,1,0:T(8,128)(2,1)}), bf16[16,3,8,1280]{3,2,1,0:T(8,128)(2,1)S(1)}, u32[]{:S(2)}, u32[]{:S(2)}) async-start(bf16[16,3,8,1280]{3,2,1,0:T(8,128)(2,1)} %get-tuple-element.14), calls=%async_computation.1 | async-start | bytes 1966080 | tf_op jit(solution)/shard_map/all_to_all | solution.py:317
  62.7 0.7 copy-start.3
  88.5 1.0 copy-start.2

commit v3 on v2

v3 whole, which is shorter than its diff:
```python
import jax
import jax.numpy as jnp
from jax import lax
from jax.experimental import pallas as pl
from jax.experimental.pallas import tpu as pltpu
from jax.sharding import PartitionSpec as P


BLOCK = 128
POOL = 4
PICKS = 3
D = 1280
HD = 64
TILE = 256
STEPS = D // TILE
SHARDS = 16
SUB = BLOCK // SHARDS
ROWS = 256
SUBS_A = 5
SUBS_B = 2
LT = D // 128
NEG = -1e30

VM = pltpu.VMEM
SM = pltpu.SMEM


def _pack_kernel(rank_ref, owner_ref, slot_ref, frames_ref, gpos_ref, out_ref):
    frames = frames_ref[...]
    for blk in range(2):
        for c in range(LT):
            piece = frames_ref[blk * BLOCK : (blk + 1) * BLOCK, c * 128 : (c + 1) * 128]
            out_ref[:, blk * LT + c] = piece.reshape(SHARDS, SUB, 128)
    local = (gpos_ref[...] - rank_ref[0] * ROWS).astype(jnp.float32)
    local = jnp.broadcast_to(local, (8, BLOCK)).T[:, :1]
    cols = lax.broadcasted_iota(jnp.int32, (BLOCK, ROWS), 1).astype(jnp.float32)
    onehot = jnp.where(cols == local, 1.0, 0.0).astype(jnp.bfloat16)
    picked = jnp.dot(onehot, frames, preferred_element_type=jnp.float32)
    for c in range(LT):
        piece = picked[:, c * 128 : (c + 1) * 128].reshape(SHARDS, SUB, 128)
        out_ref[:, 2 * LT + c] = piece.astype(jnp.bfloat16)
    lane = lax.broadcasted_iota(jnp.int32, (SUB, 128), 1)
    codes = jnp.zeros((SUB, 128), jnp.int32)
    for q in range(2):
        for j in range(PICKS):
            code = (slot_ref[q, j] * SHARDS + owner_ref[q, j]) * SUB
            codes = jnp.where(lane == q * PICKS + j, code, codes)
    codes = codes + lax.broadcasted_iota(jnp.int32, (SUB, 128), 0)
    codes = codes.astype(jnp.float32).astype(jnp.bfloat16)
    for s in range(SHARDS):
        out_ref[s, 3 * LT] = codes


def pack(rank, owner, slot, frames, gpos):
    return pl.pallas_call(
        _pack_kernel,
        out_shape=VM((SHARDS, 3 * LT + 1, SUB, 128), jnp.bfloat16),
        in_specs=[pl.BlockSpec(memory_space=SM)] * 3 + [pl.BlockSpec(memory_space=VM)] * 2,
        out_specs=pl.BlockSpec(memory_space=VM),
        name="pack",
    )(rank, owner, slot, frames, gpos)


def _select_kernel(held_ref, a_ref, b_ref, buf, sem):
    copies = []

    def send(k, dest):
        copy = pltpu.make_async_copy(buf.at[k], dest, sem.at[k])
        copy.start()
        copies.append(copy)

    codes = held_ref[:, 3 * LT].astype(jnp.float32).reshape(BLOCK, 128)
    blocks = []
    for slot in range(2):
        tiles = [
            held_ref[:, slot * LT + c].astype(jnp.float32).reshape(BLOCK, 128).astype(jnp.bfloat16)
            for c in range(LT)
        ]
        blocks.append(jnp.concatenate(tiles, axis=1))
    rows = jnp.concatenate(blocks, axis=0)
    cols = lax.broadcasted_iota(jnp.int32, (BLOCK, ROWS), 1).astype(jnp.float32)
    for c in range(LT):
        total = held_ref[0, 2 * LT + c].astype(jnp.float32)
        for i in range(1, SHARDS):
            total = total + held_ref[i, 2 * LT + c].astype(jnp.float32)
        total = total.astype(jnp.bfloat16)
        for r in range(SHARDS):
            buf[2 * PICKS, r, :, c * 128 : (c + 1) * 128] = total
    send(2 * PICKS, a_ref.at[:, SUBS_A - 1])
    for k in range(2 * PICKS):
        onehot = jnp.where(cols == codes[:, k : k + 1], 1.0, 0.0).astype(jnp.bfloat16)
        got = jnp.dot(onehot, rows, preferred_element_type=jnp.float32)
        buf[k] = got.reshape(SHARDS, SUB, D).astype(jnp.bfloat16)
        send(k, a_ref.at[:, k] if k < SUBS_A - 1 else b_ref.at[:, k - SUBS_A + 1])
    for copy in copies:
        copy.wait()


def select(held):
    return pl.pallas_call(
        _select_kernel,
        out_shape=(
            jax.ShapeDtypeStruct((SHARDS, SUBS_A, SUB, D), jnp.bfloat16),
            jax.ShapeDtypeStruct((SHARDS, SUBS_B, SUB, D), jnp.bfloat16),
        ),
        in_specs=[pl.BlockSpec(memory_space=VM)],
        out_specs=(pl.BlockSpec(memory_space=pl.ANY), pl.BlockSpec(memory_space=pl.ANY)),
        scratch_shapes=[
            pltpu.VMEM((2 * PICKS + 1, SHARDS, SUB, D), jnp.bfloat16),
            pltpu.SemaphoreType.DMA((2 * PICKS + 1,)),
        ],
        name="select",
    )(pltpu.with_memory_space_constraint(held, VM))


def _dot(a, b):
    return jnp.dot(a, b, preferred_element_type=jnp.float32)


def _attend(query, keys, values, bias):
    lanes = lax.broadcasted_iota(jnp.int32, (BLOCK, TILE), 1) // HD
    zero = jnp.zeros_like(query)
    stacked = jnp.concatenate([jnp.where(lanes == i, query, zero) for i in range(4)], axis=0)
    scores = lax.dot_general(
        stacked, keys, (((1,), (1,)), ((), ())), preferred_element_type=jnp.float32
    )
    scores = scores + bias
    top = jnp.max(scores, axis=1, keepdims=True)
    weight = jnp.exp(scores - top).astype(jnp.bfloat16)
    ones = jnp.ones((keys.shape[0], 128), jnp.bfloat16)
    low = lax.broadcasted_iota(jnp.int32, (BLOCK, 128), 1) < HD
    outs, sums, tops = [], [], []
    for pair in range(2):
        ext = jnp.concatenate([values[:, pair * 128 : (pair + 1) * 128], ones], axis=1)
        res = _dot(weight[pair * 256 : (pair + 1) * 256], ext)
        outs.append(jnp.where(low, res[:BLOCK, :128], res[BLOCK:, :128]))
        sums.append(jnp.where(low, res[:BLOCK, 128:], res[BLOCK:, 128:]))
        tops.append(
            jnp.where(
                low,
                top[pair * 256 : pair * 256 + BLOCK],
                top[pair * 256 + BLOCK : (pair + 1) * 256],
            )
        )
    return (
        jnp.concatenate(outs, axis=1),
        jnp.concatenate(sums, axis=1),
        jnp.concatenate(tops, axis=1),
    )


def _own_kernel(
    rank_ref, len_ref, owner_ref, slot_ref, gpos_ref, own_ref, wq_ref, wk_ref, wv_ref,
    q_ref, k_ref, v_ref, bias_ref,
):
    own = own_ref[...]
    q_ref[...] = _dot(own, wq_ref[...]).astype(jnp.bfloat16) * jnp.bfloat16(0.125)
    k_ref[...] = _dot(own, wk_ref[...]).astype(jnp.bfloat16)
    v_ref[...] = _dot(own, wv_ref[...]).astype(jnp.bfloat16)

    @pl.when(pl.program_id(0) == 0)
    def _():
        live = len_ref[0]
        lane = lax.broadcasted_iota(jnp.int32, (1, 4 * BLOCK), 1)

        def row(parts):
            dead = lane < 0
            for at, block in parts:
                dead = dead | (at & ((block < 0) | (block >= live)))
            return jnp.where(dead, NEG, 0.0)

        def picked(q, j):
            return owner_ref[q, j] * 2 + slot_ref[q, j]

        for q in range(2):
            near = [(lane // BLOCK == i, rank_ref[0] * 2 + q - 1 + i) for i in range(3)]
            bias_ref[q : q + 1, :] = row(near)
        glob = jnp.where(gpos_ref[...] < live * BLOCK, 0.0, NEG)
        rows = lane // SUB
        far = row([((rows % 3 == j), picked(0, j)) for j in range(3)])
        bias_ref[2:3, :] = jnp.concatenate([far[:, : 3 * BLOCK], glob], axis=1)
        far = row([((rows % 2 == j), picked(1, j + 1)) for j in range(2)])
        more = row([(lane >= 0, picked(1, 0))])
        bias_ref[3:4, :] = jnp.concatenate([far[:, : 2 * BLOCK], glob, more[:, :BLOCK]], axis=1)
        bias_ref[4:8, :] = jnp.zeros((4, 4 * BLOCK), jnp.float32)


def _halo_kernel(lo_ref, hi_ref, bias_ref, q_ref, k_ref, v_ref, wk_ref, wv_ref, o_ref, l_ref, m_ref):
    rim = jnp.concatenate([lo_ref[...], hi_ref[...]], axis=0)

    def widen(own_ref, w_ref):
        far = _dot(rim, w_ref[...]).astype(jnp.bfloat16)
        return jnp.concatenate([far[:BLOCK], own_ref[...], far[BLOCK:]], axis=0)

    keys = widen(k_ref, wk_ref)
    values = widen(v_ref, wv_ref)
    for b in range(2):
        at = slice(b * BLOCK, b * BLOCK + 3 * BLOCK)
        res = _attend(
            q_ref[b * BLOCK : (b + 1) * BLOCK], keys[at], values[at], bias_ref[b : b + 1, : 3 * BLOCK]
        )
        for ref, val in zip((o_ref, l_ref, m_ref), res):
            ref[b * BLOCK : (b + 1) * BLOCK, :] = val


def _whole(shape):
    return pl.BlockSpec(shape, lambda p: (0,) * len(shape))


def _cols(rows, shift=0):
    return pl.BlockSpec((rows, TILE), lambda p: (0, p + shift))


def own_part(rank, length, owner, slot, gpos, own, w_query, w_kv):
    half = jax.ShapeDtypeStruct((ROWS, D), jnp.bfloat16)
    return pl.pallas_call(
        _own_kernel,
        grid=(STEPS,),
        out_shape=(half, half, half, jax.ShapeDtypeStruct((8, 4 * BLOCK), jnp.float32)),
        in_specs=[pl.BlockSpec(memory_space=SM)] * 4
        + [_whole((1, BLOCK)), _whole((ROWS, D)), _cols(D), _cols(D), _cols(D, STEPS)],
        out_specs=(_cols(ROWS),) * 3 + (_whole((8, 4 * BLOCK)),),
        name="own",
    )(rank, length, owner, slot, gpos, own, w_query, w_kv, w_kv)


def halo_part(lo, hi, bias, q, k, v, w_kv):
    f32 = jax.ShapeDtypeStruct((ROWS, D), jnp.float32)
    lo = pltpu.with_memory_space_constraint(lo, VM)
    hi = pltpu.with_memory_space_constraint(hi, VM)
    return pl.pallas_call(
        _halo_kernel,
        grid=(STEPS,),
        out_shape=(f32, f32, f32),
        in_specs=[
            pl.BlockSpec(memory_space=VM),
            pl.BlockSpec(memory_space=VM),
            _whole((8, 4 * BLOCK)),
            *[_cols(ROWS)] * 3,
            _cols(D),
            _cols(D, STEPS),
        ],
        out_specs=(_cols(ROWS),) * 3,
        name="halo",
    )(lo, hi, bias, q, k, v, w_kv, w_kv)


def _finish(acc, out_ref, gain_ref, live):
    tiles = []
    for c in range(D // 128):
        total = acc[c, pl.ds(0, 32, stride=POOL), :]
        for i in range(1, POOL):
            total = total + acc[c, pl.ds(i, 32, stride=POOL), :]
        tiles.append(total)
    pooled = jnp.concatenate(tiles, axis=1) * (1.0 / POOL)
    mean = jnp.mean(pooled, axis=1, keepdims=True)
    centered = pooled - mean
    var = jnp.mean(centered * centered, axis=1, keepdims=True)
    normed = centered * lax.rsqrt(var + 1e-05) * gain_ref[...]
    out_ref[...] = jnp.where(live, normed, 0.0).astype(jnp.bfloat16)


def _merge(query, keys, values, bias, o_ref, l_ref, m_ref):
    out, total, top = _attend(query, keys, values, bias)
    near = m_ref[...]
    both = jnp.maximum(near, top)
    a = jnp.exp(near - both)
    b = jnp.exp(top - both)
    return ((a * o_ref[...] + b * out) / (a * l_ref[...] + b * total)).astype(jnp.bfloat16)


def _accumulate(step, context, wo_ref, acc):
    part = _dot(context, wo_ref[...])
    for c in range(D // 128):
        piece = part[:, c * 128 : (c + 1) * 128]
        acc[c] = jnp.where(step == 0, piece, acc[c] + piece)


def _first_kernel(
    rank_ref, len_ref, rows_ref, bias_ref, q_ref, o_ref, l_ref, m_ref, wk_ref, wv_ref, wo_ref, gain_ref,
    out_ref, gk_ref, gv_ref, acc,
):
    step = pl.program_id(0)
    rows = rows_ref[...]

    def split(w_ref, keep_ref):
        full = _dot(rows, w_ref[...]).reshape(SHARDS, SUBS_A, SUB, TILE)
        near = full[:, :PICKS].reshape(PICKS * BLOCK, TILE).astype(jnp.bfloat16)
        more = full[:, PICKS].reshape(BLOCK, TILE).astype(jnp.bfloat16)
        glob = full[:, PICKS + 1].reshape(BLOCK, TILE).astype(jnp.bfloat16)
        keep_ref[:BLOCK, :] = glob
        keep_ref[BLOCK:, :] = more
        return jnp.concatenate([near, glob], axis=0)

    keys = split(wk_ref, gk_ref)
    values = split(wv_ref, gv_ref)
    context = _merge(q_ref[...], keys, values, bias_ref[2:3, :], o_ref, l_ref, m_ref)
    _accumulate(step, context, wo_ref, acc)

    @pl.when(step == STEPS - 1)
    def _():
        _finish(acc, out_ref, gain_ref, rank_ref[0] * 2 < len_ref[0])


def _second_kernel(
    rank_ref, len_ref, rows_ref, bias_ref, q_ref, o_ref, l_ref, m_ref, wk_ref, wv_ref, wo_ref, gain_ref,
    gk_ref, gv_ref, prev_ref, out_ref, acc,
):
    step = pl.program_id(0)
    rows = rows_ref[...]
    keys = jnp.concatenate([_dot(rows, wk_ref[...]).astype(jnp.bfloat16), gk_ref[...]], axis=0)
    values = jnp.concatenate([_dot(rows, wv_ref[...]).astype(jnp.bfloat16), gv_ref[...]], axis=0)
    context = _merge(q_ref[...], keys, values, bias_ref[3:4, :], o_ref, l_ref, m_ref)
    _accumulate(step, context, wo_ref, acc)

    @pl.when(step == STEPS - 1)
    def _():
        _finish(acc, out_ref, gain_ref, rank_ref[0] * 2 + 1 < len_ref[0])


def _half(b):
    return pl.BlockSpec((BLOCK, TILE), lambda p: (b, p))


def _late_specs(b):
    return [
        *[pl.BlockSpec(memory_space=SM)] * 2,
        pl.BlockSpec(memory_space=VM),
        _whole((8, 4 * BLOCK)),
        *[_half(b)] * 4,
        _cols(D),
        _cols(D, STEPS),
        pl.BlockSpec((TILE, D), lambda p: (p, 0)),
        _whole((1, D)),
    ]


def first(rank, length, rows, bias, q, o, l, m, w_kv, w_out, gain):
    kept = jax.ShapeDtypeStruct((2 * BLOCK, D), jnp.bfloat16)
    rows = pltpu.with_memory_space_constraint(rows, VM)
    return pl.pallas_call(
        _first_kernel,
        grid=(STEPS,),
        out_shape=(jax.ShapeDtypeStruct((64, D), jnp.bfloat16), kept, kept),
        in_specs=_late_specs(0),
        out_specs=(pl.BlockSpec((32, D), lambda p: (0, 0)), _cols(2 * BLOCK), _cols(2 * BLOCK)),
        scratch_shapes=[pltpu.VMEM((D // 128, BLOCK, 128), jnp.float32)],
        name="first",
    )(rank, length, rows, bias, q, o, l, m, w_kv, w_kv, w_out, gain)


def second(rank, length, rows, bias, q, o, l, m, w_kv, w_out, gain, gk, gv, prev):
    rows = pltpu.with_memory_space_constraint(rows, VM)
    return pl.pallas_call(
        _second_kernel,
        grid=(STEPS,),
        out_shape=jax.ShapeDtypeStruct((64, D), jnp.bfloat16),
        in_specs=[
            *_late_specs(1),
            _cols(2 * BLOCK),
            _cols(2 * BLOCK),
            pl.BlockSpec(memory_space=pl.ANY),
        ],
        out_specs=pl.BlockSpec((32, D), lambda p: (1, 0)),
        scratch_shapes=[pltpu.VMEM((D // 128, BLOCK, 128), jnp.float32)],
        input_output_aliases={14: 0},
        name="second",
    )(rank, length, rows, bias, q, o, l, m, w_kv, w_kv, w_out, gain, gk, gv, prev)


def exchange(value):
    return lax.all_to_all(value, "tm", split_axis=0, concat_axis=0, tiled=True)


def program(frames, w_query, w_kv, w_out, norm_gain, rand_owner, rand_slot, global_pos, length):
    shards = lax.axis_size("tm")
    rank = lax.axis_index("tm").astype(jnp.int32).reshape(1)
    gpos = global_pos.reshape(1, BLOCK)
    gain = norm_gain.reshape(1, D)
    up = [(i, i + 1) for i in range(shards - 1)]
    down = [(j, i) for i, j in up]
    packed = pack(rank, rand_owner, rand_slot, frames, gpos)
    held = exchange(packed)
    q, k, v, bias = own_part(rank, length, rand_owner, rand_slot, gpos, frames, w_query, w_kv)
    lo = lax.ppermute(frames[BLOCK:], "tm", up)
    hi = lax.ppermute(frames[:BLOCK], "tm", down)
    send_a, send_b = select(held)
    got_a = exchange(send_a).reshape(SUBS_A * BLOCK, D)
    got_b = exchange(send_b).reshape(SUBS_B * BLOCK, D)
    o, l, m = halo_part(lo, hi, bias, q, k, v, w_kv)
    half, gk, gv = first(rank, length, got_a, bias, q, o, l, m, w_kv, w_out, gain)
    return second(rank, length, got_b, bias, q, o, l, m, w_kv, w_out, gain, gk, gv, half)


def solution(mesh):
    placed = (
        P(("rec", "tm"), None),
        P(),
        P(),
        P(),
        P(),
        P(("rec", "tm"), None),
        P(("rec", "tm"), None),
        P("rec"),
        P("rec"),
    )
    return jax.shard_map(
        program, mesh=mesh, in_specs=placed, out_specs=P(("rec", "tm"), None), check_vma=False
    )
```

time: 101 us -> 110 us (1.089)
  the two profiles are of different devices: /device:TPU:2 before, /device:TPU:104 now
where the time goes in v3:
time: 110 us; the launch traced here: 109 us
  blocking collectives  49.1 us (45%)
  Pallas kernels  45 us (41%)
  starting transfers between devices  13 us (12%)
  local copies, waits for them, and re-layouts  1.38 us (1%)
    all_to_all x2, blocking collectives, exchange(): return lax.all_to_all(value, 'tm', split_axis=0, concat_axis=0, tiled=True)  49.1 us
    pallas_call x1, Pallas kernels, first(): pl.pallas_call(_first_kernel, grid=(STEPS,), out_shape=(jax.ShapeDtypeStr...  12.4 us
    pallas_call x1, Pallas kernels, halo_part(): pl.pallas_call(_halo_kernel, grid=(STEPS,), out_shape=(f32, f32, f32), in...  10.7 us
    pallas_call x1, Pallas kernels, second(): pl.pallas_call(_second_kernel, grid=(STEPS,), out_shape=jax.ShapeDtypeStr...  10.5 us
    pallas_call x1, Pallas kernels, own_part(): pl.pallas_call(_own_kernel, grid=(STEPS,), out_shape=(half, half, half, j...  8.24 us
    all_to_all x1, starting transfers between devices, exchange(): return lax.all_to_all(value, 'tm', split_axis=0, concat_axis=0, tiled=True)  5.01 us
    ppermute x1, starting transfers between devices, program(): hi = lax.ppermute(frames[:BLOCK], 'tm', down)  4.57 us
    ppermute x1, starting transfers between devices, program(): lo = lax.ppermute(frames[BLOCK:], 'tm', up)  3.37 us
  transfers between devices with their start and end apart: 3, of which 0 were waited for; matrix products, arithmetic and copies ran while one was open for 1% of the time, Pallas kernels for 29%

profile of v3, /device:TPU:104, one launch (start us, length us, event | category | flops | bytes accessed | tf_op | source)
XLA Modules:
  0.0 109.1 jit_solution(11030607127295443069)
XLA Ops:
  0.0 1.5 %pack.1 = bf16[16,31,8,128]{3,2,1,0:T(8,128)(2,1)S(1)} custom-call(s32[1]{0:T(128)} %bitcast.rank_ref, s32[2,3]{1,0:T(2,128)} %owner_ref.3, s32[2,3]{1,0:T(2,128)} %slot_ref.3, bf16[256,1280]{1,0:T(8,128)(2,1)} %own_ref.1, s32[1,128]{1,0:T(1,128)} %bitcast.6), custom_call_target="tpu_custom_call" | custom-call | tf_op jit(solution)/shard_map/pack/pallas_call | solution.py:55
  1.5 21.4 %all_to_all.15.held_ref = bf16[16,31,8,128]{3,2,1,0:T(8,128)(2,1)S(1)} all-to-all(bf16[16,31,8,128]{3,2,1,0:T(8,128)(2,1)S(1)} %pack.1), channel_id=1, replica_groups=mesh['rec'=16,'tm'=16] {'tm'}, dimensions={0} | all-to-all | bytes 2031616 | tf_op jit(solution)/shard_map/all_to_all | solution.py:372
  22.9 1.7 %select.1 = (bf16[16,5,8,1280]{3,2,1,0:T(8,128)(2,1)}, bf16[16,2,8,1280]{3,2,1,0:T(8,128)(2,1)}) custom-call(bf16[16,31,8,128]{3,2,1,0:T(8,128)(2,1)S(1)} %all_to_all.15.held_ref), custom_call_target="tpu_custom_call" | custom-call | tf_op jit(solution)/shard_map/select/pallas_call | solution.py:100
  24.6 0.0 copy-start
  24.6 27.6 %all_to_all.16 = bf16[16,5,8,1280]{3,2,1,0:T(8,128)(2,1)S(1)} all-to-all(bf16[16,5,8,1280]{3,2,1,0:T(8,128)(2,1)} %get-tuple-element.25), channel_id=1, replica_groups=mesh['rec'=16,'tm'=16] {'tm'}, dimensions={0} | all-to-all | bytes 3276800 | tf_op jit(solution)/shard_map/all_to_all | solution.py:372
  52.2 0.0 copy-start.1
  52.2 5.0 %all-to-all-start.1 = ((bf16[16,2,8,1280]{3,2,1,0:T(8,128)(2,1)}), bf16[16,2,8,1280]{3,2,1,0:T(8,128)(2,1)S(1)}, u32[]{:S(2)}, u32[]{:S(2)}) async-start(bf16[16,2,8,1280]{3,2,1,0:T(8,128)(2,1)} %get-tuple-element.17), calls=%async_computation.1 | async-start | bytes 1310720 | tf_op jit(solution)/shard_map/all_to_all | solution.py:372
  57.3 0.0 copy-done
  57.3 0.8 fusion
  58.0 3.4 %collective-permute-start = (bf16[128,1280]{1,0:T(8,128)(2,1)}, bf16[128,1280]{1,0:T(8,128)(2,1)S(1)}, u32[]{:S(2)}, u32[]{:S(2)}) collective-permute-start(bf16[128,1280]{1,0:T(8,128)(2,1)} %get-tuple-element.30), channel_id=1, source_target_pairs={{0,1},{1,2},{2,3},{3,4},{4,5},{5,6},{6,7},{7,8},{8,9},{9,10},{10,1... | collective-permute-start | bytes 983048 | tf_op jit(solution)/shard_map/ppermute | solution.py:385
  61.4 4.6 %collective-permute-start.1 = (bf16[128,1280]{1,0:T(8,128)(2,1)S(1)}, bf16[128,1280]{1,0:T(8,128)(2,1)S(1)}, u32[]{:S(2)}, u32[]{:S(2)}) collective-permute-start(bf16[128,1280]{1,0:T(8,128)(2,1)S(1)} %get-tuple-element.29), channel_id=1, source_target_pairs={{1,0},{2,1},{3,2},{4,3},{5,4},{6,5},{7,6},{8,7},{9,8},{10,9},{11,1... | collective-permute-start | bytes 983048 | tf_op jit(solution)/shard_map/ppermute | solution.py:386
  66.6 0.0 copy-done.1
  66.6 0.6 reshape.18.gain_ref
  67.2 8.2 %own.1 = (bf16[256,1280]{1,0:T(8,128)(2,1)}, bf16[256,1280]{1,0:T(8,128)(2,1)}, bf16[256,1280]{1,0:T(8,128)(2,1)}, f32[8,512]{1,0:T(8,128)}) custom-call(s32[1]{0:T(128)} %bitcast.rank_ref, s32[1]{0:T(128)S(6)} %copy.12.len_ref, s32[2,3]{1,0:T(2,128)} %owner_ref.3, s32[2,3]{1,0:T(2,128)} %slot_ref.3, s32[1,128]{1,0:T(1,128)} %bitcast.7, ...), custom_call_target="tpu_custom_call" | custom-call | tf_op jit(solution)/shard_map/own/pallas_call | solution.py:216
  75.5 0.0 collective-permute-done.lo_ref
  75.5 0.0 collective-permute-done.1.hi_ref
  75.5 10.7 %halo.1 = (f32[256,1280]{1,0:T(8,128)}, f32[256,1280]{1,0:T(8,128)}, f32[256,1280]{1,0:T(8,128)}) custom-call(bf16[128,1280]{1,0:T(8,128)(2,1)S(1)} %collective-permute-done.lo_ref, bf16[128,1280]{1,0:T(8,128)(2,1)S(1)} %collective-permute-done.1.hi_ref, f32[8,512]{1,0:T(8,128)} %get-tuple-element.18.bias_ref, bf16[256,1280]{1,0:T(8,128)(2,1)} %get-tuple-element.19.q_ref, ...), custom_call_target="tpu_custom_call" | custom-call | tf_op jit(solution)/shard_map/halo/pallas_call | solution.py:231
  86.2 12.4 %first.1 = (bf16[64,1280]{1,0:T(8,128)(2,1)}, bf16[256,1280]{1,0:T(8,128)(2,1)}, bf16[256,1280]{1,0:T(8,128)(2,1)}) custom-call(s32[1]{0:T(128)} %bitcast.rank_ref, s32[1]{0:T(128)S(6)} %copy.12.len_ref, bf16[640,1280]{1,0:T(8,128)(2,1)S(1)} %bitcast.4, f32[8,512]{1,0:T(8,128)} %get-tuple-element.18.bias_ref, bf16[256,1280]{1,0:T(8,128)(2,1)} %get-tuple-element.19.q_ref, ...), custom_call_target="tpu_custom_call" | custom-call | tf_op jit(solution)/shard_map/first/pallas_call | solution.py:341
  98.6 0.0 all-to-all-done.1
  98.6 10.5 %second.1 = bf16[64,1280]{1,0:T(8,128)(2,1)} custom-call(s32[1]{0:T(128)} %bitcast.rank_ref, s32[1]{0:T(128)S(6)} %copy.12.len_ref, bf16[256,1280]{1,0:T(8,128)(2,1)S(1)} %bitcast.5, f32[8,512]{1,0:T(8,128)} %get-tuple-element.18.bias_ref, bf16[256,1280]{1,0:T(8,128)(2,1)} %get-tuple-element.19.q_ref, ...), custom_call_target="tpu_custom_call", output_to_operand_aliasing={{}: (14, {})} | custom-call | tf_op jit(solution)/shard_map/second/pallas_call | solution.py:354
Async XLA Ops:
  24.6 32.7 %copy-start = (bf16[256,1280]{1,0:T(8,128)(2,1)S(1)}, bf16[256,1280]{1,0:T(8,128)(2,1)}, u32[]{:S(2)}) copy-start(bf16[256,1280]{1,0:T(8,128)(2,1)} %own_ref.1) | copy-start | bytes 1966084
  52.2 14.4 %copy-start.1 = (f32[1280]{0:T(1024)S(1)}, f32[1280]{0:T(1024)}, u32[]{:S(2)}) copy-start(f32[1280]{0:T(1024)} %param.13) | copy-start | bytes 15364
  52.2 46.4 %all-to-all-start.1 = ((bf16[16,2,8,1280]{3,2,1,0:T(8,128)(2,1)}), bf16[16,2,8,1280]{3,2,1,0:T(8,128)(2,1)S(1)}, u32[]{:S(2)}, u32[]{:S(2)}) async-start(bf16[16,2,8,1280]{3,2,1,0:T(8,128)(2,1)} %get-tuple-element.17), calls=%async_computation.1 | async-start | bytes 1310720 | tf_op jit(solution)/shard_map/all_to_all | solution.py:372
  58.0 17.4 %collective-permute-start = (bf16[128,1280]{1,0:T(8,128)(2,1)}, bf16[128,1280]{1,0:T(8,128)(2,1)S(1)}, u32[]{:S(2)}, u32[]{:S(2)}) collective-permute-start(bf16[128,1280]{1,0:T(8,128)(2,1)} %get-tuple-element.30), channel_id=1, source_target_pairs={{0,1},{1,2},{2,3},{3,4},{4,5},{5,6},{6,7},{7,8},{8,9},{9,10},{10,1... | collective-permute-start | bytes 983048 | tf_op jit(solution)/shard_map/ppermute | solution.py:385
  61.4 14.1 %collective-permute-start.1 = (bf16[128,1280]{1,0:T(8,128)(2,1)S(1)}, bf16[128,1280]{1,0:T(8,128)(2,1)S(1)}, u32[]{:S(2)}, u32[]{:S(2)}) collective-permute-start(bf16[128,1280]{1,0:T(8,128)(2,1)S(1)} %get-tuple-element.29), channel_id=1, source_target_pairs={{1,0},{2,1},{3,2},{4,3},{5,4},{6,5},{7,6},{8,7},{9,8},{10,9},{11,1... | collective-permute-start | bytes 983048 | tf_op jit(solution)/shard_map/ppermute | solution.py:386

commit v4 on v3

--- a/solution.py
+++ b/solution.py
@@ -16,8 +16,8 @@
 SHARDS = 16
 SUB = BLOCK // SHARDS
 ROWS = 256
-SUBS_A = 5
-SUBS_B = 2
+SUBS_A = 4
+SUBS_B = 3
 LT = D // 128
 NEG = -1e30
 
@@ -117,17 +117,20 @@
     return jnp.dot(a, b, preferred_element_type=jnp.float32)
 
 
-def _attend(query, keys, values, bias):
+def _scores(query, keys):
     lanes = lax.broadcasted_iota(jnp.int32, (BLOCK, TILE), 1) // HD
     zero = jnp.zeros_like(query)
     stacked = jnp.concatenate([jnp.where(lanes == i, query, zero) for i in range(4)], axis=0)
-    scores = lax.dot_general(
+    return lax.dot_general(
         stacked, keys, (((1,), (1,)), ((), ())), preferred_element_type=jnp.float32
     )
+
+
+def _weigh(scores, values, bias):
     scores = scores + bias
     top = jnp.max(scores, axis=1, keepdims=True)
     weight = jnp.exp(scores - top).astype(jnp.bfloat16)
-    ones = jnp.ones((keys.shape[0], 128), jnp.bfloat16)
+    ones = jnp.ones((values.shape[0], 128), jnp.bfloat16)
     low = lax.broadcasted_iota(jnp.int32, (BLOCK, 128), 1) < HD
     outs, sums, tops = [], [], []
     for pair in range(2):
@@ -142,11 +145,18 @@
                 top[pair * 256 + BLOCK : (pair + 1) * 256],
             )
         )
-    return (
-        jnp.concatenate(outs, axis=1),
-        jnp.concatenate(sums, axis=1),
-        jnp.concatenate(tops, axis=1),
-    )
+    return tuple(jnp.concatenate(x, axis=1) for x in (outs, sums, tops))
+
+
+def _attend(query, keys, values, bias):
+    return _weigh(_scores(query, keys), values, bias)
+
+
+def _join(near, far):
+    both = jnp.maximum(near[2], far[2])
+    a = jnp.exp(near[2] - both)
+    b = jnp.exp(far[2] - both)
+    return a * near[0] + b * far[0], a * near[1] + b * far[1], both
 
 
 def _own_kernel(
@@ -177,11 +187,9 @@
             bias_ref[q : q + 1, :] = row(near)
         glob = jnp.where(gpos_ref[...] < live * BLOCK, 0.0, NEG)
         rows = lane // SUB
-        far = row([((rows % 3 == j), picked(0, j)) for j in range(3)])
-        bias_ref[2:3, :] = jnp.concatenate([far[:, : 3 * BLOCK], glob], axis=1)
-        far = row([((rows % 2 == j), picked(1, j + 1)) for j in range(2)])
-        more = row([(lane >= 0, picked(1, 0))])
-        bias_ref[3:4, :] = jnp.concatenate([far[:, : 2 * BLOCK], glob, more[:, :BLOCK]], axis=1)
+        for q in range(2):
+            far = row([((rows % PICKS == j), picked(q, j)) for j in range(PICKS)])
+            bias_ref[2 + q : 3 + q, :] = jnp.concatenate([far[:, : PICKS * BLOCK], glob], axis=1)
         bias_ref[4:8, :] = jnp.zeros((4, 4 * BLOCK), jnp.float32)
 
 
@@ -245,9 +253,12 @@
     )(lo, hi, bias, q, k, v, w_kv, w_kv)
 
 
-def _finish(acc, out_ref, gain_ref, live):
+def _finish(context, wo_ref, acc, out_ref, gain_ref, live):
+    projected = _dot(context, wo_ref[...])
     tiles = []
-    for c in range(D // 128):
+    for c in range(LT):
+        acc[c] = projected[:, c * 128 : (c + 1) * 128]
+    for c in range(LT):
         total = acc[c, pl.ds(0, 32, stride=POOL), :]
         for i in range(1, POOL):
             total = total + acc[c, pl.ds(i, 32, stride=POOL), :]
@@ -260,112 +271,201 @@
     out_ref[...] = jnp.where(live, normed, 0.0).astype(jnp.bfloat16)
 
 
-def _merge(query, keys, values, bias, o_ref, l_ref, m_ref):
-    out, total, top = _attend(query, keys, values, bias)
-    near = m_ref[...]
-    both = jnp.maximum(near, top)
-    a = jnp.exp(near - both)
-    b = jnp.exp(top - both)
-    return ((a * o_ref[...] + b * out) / (a * l_ref[...] + b * total)).astype(jnp.bfloat16)
-
-
-def _accumulate(step, context, wo_ref, acc):
-    part = _dot(context, wo_ref[...])
-    for c in range(D // 128):
-        piece = part[:, c * 128 : (c + 1) * 128]
-        acc[c] = jnp.where(step == 0, piece, acc[c] + piece)
+def _tile(p, base=0):
+    return slice(base + p * TILE, base + (p + 1) * TILE)
+
+
+def _stage(query, keys_ref, values_ref, scores_ref, weight_ref, bias):
+    width = keys_ref.shape[0]
+    scores_ref[:, :width] = _scores(query, keys_ref[...])
+    tops = []
+    for r in range(0, 4 * BLOCK, 64):
+        piece = scores_ref[r : r + 64, :width] + bias
+        top = jnp.max(piece, axis=1, keepdims=True)
+        weight_ref[r : r + 64, :width] = jnp.exp(piece - top).astype(jnp.bfloat16)
+        tops.append(top)
+    top = jnp.concatenate(tops, axis=0)
+    ones = jnp.ones((width, 128), jnp.bfloat16)
+    low = lax.broadcasted_iota(jnp.int32, (BLOCK, 128), 1) < HD
+    outs, sums, maxes = [], [], []
+    for pair in range(2):
+        base = pair * 256
+        ext = jnp.concatenate([values_ref[:, pair * 128 : (pair + 1) * 128], ones], axis=1)
+        res = _dot(weight_ref[base : base + 256, :width], ext)
+        outs.append(jnp.where(low, res[:BLOCK, :128], res[BLOCK:, :128]))
+        sums.append(jnp.where(low, res[:BLOCK, 128:], res[BLOCK:, 128:]))
+        maxes.append(jnp.where(low, top[base : base + BLOCK], top[base + BLOCK : base + 256]))
+    return tuple(jnp.concatenate(x, axis=1) for x in (outs, sums, maxes))
+
+
+class _Fetch:
+    def __init__(self, half, q_ref, o_ref, l_ref, m_ref, wkv_ref, wo_ref, bufs, sem):
+        q, o, l, m, wkv, wo = bufs
+        self.copies = {}
+        count = 0
+
+        def start(key, src, dst):
+            nonlocal count
+            copy = pltpu.make_async_copy(src, dst, sem.at[count])
+            copy.start()
+            self.copies[key] = copy
+            count += 1
+
+        def weights(p, base):
+            at = _tile(p, base)
+            start(("w", base, p), wkv_ref.at[:, at], wkv.at[:, at])
+
+        weights(0, 0)
+        start("q", q_ref.at[half], q)
+        weights(0, D)
+        weights(1, 0)
+        for key, src, dst in (("o", o_ref, o), ("l", l_ref, l), ("m", m_ref, m)):
+            start(key, src, dst)
+        for p in range(1, STEPS):
+            weights(p, D)
+            if p + 1 < STEPS:
+                weights(p + 1, 0)
+        start("wo", wo_ref, wo)
+
+    def wait(self, *keys):
+        for key in keys:
+            self.copies.pop(key).wait()
 
 
 def _first_kernel(
-    rank_ref, len_ref, rows_ref, bias_ref, q_ref, o_ref, l_ref, m_ref, wk_ref, wv_ref, wo_ref, gain_ref,
-    out_ref, gk_ref, gv_ref, acc,
+    rank_ref, len_ref, rows_ref, bias_ref, q_hbm, o_hbm, l_hbm, m_hbm, wkv_hbm, wo_hbm, gain_ref,
+    out_ref, o1_ref, l1_ref, m1_ref, acc, q_ref, o_ref, l_ref, m_ref, wkv_ref, wo_ref, sem,
+    keys_ref, values_ref, scores_ref, weight_ref, context_ref, scores1_ref, weight1_ref,
 ):
-    step = pl.program_id(0)
-    rows = rows_ref[...]
-
-    def split(w_ref, keep_ref):
-        full = _dot(rows, w_ref[...]).reshape(SHARDS, SUBS_A, SUB, TILE)
-        near = full[:, :PICKS].reshape(PICKS * BLOCK, TILE).astype(jnp.bfloat16)
-        more = full[:, PICKS].reshape(BLOCK, TILE).astype(jnp.bfloat16)
-        glob = full[:, PICKS + 1].reshape(BLOCK, TILE).astype(jnp.bfloat16)
-        keep_ref[:BLOCK, :] = glob
-        keep_ref[BLOCK:, :] = more
-        return jnp.concatenate([near, glob], axis=0)
-
-    keys = split(wk_ref, gk_ref)
-    values = split(wv_ref, gv_ref)
-    context = _merge(q_ref[...], keys, values, bias_ref[2:3, :], o_ref, l_ref, m_ref)
-    _accumulate(step, context, wo_ref, acc)
-
-    @pl.when(step == STEPS - 1)
-    def _():
-        _finish(acc, out_ref, gain_ref, rank_ref[0] * 2 < len_ref[0])
+    fetch = _Fetch(
+        slice(0, ROWS), q_hbm, o_hbm, l_hbm, m_hbm, wkv_hbm, wo_hbm,
+        (q_ref, o_ref, l_ref, m_ref, wkv_ref, wo_ref), sem,
+    )
+    far_rows = PICKS * BLOCK
+
+    def project(p):
+        fetch.wait(("w", 0, p), ("w", D, p))
+        for base, ref in ((0, keys_ref), (D, values_ref)):
+            full = _dot(rows_ref[...], wkv_ref[:, _tile(p, base)]).reshape(SHARDS, SUBS_A, SUB, TILE)
+            ref[p % 2, :far_rows] = full[:, :PICKS].reshape(far_rows, TILE).astype(jnp.bfloat16)
+            ref[p % 2, far_rows:] = full[:, PICKS].reshape(BLOCK, TILE).astype(jnp.bfloat16)
+
+    bias = bias_ref[2:3, :]
+    project(0)
+    fetch.wait("q")
+    for p in range(STEPS):
+        at = _tile(p)
+        if p + 1 < STEPS:
+            project(p + 1)
+        if p == 0:
+            fetch.wait("o", "l", "m")
+        rows = slice(0, BLOCK)
+        far = _stage(
+            q_ref[rows, at], keys_ref.at[p % 2], values_ref.at[p % 2], scores_ref.at[p % 2],
+            weight_ref.at[p % 2], bias,
+        )
+        out, total, _ = _join((o_ref[rows, at], l_ref[rows, at], m_ref[rows, at]), far)
+        context_ref[:, at] = (out / total).astype(jnp.bfloat16)
+        rows = slice(BLOCK, ROWS)
+        glob = pl.ds(far_rows, BLOCK)
+        far = _stage(
+            q_ref[rows, at], keys_ref.at[p % 2, glob], values_ref.at[p % 2, glob],
+            scores1_ref.at[p % 2], weight1_ref.at[p % 2], bias[:, far_rows:],
+        )
+        joined = _join((o_ref[rows, at], l_ref[rows, at], m_ref[rows, at]), far)
+        for ref, val in zip((o1_ref, l1_ref, m1_ref), joined):
+            ref[:, at] = val
+    fetch.wait("wo")
+    _finish(context_ref[...], wo_ref, acc, out_ref, gain_ref, rank_ref[0] * 2 < len_ref[0])
 
 
 def _second_kernel(
-    rank_ref, len_ref, rows_ref, bias_ref, q_ref, o_ref, l_ref, m_ref, wk_ref, wv_ref, wo_ref, gain_ref,
-    gk_ref, gv_ref, prev_ref, out_ref, acc,
+    rank_ref, len_ref, rows_ref, bias_ref, q_hbm, o_hbm, l_hbm, m_hbm, wkv_hbm, wo_hbm, gain_ref,
+    prev_ref, out_ref, acc, q_ref, o_ref, l_ref, m_ref, wkv_ref, wo_ref, sem,
+    keys_ref, values_ref, scores_ref, weight_ref, context_ref,
 ):
-    step = pl.program_id(0)
-    rows = rows_ref[...]
-    keys = jnp.concatenate([_dot(rows, wk_ref[...]).astype(jnp.bfloat16), gk_ref[...]], axis=0)
-    values = jnp.concatenate([_dot(rows, wv_ref[...]).astype(jnp.bfloat16), gv_ref[...]], axis=0)
-    context = _merge(q_ref[...], keys, values, bias_ref[3:4, :], o_ref, l_ref, m_ref)
-    _accumulate(step, context, wo_ref, acc)
-
-    @pl.when(step == STEPS - 1)
-    def _():
-        _finish(acc, out_ref, gain_ref, rank_ref[0] * 2 + 1 < len_ref[0])
-
-
-def _half(b):
-    return pl.BlockSpec((BLOCK, TILE), lambda p: (b, p))
-
-
-def _late_specs(b):
-    return [
-        *[pl.BlockSpec(memory_space=SM)] * 2,
-        pl.BlockSpec(memory_space=VM),
-        _whole((8, 4 * BLOCK)),
-        *[_half(b)] * 4,
-        _cols(D),
-        _cols(D, STEPS),
-        pl.BlockSpec((TILE, D), lambda p: (p, 0)),
-        _whole((1, D)),
+    fetch = _Fetch(
+        slice(BLOCK, ROWS), q_hbm, o_hbm, l_hbm, m_hbm, wkv_hbm, wo_hbm,
+        (q_ref, o_ref, l_ref, m_ref, wkv_ref, wo_ref), sem,
+    )
+
+    def project(p):
+        fetch.wait(("w", 0, p), ("w", D, p))
+        for base, ref in ((0, keys_ref), (D, values_ref)):
+            ref[p % 2] = _dot(rows_ref[...], wkv_ref[:, _tile(p, base)]).astype(jnp.bfloat16)
+
+    bias = bias_ref[3:4, : PICKS * BLOCK]
+    project(0)
+    fetch.wait("q")
+    for p in range(STEPS):
+        at = _tile(p)
+        if p + 1 < STEPS:
+            project(p + 1)
+        if p == 0:
+            fetch.wait("o", "l", "m")
+        far = _stage(
+            q_ref[:, at], keys_ref.at[p % 2], values_ref.at[p % 2], scores_ref.at[p % 2],
+            weight_ref.at[p % 2], bias,
+        )
+        near = (o_ref[:, at], l_ref[:, at], m_ref[:, at])
+        out, total, _ = _join(near, far)
+        context_ref[:, at] = (out / total).astype(jnp.bfloat16)
+    fetch.wait("wo")
+    _finish(context_ref[...], wo_ref, acc, out_ref, gain_ref, rank_ref[0] * 2 + 1 < len_ref[0])
+
+
+def _late(rows, *widths):
+    wide = widths[0]
+    scratch = [
+        VM((LT, BLOCK, 128), jnp.float32),
+        VM((rows, D), jnp.bfloat16),
+        *[VM((rows, D), jnp.float32)] * 3,
+        VM((D, 2 * D), jnp.bfloat16),
+        VM((D, D), jnp.bfloat16),
+        pltpu.SemaphoreType.DMA((2 * STEPS + 5,)),
+        VM((2, wide, TILE), jnp.bfloat16),
+        VM((2, wide, TILE), jnp.bfloat16),
+        VM((2, 4 * BLOCK, wide), jnp.float32),
+        VM((2, 4 * BLOCK, wide), jnp.bfloat16),
+        VM((BLOCK, D), jnp.bfloat16),
     ]
+    for width in widths[1:]:
+        scratch += [VM((2, 4 * BLOCK, width), jnp.float32), VM((2, 4 * BLOCK, width), jnp.bfloat16)]
+    return dict(grid=(1,), scratch_shapes=scratch)
+
+
+LATE_SPECS = [
+    *[pl.BlockSpec(memory_space=SM)] * 2,
+    *[pl.BlockSpec(memory_space=VM)] * 2,
+    *[pl.BlockSpec(memory_space=pl.ANY)] * 6,
+    pl.BlockSpec(memory_space=VM),
+]
 
 
 def first(rank, length, rows, bias, q, o, l, m, w_kv, w_out, gain):
-    kept = jax.ShapeDtypeStruct((2 * BLOCK, D), jnp.bfloat16)
+    f32 = jax.ShapeDtypeStruct((BLOCK, D), jnp.float32)
     rows = pltpu.with_memory_space_constraint(rows, VM)
     return pl.pallas_call(
         _first_kernel,
-        grid=(STEPS,),
-        out_shape=(jax.ShapeDtypeStruct((64, D), jnp.bfloat16), kept, kept),
-        in_specs=_late_specs(0),
-        out_specs=(pl.BlockSpec((32, D), lambda p: (0, 0)), _cols(2 * BLOCK), _cols(2 * BLOCK)),
-        scratch_shapes=[pltpu.VMEM((D // 128, BLOCK, 128), jnp.float32)],
+        out_shape=(jax.ShapeDtypeStruct((64, D), jnp.bfloat16), f32, f32, f32),
+        in_specs=LATE_SPECS,
+        out_specs=(pl.BlockSpec((32, D), lambda p: (0, 0)),) + (_whole((BLOCK, D)),) * 3,
         name="first",
-    )(rank, length, rows, bias, q, o, l, m, w_kv, w_kv, w_out, gain)
-
-
-def second(rank, length, rows, bias, q, o, l, m, w_kv, w_out, gain, gk, gv, prev):
+        **_late(ROWS, SUBS_A * BLOCK, BLOCK),
+    )(rank, length, rows, bias, q, o, l, m, w_kv, w_out, gain)
+
+
+def second(rank, length, rows, bias, q, o, l, m, w_kv, w_out, gain, prev):
     rows = pltpu.with_memory_space_constraint(rows, VM)
     return pl.pallas_call(
         _second_kernel,
-        grid=(STEPS,),
         out_shape=jax.ShapeDtypeStruct((64, D), jnp.bfloat16),
-        in_specs=[
-            *_late_specs(1),
-            _cols(2 * BLOCK),
-            _cols(2 * BLOCK),
-            pl.BlockSpec(memory_space=pl.ANY),
-        ],
+        in_specs=LATE_SPECS + [pl.BlockSpec(memory_space=pl.ANY)],
         out_specs=pl.BlockSpec((32, D), lambda p: (1, 0)),
-        scratch_shapes=[pltpu.VMEM((D // 128, BLOCK, 128), jnp.float32)],
-        input_output_aliases={14: 0},
+        input_output_aliases={11: 0},
         name="second",
-    )(rank, length, rows, bias, q, o, l, m, w_kv, w_kv, w_out, gain, gk, gv, prev)
+        **_late(BLOCK, SUBS_B * BLOCK),
+    )(rank, length, rows, bias, q, o, l, m, w_kv, w_out, gain, prev)
 
 
 def exchange(value):
@@ -388,8 +488,8 @@
     got_a = exchange(send_a).reshape(SUBS_A * BLOCK, D)
     got_b = exchange(send_b).reshape(SUBS_B * BLOCK, D)
     o, l, m = halo_part(lo, hi, bias, q, k, v, w_kv)
-    half, gk, gv = first(rank, length, got_a, bias, q, o, l, m, w_kv, w_out, gain)
-    return second(rank, length, got_b, bias, q, o, l, m, w_kv, w_out, gain, gk, gv, half)
+    half, o1, l1, m1 = first(rank, length, got_a, bias, q, o, l, m, w_kv, w_out, gain)
+    return second(rank, length, got_b, bias, q, o1, l1, m1, w_kv, w_out, gain, half)
 
 
 def solution(mesh):

time: 110 us -> 107 us (0.973)
  the two profiles are of different devices: /device:TPU:104 before, /device:TPU:2 now
where the time goes in v4:
time: 107 us; the launch traced here: 105 us
  blocking collectives  45.5 us (43%)
  Pallas kernels  44.8 us (42%)
  starting transfers between devices  10.8 us (10%)
  local copies, waits for them, and re-layouts  1.38 us (1%)
  waiting for transfers between devices  1.18 us (1%)
    all_to_all x2, blocking collectives, exchange(): return lax.all_to_all(value, 'tm', split_axis=0, concat_axis=0, tiled=True)  45.5 us
    pallas_call x1, Pallas kernels, first(): pl.pallas_call(_first_kernel, out_shape=(jax.ShapeDtypeStruct((64, D), jn...  12.8 us
    pallas_call x1, Pallas kernels, halo_part(): pl.pallas_call(_halo_kernel, grid=(STEPS,), out_shape=(f32, f32, f32), in...  10.5 us
    pallas_call x1, Pallas kernels, second(): pl.pallas_call(_second_kernel, out_shape=jax.ShapeDtypeStruct((64, D), jn...  10.1 us
    pallas_call x1, Pallas kernels, own_part(): pl.pallas_call(_own_kernel, grid=(STEPS,), out_shape=(half, half, half, j...  8.24 us
    all_to_all x1, starting transfers between devices, exchange(): return lax.all_to_all(value, 'tm', split_axis=0, concat_axis=0, tiled=True)  5.02 us
    ppermute x1, starting transfers between devices, program(): lo = lax.ppermute(frames[BLOCK:], 'tm', up)  3.71 us
  transfers between devices with their start and end apart: 3, of which 1 were waited for; matrix products, arithmetic and copies ran while one was open for 1% of the time, Pallas kernels for 30%

profile of v4, /device:TPU:2, one launch (start us, length us, event | category | flops | bytes accessed | tf_op | source)
XLA Modules:
  0.0 104.6 jit_solution(6803352523374342762)
XLA Ops:
  0.0 1.5 %pack.1 = bf16[16,31,8,128]{3,2,1,0:T(8,128)(2,1)S(1)} custom-call(s32[1]{0:T(128)} %bitcast.rank_ref, s32[2,3]{1,0:T(2,128)} %owner_ref.3, s32[2,3]{1,0:T(2,128)} %slot_ref.3, bf16[256,1280]{1,0:T(8,128)(2,1)} %own_ref.1, s32[1,128]{1,0:T(1,128)} %bitcast.6), custom_call_target="tpu_custom_call" | custom-call | tf_op jit(solution)/shard_map/pack/pallas_call | solution.py:55
  1.5 22.7 %all_to_all.15.held_ref = bf16[16,31,8,128]{3,2,1,0:T(8,128)(2,1)S(1)} all-to-all(bf16[16,31,8,128]{3,2,1,0:T(8,128)(2,1)S(1)} %pack.1), channel_id=1, replica_groups=mesh['rec'=16,'tm'=16] {'tm'}, dimensions={0} | all-to-all | bytes 2031616 | tf_op jit(solution)/shard_map/all_to_all | solution.py:472
  24.2 1.7 %select.1 = (bf16[16,4,8,1280]{3,2,1,0:T(8,128)(2,1)}, bf16[16,3,8,1280]{3,2,1,0:T(8,128)(2,1)}) custom-call(bf16[16,31,8,128]{3,2,1,0:T(8,128)(2,1)S(1)} %all_to_all.15.held_ref), custom_call_target="tpu_custom_call" | custom-call | tf_op jit(solution)/shard_map/select/pallas_call | solution.py:100
  25.9 22.7 %all_to_all.16 = bf16[16,4,8,1280]{3,2,1,0:T(8,128)(2,1)S(1)} all-to-all(bf16[16,4,8,1280]{3,2,1,0:T(8,128)(2,1)} %get-tuple-element.21), channel_id=1, replica_groups=mesh['rec'=16,'tm'=16] {'tm'}, dimensions={0} | all-to-all | bytes 2621440 | tf_op jit(solution)/shard_map/all_to_all | solution.py:472
  48.7 0.0 copy-start
  48.7 0.0 copy-start.1
  48.7 5.0 %all-to-all-start.1 = ((bf16[16,3,8,1280]{3,2,1,0:T(8,128)(2,1)}), bf16[16,3,8,1280]{3,2,1,0:T(8,128)(2,1)S(1)}, u32[]{:S(2)}, u32[]{:S(2)}) async-start(bf16[16,3,8,1280]{3,2,1,0:T(8,128)(2,1)} %get-tuple-element.18), calls=%async_computation.1 | async-start | bytes 1966080 | tf_op jit(solution)/shard_map/all_to_all | solution.py:472
  53.7 0.0 copy-done
  53.7 0.8 fusion
  54.5 2.1 %collective-permute-start.1 = (bf16[128,1280]{1,0:T(8,128)(2,1)}, bf16[128,1280]{1,0:T(8,128)(2,1)S(1)}, u32[]{:S(2)}, u32[]{:S(2)}) collective-permute-start(bf16[128,1280]{1,0:T(8,128)(2,1)} %get-tuple-element.31), channel_id=1, source_target_pairs={{1,0},{2,1},{3,2},{4,3},{5,4},{6,5},{7,6},{8,7},{9,8},{10,9},{11,1... | collective-permute-start | bytes 983048 | tf_op jit(solution)/shard_map/ppermute | solution.py:486
  56.6 3.7 %collective-permute-start = (bf16[128,1280]{1,0:T(8,128)(2,1)S(1)}, bf16[128,1280]{1,0:T(8,128)(2,1)S(1)}, u32[]{:S(2)}, u32[]{:S(2)}) collective-permute-start(bf16[128,1280]{1,0:T(8,128)(2,1)S(1)} %get-tuple-element.32), channel_id=1, source_target_pairs={{0,1},{1,2},{2,3},{3,4},{4,5},{5,6},{6,7},{7,8},{8,9},{9,10},{10,1... | collective-permute-start | bytes 983048 | tf_op jit(solution)/shard_map/ppermute | solution.py:485
  61.0 0.0 copy-done.1
  61.0 0.6 reshape.19.gain_ref
  61.6 8.2 %own.1 = (bf16[256,1280]{1,0:T(8,128)(2,1)}, bf16[256,1280]{1,0:T(8,128)(2,1)}, bf16[256,1280]{1,0:T(8,128)(2,1)}, f32[8,512]{1,0:T(8,128)}) custom-call(s32[1]{0:T(128)} %bitcast.rank_ref, s32[1]{0:T(128)S(6)} %copy.12.len_ref, s32[2,3]{1,0:T(2,128)} %owner_ref.3, s32[2,3]{1,0:T(2,128)} %slot_ref.3, s32[1,128]{1,0:T(1,128)} %bitcast.7, ...), custom_call_target="tpu_custom_call" | custom-call | tf_op jit(solution)/shard_map/own/pallas_call | solution.py:224
  69.8 1.2 %collective-permute-done.1.hi_ref = bf16[128,1280]{1,0:T(8,128)(2,1)S(1)} collective-permute-done((bf16[128,1280]{1,0:T(8,128)(2,1)}, bf16[128,1280]{1,0:T(8,128)(2,1)S(1)}, u32[]{:S(2)}, u32[]{:S(2)}) %collective-permute-start.1) | collective-permute-done | bytes 327712 | tf_op jit(solution)/shard_map/ppermute | solution.py:486
  71.0 0.0 collective-permute-done.lo_ref
  71.0 10.5 %halo.1 = (f32[256,1280]{1,0:T(8,128)}, f32[256,1280]{1,0:T(8,128)}, f32[256,1280]{1,0:T(8,128)}) custom-call(bf16[128,1280]{1,0:T(8,128)(2,1)S(1)} %collective-permute-done.lo_ref, bf16[128,1280]{1,0:T(8,128)(2,1)S(1)} %collective-permute-done.1.hi_ref, f32[8,512]{1,0:T(8,128)} %get-tuple-element.19.bias_ref, ...), custom_call_target="tpu_custom_call" | custom-call | tf_op jit(solution)/shard_map/halo/pallas_call | solution.py:239
  81.5 12.8 %first.1 = (bf16[64,1280]{1,0:T(8,128)(2,1)}, f32[128,1280]{1,0:T(8,128)}, f32[128,1280]{1,0:T(8,128)}, f32[128,1280]{1,0:T(8,128)}) custom-call(s32[1]{0:T(128)} %bitcast.rank_ref, s32[1]{0:T(128)S(6)} %copy.12.len_ref, bf16[512,1280]{1,0:T(8,128)(2,1)S(1)} %bitcast.4, f32[8,512]{1,0:T(8,128)} %get-tuple-element.19.bias_ref, ...), custom_call_target="tpu_custom_call" | custom-call | tf_op jit(solution)/shard_map/first/pallas_call | solution.py:448
  94.3 0.0 all-to-all-done.1
  94.3 10.1 %second.1 = bf16[64,1280]{1,0:T(8,128)(2,1)} custom-call(s32[1]{0:T(128)} %bitcast.rank_ref, s32[1]{0:T(128)S(6)} %copy.12.len_ref, bf16[384,1280]{1,0:T(8,128)(2,1)S(1)} %bitcast.5, f32[8,512]{1,0:T(8,128)} %get-tuple-element.19.bias_ref, bf16[256,1280]{1,0:T(8,128)(2,1)} %get-tuple-element.20.q_ref.q_hbm, ...), custom_call_target="tpu_custom_call", output_to_operand_aliasing={{}: (11, {})} | custom-call | tf_op jit(solution)/shard_map/second/pallas_call | solution.py:460
Async XLA Ops:
  48.7 5.0 %copy-start = (bf16[256,1280]{1,0:T(8,128)(2,1)S(1)}, bf16[256,1280]{1,0:T(8,128)(2,1)}, u32[]{:S(2)}) copy-start(bf16[256,1280]{1,0:T(8,128)(2,1)} %own_ref.1) | copy-start | bytes 1966084
  48.7 12.3 %copy-start.1 = (f32[1280]{0:T(1024)S(1)}, f32[1280]{0:T(1024)}, u32[]{:S(2)}) copy-start(f32[1280]{0:T(1024)} %param.13) | copy-start | bytes 15364
  48.7 45.7 %all-to-all-start.1 = ((bf16[16,3,8,1280]{3,2,1,0:T(8,128)(2,1)}), bf16[16,3,8,1280]{3,2,1,0:T(8,128)(2,1)S(1)}, u32[]{:S(2)}, u32[]{:S(2)}) async-start(bf16[16,3,8,1280]{3,2,1,0:T(8,128)(2,1)} %get-tuple-element.18), calls=%async_computation.1 | async-start | bytes 1966080 | tf_op jit(solution)/shard_map/all_to_all | solution.py:472
  54.5 16.5 %collective-permute-start.1 = (bf16[128,1280]{1,0:T(8,128)(2,1)}, bf16[128,1280]{1,0:T(8,128)(2,1)S(1)}, u32[]{:S(2)}, u32[]{:S(2)}) collective-permute-start(bf16[128,1280]{1,0:T(8,128)(2,1)} %get-tuple-element.31), channel_id=1, source_target_pairs={{1,0},{2,1},{3,2},{4,3},{5,4},{6,5},{7,6},{8,7},{9,8},{10,9},{11,1... | collective-permute-start | bytes 983048 | tf_op jit(solution)/shard_map/ppermute | solution.py:486
  56.6 14.4 %collective-permute-start = (bf16[128,1280]{1,0:T(8,128)(2,1)S(1)}, bf16[128,1280]{1,0:T(8,128)(2,1)S(1)}, u32[]{:S(2)}, u32[]{:S(2)}) collective-permute-start(bf16[128,1280]{1,0:T(8,128)(2,1)S(1)} %get-tuple-element.32), channel_id=1, source_target_pairs={{0,1},{1,2},{2,3},{3,4},{4,5},{5,6},{6,7},{7,8},{8,9},{9,10},{10,1... | collective-permute-start | bytes 983048 | tf_op jit(solution)/shard_map/ppermute | solution.py:485

commit v5 on v4

--- a/solution.py
+++ b/solution.py
@@ -16,8 +16,7 @@
 SHARDS = 16
 SUB = BLOCK // SHARDS
 ROWS = 256
-SUBS_A = 4
-SUBS_B = 3
+SUBS = 2 * PICKS + 1
 LT = D // 128
 NEG = -1e30
 
@@ -61,7 +60,7 @@
     )(rank, owner, slot, frames, gpos)
 
 
-def _select_kernel(held_ref, a_ref, b_ref, buf, sem):
+def _select_kernel(held_ref, out_ref, buf, sem):
     copies = []
 
     def send(k, dest):
@@ -86,12 +85,12 @@
         total = total.astype(jnp.bfloat16)
         for r in range(SHARDS):
             buf[2 * PICKS, r, :, c * 128 : (c + 1) * 128] = total
-    send(2 * PICKS, a_ref.at[:, SUBS_A - 1])
+    send(2 * PICKS, out_ref.at[:, 2 * PICKS])
     for k in range(2 * PICKS):
         onehot = jnp.where(cols == codes[:, k : k + 1], 1.0, 0.0).astype(jnp.bfloat16)
         got = jnp.dot(onehot, rows, preferred_element_type=jnp.float32)
         buf[k] = got.reshape(SHARDS, SUB, D).astype(jnp.bfloat16)
-        send(k, a_ref.at[:, k] if k < SUBS_A - 1 else b_ref.at[:, k - SUBS_A + 1])
+        send(k, out_ref.at[:, k])
     for copy in copies:
         copy.wait()
 
@@ -99,12 +98,9 @@
 def select(held):
     return pl.pallas_call(
         _select_kernel,
-        out_shape=(
-            jax.ShapeDtypeStruct((SHARDS, SUBS_A, SUB, D), jnp.bfloat16),
-            jax.ShapeDtypeStruct((SHARDS, SUBS_B, SUB, D), jnp.bfloat16),
-        ),
+        out_shape=jax.ShapeDtypeStruct((SHARDS, SUBS, SUB, D), jnp.bfloat16),
         in_specs=[pl.BlockSpec(memory_space=VM)],
-        out_specs=(pl.BlockSpec(memory_space=pl.ANY), pl.BlockSpec(memory_space=pl.ANY)),
+        out_specs=pl.BlockSpec(memory_space=pl.ANY),
         scratch_shapes=[
             pltpu.VMEM((2 * PICKS + 1, SHARDS, SUB, D), jnp.bfloat16),
             pltpu.SemaphoreType.DMA((2 * PICKS + 1,)),
@@ -189,7 +185,8 @@
         rows = lane // SUB
         for q in range(2):
             far = row([((rows % PICKS == j), picked(q, j)) for j in range(PICKS)])
-            bias_ref[2 + q : 3 + q, :] = jnp.concatenate([far[:, : PICKS * BLOCK], glob], axis=1)
+            parts = [far[:, : PICKS * BLOCK], glob]
+            bias_ref[2 + q : 3 + q, :] = jnp.concatenate(parts if q == 0 else parts[::-1], axis=1)
         bias_ref[4:8, :] = jnp.zeros((4, 4 * BLOCK), jnp.float32)
 
 
@@ -253,8 +250,7 @@
     )(lo, hi, bias, q, k, v, w_kv, w_kv)
 
 
-def _finish(context, wo_ref, acc, out_ref, gain_ref, live):
-    projected = _dot(context, wo_ref[...])
+def _finish(projected, acc, gain_ref, live):
     tiles = []
     for c in range(LT):
         acc[c] = projected[:, c * 128 : (c + 1) * 128]
@@ -268,7 +264,7 @@
     centered = pooled - mean
     var = jnp.mean(centered * centered, axis=1, keepdims=True)
     normed = centered * lax.rsqrt(var + 1e-05) * gain_ref[...]
-    out_ref[...] = jnp.where(live, normed, 0.0).astype(jnp.bfloat16)
+    return jnp.where(live, normed, 0.0).astype(jnp.bfloat16)
 
 
 def _tile(p, base=0):
@@ -299,7 +295,7 @@
 
 
 class _Fetch:
-    def __init__(self, half, q_ref, o_ref, l_ref, m_ref, wkv_ref, wo_ref, bufs, sem):
+    def __init__(self, q_ref, o_ref, l_ref, m_ref, wkv_ref, wo_ref, bufs, sem):
         q, o, l, m, wkv, wo = bufs
         self.copies = {}
         count = 0
@@ -316,7 +312,7 @@
             start(("w", base, p), wkv_ref.at[:, at], wkv.at[:, at])
 
         weights(0, 0)
-        start("q", q_ref.at[half], q)
+        start("q", q_ref, q)
         weights(0, D)
         weights(1, 0)
         for key, src, dst in (("o", o_ref, o), ("l", l_ref, l), ("m", m_ref, m)):
@@ -332,25 +328,25 @@
             self.copies.pop(key).wait()
 
 
-def _first_kernel(
+def _late_kernel(
     rank_ref, len_ref, rows_ref, bias_ref, q_hbm, o_hbm, l_hbm, m_hbm, wkv_hbm, wo_hbm, gain_ref,
-    out_ref, o1_ref, l1_ref, m1_ref, acc, q_ref, o_ref, l_ref, m_ref, wkv_ref, wo_ref, sem,
-    keys_ref, values_ref, scores_ref, weight_ref, context_ref, scores1_ref, weight1_ref,
+    out_ref, acc, q_ref, o_ref, l_ref, m_ref, wkv_ref, wo_ref, sem,
+    keys_ref, values_ref, scores_ref, weight_ref, context_ref,
 ):
     fetch = _Fetch(
-        slice(0, ROWS), q_hbm, o_hbm, l_hbm, m_hbm, wkv_hbm, wo_hbm,
-        (q_ref, o_ref, l_ref, m_ref, wkv_ref, wo_ref), sem,
+        q_hbm, o_hbm, l_hbm, m_hbm, wkv_hbm, wo_hbm, (q_ref, o_ref, l_ref, m_ref, wkv_ref, wo_ref), sem
     )
-    far_rows = PICKS * BLOCK
+    near = PICKS * BLOCK
 
     def project(p):
         fetch.wait(("w", 0, p), ("w", D, p))
-        for base, ref in ((0, keys_ref), (D, values_ref)):
-            full = _dot(rows_ref[...], wkv_ref[:, _tile(p, base)]).reshape(SHARDS, SUBS_A, SUB, TILE)
-            ref[p % 2, :far_rows] = full[:, :PICKS].reshape(far_rows, TILE).astype(jnp.bfloat16)
-            ref[p % 2, far_rows:] = full[:, PICKS].reshape(BLOCK, TILE).astype(jnp.bfloat16)
-
-    bias = bias_ref[2:3, :]
+        both = [_dot(rows_ref[...], wkv_ref[:, _tile(p, base)]) for base in (0, D)]
+        for full, ref in zip(both, (keys_ref, values_ref)):
+            full = full.reshape(SHARDS, SUBS, SUB, TILE)
+            ref[p % 2, :near] = full[:, :PICKS].reshape(near, TILE).astype(jnp.bfloat16)
+            ref[p % 2, near : near + BLOCK] = full[:, 2 * PICKS].reshape(BLOCK, TILE).astype(jnp.bfloat16)
+            ref[p % 2, near + BLOCK :] = full[:, PICKS : 2 * PICKS].reshape(near, TILE).astype(jnp.bfloat16)
+
     project(0)
     fetch.wait("q")
     for p in range(STEPS):
@@ -359,113 +355,50 @@
             project(p + 1)
         if p == 0:
             fetch.wait("o", "l", "m")
-        rows = slice(0, BLOCK)
-        far = _stage(
-            q_ref[rows, at], keys_ref.at[p % 2], values_ref.at[p % 2], scores_ref.at[p % 2],
-            weight_ref.at[p % 2], bias,
-        )
-        out, total, _ = _join((o_ref[rows, at], l_ref[rows, at], m_ref[rows, at]), far)
-        context_ref[:, at] = (out / total).astype(jnp.bfloat16)
-        rows = slice(BLOCK, ROWS)
-        glob = pl.ds(far_rows, BLOCK)
-        far = _stage(
-            q_ref[rows, at], keys_ref.at[p % 2, glob], values_ref.at[p % 2, glob],
-            scores1_ref.at[p % 2], weight1_ref.at[p % 2], bias[:, far_rows:],
-        )
-        joined = _join((o_ref[rows, at], l_ref[rows, at], m_ref[rows, at]), far)
-        for ref, val in zip((o1_ref, l1_ref, m1_ref), joined):
-            ref[:, at] = val
+        for b in range(2):
+            rows = slice(b * BLOCK, (b + 1) * BLOCK)
+            used = pl.ds(b * near, near + BLOCK)
+            far = _stage(
+                q_ref[rows, at], keys_ref.at[p % 2, used], values_ref.at[p % 2, used],
+                scores_ref.at[b], weight_ref.at[b], bias_ref[2 + b : 3 + b, :],
+            )
+            out, total, _ = _join((o_ref[rows, at], l_ref[rows, at], m_ref[rows, at]), far)
+            context_ref[rows, at] = (out / total).astype(jnp.bfloat16)
     fetch.wait("wo")
-    _finish(context_ref[...], wo_ref, acc, out_ref, gain_ref, rank_ref[0] * 2 < len_ref[0])
-
-
-def _second_kernel(
-    rank_ref, len_ref, rows_ref, bias_ref, q_hbm, o_hbm, l_hbm, m_hbm, wkv_hbm, wo_hbm, gain_ref,
-    prev_ref, out_ref, acc, q_ref, o_ref, l_ref, m_ref, wkv_ref, wo_ref, sem,
-    keys_ref, values_ref, scores_ref, weight_ref, context_ref,
-):
-    fetch = _Fetch(
-        slice(BLOCK, ROWS), q_hbm, o_hbm, l_hbm, m_hbm, wkv_hbm, wo_hbm,
-        (q_ref, o_ref, l_ref, m_ref, wkv_ref, wo_ref), sem,
-    )
-
-    def project(p):
-        fetch.wait(("w", 0, p), ("w", D, p))
-        for base, ref in ((0, keys_ref), (D, values_ref)):
-            ref[p % 2] = _dot(rows_ref[...], wkv_ref[:, _tile(p, base)]).astype(jnp.bfloat16)
-
-    bias = bias_ref[3:4, : PICKS * BLOCK]
-    project(0)
-    fetch.wait("q")
-    for p in range(STEPS):
-        at = _tile(p)
-        if p + 1 < STEPS:
-            project(p + 1)
-        if p == 0:
-            fetch.wait("o", "l", "m")
-        far = _stage(
-            q_ref[:, at], keys_ref.at[p % 2], values_ref.at[p % 2], scores_ref.at[p % 2],
-            weight_ref.at[p % 2], bias,
-        )
-        near = (o_ref[:, at], l_ref[:, at], m_ref[:, at])
-        out, total, _ = _join(near, far)
-        context_ref[:, at] = (out / total).astype(jnp.bfloat16)
-    fetch.wait("wo")
-    _finish(context_ref[...], wo_ref, acc, out_ref, gain_ref, rank_ref[0] * 2 + 1 < len_ref[0])
-
-
-def _late(rows, *widths):
-    wide = widths[0]
-    scratch = [
-        VM((LT, BLOCK, 128), jnp.float32),
-        VM((rows, D), jnp.bfloat16),
-        *[VM((rows, D), jnp.float32)] * 3,
-        VM((D, 2 * D), jnp.bfloat16),
-        VM((D, D), jnp.bfloat16),
-        pltpu.SemaphoreType.DMA((2 * STEPS + 5,)),
-        VM((2, wide, TILE), jnp.bfloat16),
-        VM((2, wide, TILE), jnp.bfloat16),
-        VM((2, 4 * BLOCK, wide), jnp.float32),
-        VM((2, 4 * BLOCK, wide), jnp.bfloat16),
-        VM((BLOCK, D), jnp.bfloat16),
-    ]
-    for width in widths[1:]:
-        scratch += [VM((2, 4 * BLOCK, width), jnp.float32), VM((2, 4 * BLOCK, width), jnp.bfloat16)]
-    return dict(grid=(1,), scratch_shapes=scratch)
-
-
-LATE_SPECS = [
-    *[pl.BlockSpec(memory_space=SM)] * 2,
-    *[pl.BlockSpec(memory_space=VM)] * 2,
-    *[pl.BlockSpec(memory_space=pl.ANY)] * 6,
-    pl.BlockSpec(memory_space=VM),
-]
-
-
-def first(rank, length, rows, bias, q, o, l, m, w_kv, w_out, gain):
-    f32 = jax.ShapeDtypeStruct((BLOCK, D), jnp.float32)
+    projected = _dot(context_ref[...], wo_ref[...])
+    for b in range(2):
+        live = rank_ref[0] * 2 + b < len_ref[0]
+        part = projected[b * BLOCK : (b + 1) * BLOCK]
+        out_ref[b * 32 : (b + 1) * 32, :] = _finish(part, acc.at[b], gain_ref, live)
+
+
+def late(rank, length, rows, bias, q, o, l, m, w_kv, w_out, gain):
     rows = pltpu.with_memory_space_constraint(rows, VM)
     return pl.pallas_call(
-        _first_kernel,
-        out_shape=(jax.ShapeDtypeStruct((64, D), jnp.bfloat16), f32, f32, f32),
-        in_specs=LATE_SPECS,
-        out_specs=(pl.BlockSpec((32, D), lambda p: (0, 0)),) + (_whole((BLOCK, D)),) * 3,
-        name="first",
-        **_late(ROWS, SUBS_A * BLOCK, BLOCK),
+        _late_kernel,
+        out_shape=jax.ShapeDtypeStruct((64, D), jnp.bfloat16),
+        in_specs=[
+            *[pl.BlockSpec(memory_space=SM)] * 2,
+            *[pl.BlockSpec(memory_space=VM)] * 2,
+            *[pl.BlockSpec(memory_space=pl.ANY)] * 6,
+            pl.BlockSpec(memory_space=VM),
+        ],
+        out_specs=pl.BlockSpec(memory_space=VM),
+        scratch_shapes=[
+            VM((2, LT, BLOCK, 128), jnp.float32),
+            VM((ROWS, D), jnp.bfloat16),
+            *[VM((ROWS, D), jnp.float32)] * 3,
+            VM((D, 2 * D), jnp.bfloat16),
+            VM((D, D), jnp.bfloat16),
+            pltpu.SemaphoreType.DMA((2 * STEPS + 5,)),
+            VM((2, SUBS * BLOCK, TILE), jnp.bfloat16),
+            VM((2, SUBS * BLOCK, TILE), jnp.bfloat16),
+            VM((2, 4 * BLOCK, 4 * BLOCK), jnp.float32),
+            VM((2, 4 * BLOCK, 4 * BLOCK), jnp.bfloat16),
+            VM((ROWS, D), jnp.bfloat16),
+        ],
+        name="late",
     )(rank, length, rows, bias, q, o, l, m, w_kv, w_out, gain)
-
-
-def second(rank, length, rows, bias, q, o, l, m, w_kv, w_out, gain, prev):
-    rows = pltpu.with_memory_space_constraint(rows, VM)
-    return pl.pallas_call(
-        _second_kernel,
-        out_shape=jax.ShapeDtypeStruct((64, D), jnp.bfloat16),
-        in_specs=LATE_SPECS + [pl.BlockSpec(memory_space=pl.ANY)],
-        out_specs=pl.BlockSpec((32, D), lambda p: (1, 0)),
-        input_output_aliases={11: 0},
-        name="second",
-        **_late(BLOCK, SUBS_B * BLOCK),
-    )(rank, length, rows, bias, q, o, l, m, w_kv, w_out, gain, prev)
 
 
 def exchange(value):
@@ -484,12 +417,10 @@
     q, k, v, bias = own_part(rank, length, rand_owner, rand_slot, gpos, frames, w_query, w_kv)
     lo = lax.ppermute(frames[BLOCK:], "tm", up)
     hi = lax.ppermute(frames[:BLOCK], "tm", down)
-    send_a, send_b = select(held)
-    got_a = exchange(send_a).reshape(SUBS_A * BLOCK, D)
-    got_b = exchange(send_b).reshape(SUBS_B * BLOCK, D)
+    reply = select(held)
+    got = exchange(reply).reshape(SUBS * BLOCK, D)
     o, l, m = halo_part(lo, hi, bias, q, k, v, w_kv)
-    half, o1, l1, m1 = first(rank, length, got_a, bias, q, o, l, m, w_kv, w_out, gain)
-    return second(rank, length, got_b, bias, q, o1, l1, m1, w_kv, w_out, gain, half)
+    return late(rank, length, got, bias, q, o, l, m, w_kv, w_out, gain)
 
 
 def solution(mesh):

time: 107 us -> 94.2 us (0.88); the launches traced: 105 us -> 92.9 us
  blocking collectives: 45.5 us -> 22.7 us
  waiting for transfers between devices: 1.18 us -> 18.8 us
  Pallas kernels: 44.8 us -> 38.4 us
    all_to_all x2 -> x1, blocking collectives: 45.5 us -> 22.7 us  [exchange(): return lax.all_to_all(value, 'tm', split_axis=0, concat_axis=0, tiled=True)]
    ppermute x1, waiting for transfers between devices: 0.01 us -> 18.1 us  [program(): lo = lax.ppermute(frames[BLOCK:], 'tm', up)]
    pallas_call x3 -> x2, Pallas kernels: 24.6 us -> 18 us  [the longest x1 16.4 us: late(): pl.pallas_call(_late_kernel, out_shape=jax.ShapeDtypeStruct((64, D), jnp....]
  transfers between devices with their start and end apart: 3 -> 3, of which waited for: 1 -> 2; matrix products, arithmetic and copies ran while one was open for 1% -> 1% of each run, Pallas kernels for 30% -> 20%
where the time goes in v5:
time: 94.2 us; the launch traced here: 92.9 us
  Pallas kernels  38.4 us (41%)
  blocking collectives  22.7 us (24%)
  waiting for transfers between devices  18.8 us (20%)
  starting transfers between devices  11 us (12%)
  local copies, waits for them, and re-layouts  1.37 us (1%)
    all_to_all x1, blocking collectives, exchange(): return lax.all_to_all(value, 'tm', split_axis=0, concat_axis=0, tiled=True)  22.7 us
    ppermute x1, waiting for transfers between devices, program(): lo = lax.ppermute(frames[BLOCK:], 'tm', up)  18.1 us
    pallas_call x1, Pallas kernels, late(): pl.pallas_call(_late_kernel, out_shape=jax.ShapeDtypeStruct((64, D), jnp....  16.4 us
    pallas_call x1, Pallas kernels, halo_part(): pl.pallas_call(_halo_kernel, grid=(STEPS,), out_shape=(f32, f32, f32), in...  10.6 us
    pallas_call x1, Pallas kernels, own_part(): pl.pallas_call(_own_kernel, grid=(STEPS,), out_shape=(half, half, half, j...  8.25 us
    all_to_all x1, starting transfers between devices, exchange(): return lax.all_to_all(value, 'tm', split_axis=0, concat_axis=0, tiled=True)  5.12 us
    ppermute x1, starting transfers between devices, program(): lo = lax.ppermute(frames[BLOCK:], 'tm', up)  3.37 us
    ppermute x1, starting transfers between devices, program(): hi = lax.ppermute(frames[:BLOCK], 'tm', down)  2.48 us
  transfers between devices with their start and end apart: 3, of which 2 were waited for; matrix products, arithmetic and copies ran while one was open for 1% of the time, Pallas kernels for 20%

profile of v5, /device:TPU:2, one launch (start us, length us, event | category | flops | bytes accessed | tf_op | source)
XLA Modules:
  0.0 92.9 jit_solution(6362572925800881141)
XLA Ops:
  0.0 1.5 %pack.1 = bf16[16,31,8,128]{3,2,1,0:T(8,128)(2,1)S(1)} custom-call(s32[1]{0:T(128)} %bitcast.rank_ref, s32[2,3]{1,0:T(2,128)} %owner_ref.3, s32[2,3]{1,0:T(2,128)} %slot_ref.3, bf16[256,1280]{1,0:T(8,128)(2,1)} %own_ref.1, s32[1,128]{1,0:T(1,128)} %bitcast.4), custom_call_target="tpu_custom_call" | custom-call | tf_op jit(solution)/shard_map/pack/pallas_call | solution.py:54
  1.5 22.7 %all_to_all.10.held_ref = bf16[16,31,8,128]{3,2,1,0:T(8,128)(2,1)S(1)} all-to-all(bf16[16,31,8,128]{3,2,1,0:T(8,128)(2,1)S(1)} %pack.1), channel_id=1, replica_groups=mesh['rec'=16,'tm'=16] {'tm'}, dimensions={0} | all-to-all | bytes 2031616 | tf_op jit(solution)/shard_map/all_to_all | solution.py:405
  24.2 1.7 %select.1 = bf16[16,7,8,1280]{3,2,1,0:T(8,128)(2,1)} custom-call(bf16[16,31,8,128]{3,2,1,0:T(8,128)(2,1)S(1)} %all_to_all.10.held_ref), custom_call_target="tpu_custom_call" | custom-call | tf_op jit(solution)/shard_map/select/pallas_call | solution.py:99
  25.9 0.0 copy-start
  25.9 0.0 copy-start.1
  25.9 5.1 %all-to-all-start.1 = ((bf16[16,7,8,1280]{3,2,1,0:T(8,128)(2,1)}), bf16[16,7,8,1280]{3,2,1,0:T(8,128)(2,1)S(1)}, u32[]{:S(2)}, u32[]{:S(2)}) async-start(bf16[16,7,8,1280]{3,2,1,0:T(8,128)(2,1)} %select.1), calls=%async_computation.1 | async-start | bytes 4587520 | tf_op jit(solution)/shard_map/all_to_all | solution.py:405
  31.0 0.0 copy-done
  31.0 0.8 fusion
  31.8 3.4 %collective-permute-start = (bf16[128,1280]{1,0:T(8,128)(2,1)}, bf16[128,1280]{1,0:T(8,128)(2,1)S(1)}, u32[]{:S(2)}, u32[]{:S(2)}) collective-permute-start(bf16[128,1280]{1,0:T(8,128)(2,1)} %get-tuple-element.20), channel_id=1, source_target_pairs={{0,1},{1,2},{2,3},{3,4},{4,5},{5,6},{6,7},{7,8},{8,9},{9,10},{10,1... | collective-permute-start | bytes 983048 | tf_op jit(solution)/shard_map/ppermute | solution.py:418
  35.2 2.5 %collective-permute-start.1 = (bf16[128,1280]{1,0:T(8,128)(2,1)S(1)}, bf16[128,1280]{1,0:T(8,128)(2,1)S(1)}, u32[]{:S(2)}, u32[]{:S(2)}) collective-permute-start(bf16[128,1280]{1,0:T(8,128)(2,1)S(1)} %get-tuple-element.19), channel_id=1, source_target_pairs={{1,0},{2,1},{3,2},{4,3},{5,4},{6,5},{7,6},{8,7},{9,8},{10,9},{11,1... | collective-permute-start | bytes 983048 | tf_op jit(solution)/shard_map/ppermute | solution.py:419
  38.3 0.0 copy-done.1
  38.3 0.6 reshape.15.gain_ref
  38.9 8.3 %own.1 = (bf16[256,1280]{1,0:T(8,128)(2,1)}, bf16[256,1280]{1,0:T(8,128)(2,1)}, bf16[256,1280]{1,0:T(8,128)(2,1)}, f32[8,512]{1,0:T(8,128)}) custom-call(s32[1]{0:T(128)} %bitcast.rank_ref, s32[1]{0:T(128)S(6)} %copy.10.len_ref, s32[2,3]{1,0:T(2,128)} %owner_ref.3, s32[2,3]{1,0:T(2,128)} %slot_ref.3, s32[1,128]{1,0:T(1,128)} %bitcast.5, ...), custom_call_target="tpu_custom_call" | custom-call | tf_op jit(solution)/shard_map/own/pallas_call | solution.py:221
  47.2 18.1 %collective-permute-done.lo_ref = bf16[128,1280]{1,0:T(8,128)(2,1)S(1)} collective-permute-done((bf16[128,1280]{1,0:T(8,128)(2,1)}, bf16[128,1280]{1,0:T(8,128)(2,1)S(1)}, u32[]{:S(2)}, u32[]{:S(2)}) %collective-permute-start) | collective-permute-done | bytes 327712 | tf_op jit(solution)/shard_map/ppermute | solution.py:418
  65.3 0.7 collective-permute-done.1.hi_ref
  66.0 10.6 %halo.1 = (f32[256,1280]{1,0:T(8,128)}, f32[256,1280]{1,0:T(8,128)}, f32[256,1280]{1,0:T(8,128)}) custom-call(bf16[128,1280]{1,0:T(8,128)(2,1)S(1)} %collective-permute-done.lo_ref, bf16[128,1280]{1,0:T(8,128)(2,1)S(1)} %collective-permute-done.1.hi_ref, f32[8,512]{1,0:T(8,128)} %get-tuple-element.12.bias_ref, ...), custom_call_target="tpu_custom_call" | custom-call | tf_op jit(solution)/shard_map/halo/pallas_call | solution.py:236
  76.6 0.0 all-to-all-done.1
  76.6 16.4 %late.1 = bf16[64,1280]{1,0:T(8,128)(2,1)} custom-call(s32[1]{0:T(128)} %bitcast.rank_ref, s32[1]{0:T(128)S(6)} %copy.10.len_ref, bf16[896,1280]{1,0:T(8,128)(2,1)S(1)} %bitcast.3, f32[8,512]{1,0:T(8,128)} %get-tuple-element.12.bias_ref, bf16[256,1280]{1,0:T(8,128)(2,1)} %get-tuple-element.13.q_ref.q_hbm, f32[256,1280]{1,0:T(8,128)} %get-tuple-element.16.o_hbm, ...), custom_call_target="tpu_custom_call" | custom-call | tf_op jit(solution)/shard_map/late/pallas_call | solution.py:377
Async XLA Ops:
  25.9 5.1 %copy-start = (bf16[256,1280]{1,0:T(8,128)(2,1)S(1)}, bf16[256,1280]{1,0:T(8,128)(2,1)}, u32[]{:S(2)}) copy-start(bf16[256,1280]{1,0:T(8,128)(2,1)} %own_ref.1) | copy-start | bytes 1966084
  25.9 12.4 %copy-start.1 = (f32[1280]{0:T(1024)S(1)}, f32[1280]{0:T(1024)}, u32[]{:S(2)}) copy-start(f32[1280]{0:T(1024)} %param.13) | copy-start | bytes 15364
  25.9 50.6 %all-to-all-start.1 = ((bf16[16,7,8,1280]{3,2,1,0:T(8,128)(2,1)}), bf16[16,7,8,1280]{3,2,1,0:T(8,128)(2,1)S(1)}, u32[]{:S(2)}, u32[]{:S(2)}) async-start(bf16[16,7,8,1280]{3,2,1,0:T(8,128)(2,1)} %select.1), calls=%async_computation.1 | async-start | bytes 4587520 | tf_op jit(solution)/shard_map/all_to_all | solution.py:405
  31.8 33.5 %collective-permute-start = (bf16[128,1280]{1,0:T(8,128)(2,1)}, bf16[128,1280]{1,0:T(8,128)(2,1)S(1)}, u32[]{:S(2)}, u32[]{:S(2)}) collective-permute-start(bf16[128,1280]{1,0:T(8,128)(2,1)} %get-tuple-element.20), channel_id=1, source_target_pairs={{0,1},{1,2},{2,3},{3,4},{4,5},{5,6},{6,7},{7,8},{8,9},{9,10},{10,1... | collective-permute-start | bytes 983048 | tf_op jit(solution)/shard_map/ppermute | solution.py:418
  35.2 30.8 %collective-permute-start.1 = (bf16[128,1280]{1,0:T(8,128)(2,1)S(1)}, bf16[128,1280]{1,0:T(8,128)(2,1)S(1)}, u32[]{:S(2)}, u32[]{:S(2)}) collective-permute-start(bf16[128,1280]{1,0:T(8,128)(2,1)S(1)} %get-tuple-element.19), channel_id=1, source_target_pairs={{1,0},{2,1},{3,2},{4,3},{5,4},{6,5},{7,6},{8,7},{9,8},{10,9},{11,1... | collective-permute-start | bytes 983048 | tf_op jit(solution)/shard_map/ppermute | solution.py:419

commit v6 on v4

--- a/solution.py
+++ b/solution.py
@@ -16,8 +16,8 @@
 SHARDS = 16
 SUB = BLOCK // SHARDS
 ROWS = 256
-SUBS_A = 4
-SUBS_B = 3
+SUBS_A = PICKS + 2
+SUBS_B = PICKS - 1
 LT = D // 128
 NEG = -1e30
 
@@ -160,9 +160,10 @@
 
 
 def _own_kernel(
-    rank_ref, len_ref, owner_ref, slot_ref, gpos_ref, own_ref, wq_ref, wk_ref, wv_ref,
-    q_ref, k_ref, v_ref, bias_ref,
+    rank_ref, len_ref, owner_ref, slot_ref, gpos_ref, own_ref, gain_ref, wq_ref, wk_ref, wv_ref,
+    q_ref, k_ref, v_ref, bias_ref, keep_ref,
 ):
+    keep_ref[...] = gain_ref[...]
     own = own_ref[...]
     q_ref[...] = _dot(own, wq_ref[...]).astype(jnp.bfloat16) * jnp.bfloat16(0.125)
     k_ref[...] = _dot(own, wk_ref[...]).astype(jnp.bfloat16)
@@ -187,9 +188,12 @@
             bias_ref[q : q + 1, :] = row(near)
         glob = jnp.where(gpos_ref[...] < live * BLOCK, 0.0, NEG)
         rows = lane // SUB
-        for q in range(2):
-            far = row([((rows % PICKS == j), picked(q, j)) for j in range(PICKS)])
-            bias_ref[2 + q : 3 + q, :] = jnp.concatenate([far[:, : PICKS * BLOCK], glob], axis=1)
+        far = row([(rows % PICKS == j, picked(0, j)) for j in range(PICKS)])
+        bias_ref[2:3, :] = jnp.concatenate([far[:, : PICKS * BLOCK], glob], axis=1)
+        one = row([(lane >= 0, picked(1, 0))])
+        far = row([(rows % SUBS_B == j, picked(1, j + 1)) for j in range(SUBS_B)])
+        parts = [glob, one[:, :BLOCK], far[:, : SUBS_B * BLOCK]]
+        bias_ref[3:4, :] = jnp.concatenate(parts, axis=1)
         bias_ref[4:8, :] = jnp.zeros((4, 4 * BLOCK), jnp.float32)
 
 
@@ -219,17 +223,21 @@
     return pl.BlockSpec((rows, TILE), lambda p: (0, p + shift))
 
 
-def own_part(rank, length, owner, slot, gpos, own, w_query, w_kv):
+def own_part(rank, length, owner, slot, gpos, own, gain, w_query, w_kv):
     half = jax.ShapeDtypeStruct((ROWS, D), jnp.bfloat16)
     return pl.pallas_call(
         _own_kernel,
         grid=(STEPS,),
-        out_shape=(half, half, half, jax.ShapeDtypeStruct((8, 4 * BLOCK), jnp.float32)),
+        out_shape=(
+            half, half, half,
+            jax.ShapeDtypeStruct((8, 4 * BLOCK), jnp.float32),
+            jax.ShapeDtypeStruct((1, D), jnp.float32),
+        ),
         in_specs=[pl.BlockSpec(memory_space=SM)] * 4
-        + [_whole((1, BLOCK)), _whole((ROWS, D)), _cols(D), _cols(D), _cols(D, STEPS)],
-        out_specs=(_cols(ROWS),) * 3 + (_whole((8, 4 * BLOCK)),),
+        + [_whole((1, BLOCK)), _whole((ROWS, D)), _whole((1, D)), _cols(D), _cols(D), _cols(D, STEPS)],
+        out_specs=(_cols(ROWS),) * 3 + (_whole((8, 4 * BLOCK)), _whole((1, D))),
         name="own",
-    )(rank, length, owner, slot, gpos, own, w_query, w_kv, w_kv)
+    )(rank, length, owner, slot, gpos, own, gain, w_query, w_kv, w_kv)
 
 
 def halo_part(lo, hi, bias, q, k, v, w_kv):
@@ -253,8 +261,7 @@
     )(lo, hi, bias, q, k, v, w_kv, w_kv)
 
 
-def _finish(context, wo_ref, acc, out_ref, gain_ref, live):
-    projected = _dot(context, wo_ref[...])
+def _finish(projected, acc, gain_ref, live):
     tiles = []
     for c in range(LT):
         acc[c] = projected[:, c * 128 : (c + 1) * 128]
@@ -268,7 +275,7 @@
     centered = pooled - mean
     var = jnp.mean(centered * centered, axis=1, keepdims=True)
     normed = centered * lax.rsqrt(var + 1e-05) * gain_ref[...]
-    out_ref[...] = jnp.where(live, normed, 0.0).astype(jnp.bfloat16)
+    return jnp.where(live, normed, 0.0).astype(jnp.bfloat16)
 
 
 def _tile(p, base=0):
@@ -299,7 +306,7 @@
 
 
 class _Fetch:
-    def __init__(self, half, q_ref, o_ref, l_ref, m_ref, wkv_ref, wo_ref, bufs, sem):
+    def __init__(self, q_ref, o_ref, l_ref, m_ref, wkv_ref, wo_ref, bufs, sem):
         q, o, l, m, wkv, wo = bufs
         self.copies = {}
         count = 0
@@ -316,7 +323,7 @@
             start(("w", base, p), wkv_ref.at[:, at], wkv.at[:, at])
 
         weights(0, 0)
-        start("q", q_ref.at[half], q)
+        start("q", q_ref, q)
         weights(0, D)
         weights(1, 0)
         for key, src, dst in (("o", o_ref, o), ("l", l_ref, l), ("m", m_ref, m)):
@@ -335,22 +342,22 @@
 def _first_kernel(
     rank_ref, len_ref, rows_ref, bias_ref, q_hbm, o_hbm, l_hbm, m_hbm, wkv_hbm, wo_hbm, gain_ref,
     out_ref, o1_ref, l1_ref, m1_ref, acc, q_ref, o_ref, l_ref, m_ref, wkv_ref, wo_ref, sem,
-    keys_ref, values_ref, scores_ref, weight_ref, context_ref, scores1_ref, weight1_ref,
+    keys_ref, values_ref, context_ref, scores_ref, weight_ref, scores1_ref, weight1_ref,
 ):
     fetch = _Fetch(
-        slice(0, ROWS), q_hbm, o_hbm, l_hbm, m_hbm, wkv_hbm, wo_hbm,
-        (q_ref, o_ref, l_ref, m_ref, wkv_ref, wo_ref), sem,
+        q_hbm, o_hbm, l_hbm, m_hbm, wkv_hbm, wo_hbm, (q_ref, o_ref, l_ref, m_ref, wkv_ref, wo_ref), sem
     )
-    far_rows = PICKS * BLOCK
+    near = PICKS * BLOCK
 
     def project(p):
         fetch.wait(("w", 0, p), ("w", D, p))
-        for base, ref in ((0, keys_ref), (D, values_ref)):
-            full = _dot(rows_ref[...], wkv_ref[:, _tile(p, base)]).reshape(SHARDS, SUBS_A, SUB, TILE)
-            ref[p % 2, :far_rows] = full[:, :PICKS].reshape(far_rows, TILE).astype(jnp.bfloat16)
-            ref[p % 2, far_rows:] = full[:, PICKS].reshape(BLOCK, TILE).astype(jnp.bfloat16)
-
-    bias = bias_ref[2:3, :]
+        both = [_dot(rows_ref[...], wkv_ref[:, _tile(p, base)]) for base in (0, D)]
+        for full, ref in zip(both, (keys_ref, values_ref)):
+            full = full.reshape(SHARDS, SUBS_A, SUB, TILE)
+            ref[p % 2, :near] = full[:, :PICKS].reshape(near, TILE).astype(jnp.bfloat16)
+            ref[p % 2, near : near + BLOCK] = full[:, PICKS + 1].reshape(BLOCK, TILE).astype(jnp.bfloat16)
+            ref[p % 2, near + BLOCK :] = full[:, PICKS].reshape(BLOCK, TILE).astype(jnp.bfloat16)
+
     project(0)
     fetch.wait("q")
     for p in range(STEPS):
@@ -360,41 +367,43 @@
         if p == 0:
             fetch.wait("o", "l", "m")
         rows = slice(0, BLOCK)
+        used = pl.ds(0, near + BLOCK)
         far = _stage(
-            q_ref[rows, at], keys_ref.at[p % 2], values_ref.at[p % 2], scores_ref.at[p % 2],
-            weight_ref.at[p % 2], bias,
+            q_ref[rows, at], keys_ref.at[p % 2, used], values_ref.at[p % 2, used],
+            scores_ref.at[p % 2], weight_ref.at[p % 2], bias_ref[2:3, :],
         )
         out, total, _ = _join((o_ref[rows, at], l_ref[rows, at], m_ref[rows, at]), far)
         context_ref[:, at] = (out / total).astype(jnp.bfloat16)
         rows = slice(BLOCK, ROWS)
-        glob = pl.ds(far_rows, BLOCK)
+        used = pl.ds(near, 2 * BLOCK)
         far = _stage(
-            q_ref[rows, at], keys_ref.at[p % 2, glob], values_ref.at[p % 2, glob],
-            scores1_ref.at[p % 2], weight1_ref.at[p % 2], bias[:, far_rows:],
+            q_ref[rows, at], keys_ref.at[p % 2, used], values_ref.at[p % 2, used],
+            scores1_ref.at[p % 2], weight1_ref.at[p % 2], bias_ref[3:4, : 2 * BLOCK],
         )
         joined = _join((o_ref[rows, at], l_ref[rows, at], m_ref[rows, at]), far)
         for ref, val in zip((o1_ref, l1_ref, m1_ref), joined):
             ref[:, at] = val
     fetch.wait("wo")
-    _finish(context_ref[...], wo_ref, acc, out_ref, gain_ref, rank_ref[0] * 2 < len_ref[0])
+    projected = _dot(context_ref[...], wo_ref[...])
+    out_ref[...] = _finish(projected, acc, gain_ref, rank_ref[0] * 2 < len_ref[0])
 
 
 def _second_kernel(
     rank_ref, len_ref, rows_ref, bias_ref, q_hbm, o_hbm, l_hbm, m_hbm, wkv_hbm, wo_hbm, gain_ref,
     prev_ref, out_ref, acc, q_ref, o_ref, l_ref, m_ref, wkv_ref, wo_ref, sem,
-    keys_ref, values_ref, scores_ref, weight_ref, context_ref,
+    keys_ref, values_ref, context_ref, scores_ref, weight_ref,
 ):
     fetch = _Fetch(
-        slice(BLOCK, ROWS), q_hbm, o_hbm, l_hbm, m_hbm, wkv_hbm, wo_hbm,
+        q_hbm.at[pl.ds(BLOCK, BLOCK)], o_hbm, l_hbm, m_hbm, wkv_hbm, wo_hbm,
         (q_ref, o_ref, l_ref, m_ref, wkv_ref, wo_ref), sem,
     )
 
     def project(p):
         fetch.wait(("w", 0, p), ("w", D, p))
-        for base, ref in ((0, keys_ref), (D, values_ref)):
-            ref[p % 2] = _dot(rows_ref[...], wkv_ref[:, _tile(p, base)]).astype(jnp.bfloat16)
-
-    bias = bias_ref[3:4, : PICKS * BLOCK]
+        both = [_dot(rows_ref[...], wkv_ref[:, _tile(p, base)]) for base in (0, D)]
+        for full, ref in zip(both, (keys_ref, values_ref)):
+            ref[p % 2] = full.astype(jnp.bfloat16)
+
     project(0)
     fetch.wait("q")
     for p in range(STEPS):
@@ -405,17 +414,16 @@
             fetch.wait("o", "l", "m")
         far = _stage(
             q_ref[:, at], keys_ref.at[p % 2], values_ref.at[p % 2], scores_ref.at[p % 2],
-            weight_ref.at[p % 2], bias,
+            weight_ref.at[p % 2], bias_ref[3:4, 2 * BLOCK :],
         )
-        near = (o_ref[:, at], l_ref[:, at], m_ref[:, at])
-        out, total, _ = _join(near, far)
+        out, total, _ = _join((o_ref[:, at], l_ref[:, at], m_ref[:, at]), far)
         context_ref[:, at] = (out / total).astype(jnp.bfloat16)
     fetch.wait("wo")
-    _finish(context_ref[...], wo_ref, acc, out_ref, gain_ref, rank_ref[0] * 2 + 1 < len_ref[0])
-
-
-def _late(rows, *widths):
-    wide = widths[0]
+    projected = _dot(context_ref[...], wo_ref[...])
+    out_ref[...] = _finish(projected, acc, gain_ref, rank_ref[0] * 2 + 1 < len_ref[0])
+
+
+def _late(rows, wide, *widths):
     scratch = [
         VM((LT, BLOCK, 128), jnp.float32),
         VM((rows, D), jnp.bfloat16),
@@ -425,11 +433,9 @@
         pltpu.SemaphoreType.DMA((2 * STEPS + 5,)),
         VM((2, wide, TILE), jnp.bfloat16),
         VM((2, wide, TILE), jnp.bfloat16),
-        VM((2, 4 * BLOCK, wide), jnp.float32),
-        VM((2, 4 * BLOCK, wide), jnp.bfloat16),
         VM((BLOCK, D), jnp.bfloat16),
     ]
-    for width in widths[1:]:
+    for width in widths:
         scratch += [VM((2, 4 * BLOCK, width), jnp.float32), VM((2, 4 * BLOCK, width), jnp.bfloat16)]
     return dict(grid=(1,), scratch_shapes=scratch)
 
@@ -451,7 +457,7 @@
         in_specs=LATE_SPECS,
         out_specs=(pl.BlockSpec((32, D), lambda p: (0, 0)),) + (_whole((BLOCK, D)),) * 3,
         name="first",
-        **_late(ROWS, SUBS_A * BLOCK, BLOCK),
+        **_late(ROWS, SUBS_A * BLOCK, 4 * BLOCK, 2 * BLOCK),
     )(rank, length, rows, bias, q, o, l, m, w_kv, w_out, gain)
 
 
@@ -464,7 +470,7 @@
         out_specs=pl.BlockSpec((32, D), lambda p: (1, 0)),
         input_output_aliases={11: 0},
         name="second",
-        **_late(BLOCK, SUBS_B * BLOCK),
+        **_late(BLOCK, SUBS_B * BLOCK, SUBS_B * BLOCK),
     )(rank, length, rows, bias, q, o, l, m, w_kv, w_out, gain, prev)
 
 
@@ -481,7 +487,9 @@
     down = [(j, i) for i, j in up]
     packed = pack(rank, rand_owner, rand_slot, frames, gpos)
     held = exchange(packed)
-    q, k, v, bias = own_part(rank, length, rand_owner, rand_slot, gpos, frames, w_query, w_kv)
+    q, k, v, bias, gain = own_part(
+        rank, length, rand_owner, rand_slot, gpos, frames, gain, w_query, w_kv
+    )
     lo = lax.ppermute(frames[BLOCK:], "tm", up)
     hi = lax.ppermute(frames[:BLOCK], "tm", down)
     send_a, send_b = select(held)

time: 107 us -> 109 us (1.019)
  the two profiles are of different devices: /device:TPU:2 before, /device:TPU:230 now
where the time goes in v6:
time: 109 us; the launch traced here: 108 us
  blocking collectives  48.5 us (44%)
  Pallas kernels  44 us (40%)
  starting transfers between devices  13.5 us (12%)
  local copies, waits for them, and re-layouts  1.38 us (1%)
    all_to_all x2, blocking collectives, exchange(): return lax.all_to_all(value, 'tm', split_axis=0, concat_axis=0, tiled=True)  48.5 us
    pallas_call x1, Pallas kernels, first(): pl.pallas_call(_first_kernel, out_shape=(jax.ShapeDtypeStruct((64, D), jn...  13.4 us
    pallas_call x1, Pallas kernels, halo_part(): pl.pallas_call(_halo_kernel, grid=(STEPS,), out_shape=(f32, f32, f32), in...  10.6 us
    pallas_call x1, Pallas kernels, second(): pl.pallas_call(_second_kernel, out_shape=jax.ShapeDtypeStruct((64, D), jn...  8.88 us
    pallas_call x1, Pallas kernels, own_part(): pl.pallas_call(_own_kernel, grid=(STEPS,), out_shape=(half, half, half, j...  8.05 us
    all_to_all x1, starting transfers between devices, exchange(): return lax.all_to_all(value, 'tm', split_axis=0, concat_axis=0, tiled=True)  5.6 us
    ppermute x1, starting transfers between devices, program(): lo = lax.ppermute(frames[BLOCK:], 'tm', up)  5.19 us
    ppermute x1, starting transfers between devices, program(): hi = lax.ppermute(frames[:BLOCK], 'tm', down)  2.75 us
  transfers between devices with their start and end apart: 3, of which 0 were waited for; matrix products, arithmetic and copies ran while one was open for 1% of the time, Pallas kernels for 30%

profile of v6, /device:TPU:230, one launch (start us, length us, event | category | flops | bytes accessed | tf_op | source)
XLA Modules:
  0.0 108.3 jit_solution(17546315390936162629)
XLA Ops:
  0.0 1.5 %pack.1 = bf16[16,31,8,128]{3,2,1,0:T(8,128)(2,1)S(1)} custom-call(s32[1]{0:T(128)} %bitcast.rank_ref, s32[2,3]{1,0:T(2,128)} %owner_ref.3, s32[2,3]{1,0:T(2,128)} %slot_ref.3, bf16[256,1280]{1,0:T(8,128)(2,1)} %own_ref.1, s32[1,128]{1,0:T(1,128)} %bitcast.6), custom_call_target="tpu_custom_call" | custom-call | tf_op jit(solution)/shard_map/pack/pallas_call | solution.py:55
  1.5 21.4 %all_to_all.15.held_ref = bf16[16,31,8,128]{3,2,1,0:T(8,128)(2,1)S(1)} all-to-all(bf16[16,31,8,128]{3,2,1,0:T(8,128)(2,1)S(1)} %pack.1), channel_id=1, replica_groups=mesh['rec'=16,'tm'=16] {'tm'}, dimensions={0} | all-to-all | bytes 2031616 | tf_op jit(solution)/shard_map/all_to_all | solution.py:478
  22.9 1.7 %select.1 = (bf16[16,5,8,1280]{3,2,1,0:T(8,128)(2,1)}, bf16[16,2,8,1280]{3,2,1,0:T(8,128)(2,1)}) custom-call(bf16[16,31,8,128]{3,2,1,0:T(8,128)(2,1)S(1)} %all_to_all.15.held_ref), custom_call_target="tpu_custom_call" | custom-call | tf_op jit(solution)/shard_map/select/pallas_call | solution.py:100
  24.6 0.0 copy-start
  24.6 27.1 %all_to_all.16 = bf16[16,5,8,1280]{3,2,1,0:T(8,128)(2,1)S(1)} all-to-all(bf16[16,5,8,1280]{3,2,1,0:T(8,128)(2,1)} %get-tuple-element.22), channel_id=1, replica_groups=mesh['rec'=16,'tm'=16] {'tm'}, dimensions={0} | all-to-all | bytes 3276800 | tf_op jit(solution)/shard_map/all_to_all | solution.py:478
  51.7 0.0 copy-start.1
  51.7 5.6 %all-to-all-start.1 = ((bf16[16,2,8,1280]{3,2,1,0:T(8,128)(2,1)}), bf16[16,2,8,1280]{3,2,1,0:T(8,128)(2,1)S(1)}, u32[]{:S(2)}, u32[]{:S(2)}) async-start(bf16[16,2,8,1280]{3,2,1,0:T(8,128)(2,1)} %get-tuple-element.19), calls=%async_computation.1 | async-start | bytes 1310720 | tf_op jit(solution)/shard_map/all_to_all | solution.py:478
  57.3 0.0 copy-done
  57.3 0.8 fusion
  58.1 2.7 %collective-permute-start.1 = (bf16[128,1280]{1,0:T(8,128)(2,1)}, bf16[128,1280]{1,0:T(8,128)(2,1)S(1)}, u32[]{:S(2)}, u32[]{:S(2)}) collective-permute-start(bf16[128,1280]{1,0:T(8,128)(2,1)} %get-tuple-element.33), channel_id=1, source_target_pairs={{1,0},{2,1},{3,2},{4,3},{5,4},{6,5},{7,6},{8,7},{9,8},{10,9},{11,1... | collective-permute-start | bytes 983048 | tf_op jit(solution)/shard_map/ppermute | solution.py:494
  60.8 5.2 %collective-permute-start = (bf16[128,1280]{1,0:T(8,128)(2,1)S(1)}, bf16[128,1280]{1,0:T(8,128)(2,1)S(1)}, u32[]{:S(2)}, u32[]{:S(2)}) collective-permute-start(bf16[128,1280]{1,0:T(8,128)(2,1)S(1)} %get-tuple-element.34), channel_id=1, source_target_pairs={{0,1},{1,2},{2,3},{3,4},{4,5},{5,6},{6,7},{7,8},{8,9},{9,10},{10,1... | collective-permute-start | bytes 983048 | tf_op jit(solution)/shard_map/ppermute | solution.py:493
  66.7 0.0 copy-done.1
  66.7 0.6 reshape.18.gain_ref
  67.3 8.0 %own.1 = (bf16[256,1280]{1,0:T(8,128)(2,1)}, bf16[256,1280]{1,0:T(8,128)(2,1)}, bf16[256,1280]{1,0:T(8,128)(2,1)}, f32[8,512]{1,0:T(8,128)}, f32[1,1280]{1,0:T(1,128)}) custom-call(s32[1]{0:T(128)} %bitcast.rank_ref, s32[1]{0:T(128)S(6)} %copy.12.len_ref, s32[2,3]{1,0:T(2,128)} %owner_ref.3, s32[2,3]{1,0:T(2,128)} %slot_ref.3, s32[1,128]{1,0:T(1,128)} %bitcast.7, ...), custom_call_target="tpu_custom_call" | custom-call | tf_op jit(solution)/shard_map/own/pallas_call | solution.py:228
  75.3 0.0 collective-permute-done.1.hi_ref
  75.3 0.0 collective-permute-done.lo_ref
  75.3 10.6 %halo.1 = (f32[256,1280]{1,0:T(8,128)}, f32[256,1280]{1,0:T(8,128)}, f32[256,1280]{1,0:T(8,128)}) custom-call(bf16[128,1280]{1,0:T(8,128)(2,1)S(1)} %collective-permute-done.lo_ref, bf16[128,1280]{1,0:T(8,128)(2,1)S(1)} %collective-permute-done.1.hi_ref, f32[8,512]{1,0:T(8,128)} %get-tuple-element.20.bias_ref, ...), custom_call_target="tpu_custom_call" | custom-call | tf_op jit(solution)/shard_map/halo/pallas_call | solution.py:247
  85.9 13.4 %first.1 = (bf16[64,1280]{1,0:T(8,128)(2,1)}, f32[128,1280]{1,0:T(8,128)}, f32[128,1280]{1,0:T(8,128)}, f32[128,1280]{1,0:T(8,128)}) custom-call(s32[1]{0:T(128)} %bitcast.rank_ref, s32[1]{0:T(128)S(6)} %copy.12.len_ref, bf16[640,1280]{1,0:T(8,128)(2,1)S(1)} %bitcast.4, f32[8,512]{1,0:T(8,128)} %get-tuple-element.20.bias_ref, ...), custom_call_target="tpu_custom_call" | custom-call | tf_op jit(solution)/shard_map/first/pallas_call | solution.py:454
  99.2 0.0 all-to-all-done.1
  99.3 8.9 %second.1 = bf16[64,1280]{1,0:T(8,128)(2,1)} custom-call(s32[1]{0:T(128)} %bitcast.rank_ref, s32[1]{0:T(128)S(6)} %copy.12.len_ref, bf16[256,1280]{1,0:T(8,128)(2,1)S(1)} %bitcast.5, f32[8,512]{1,0:T(8,128)} %get-tuple-element.20.bias_ref, bf16[256,1280]{1,0:T(8,128)(2,1)} %get-tuple-element.21.q_ref.q_hbm, ...), custom_call_target="tpu_custom_call", output_to_operand_aliasing={{}: (11, {})} | custom-call | tf_op jit(solution)/shard_map/second/pallas_call | solution.py:466
Async XLA Ops:
  24.6 32.7 %copy-start = (bf16[256,1280]{1,0:T(8,128)(2,1)S(1)}, bf16[256,1280]{1,0:T(8,128)(2,1)}, u32[]{:S(2)}) copy-start(bf16[256,1280]{1,0:T(8,128)(2,1)} %own_ref.1) | copy-start | bytes 1966084
  51.7 15.0 %copy-start.1 = (f32[1280]{0:T(1024)S(1)}, f32[1280]{0:T(1024)}, u32[]{:S(2)}) copy-start(f32[1280]{0:T(1024)} %param.13) | copy-start | bytes 15364
  51.7 47.6 %all-to-all-start.1 = ((bf16[16,2,8,1280]{3,2,1,0:T(8,128)(2,1)}), bf16[16,2,8,1280]{3,2,1,0:T(8,128)(2,1)S(1)}, u32[]{:S(2)}, u32[]{:S(2)}) async-start(bf16[16,2,8,1280]{3,2,1,0:T(8,128)(2,1)} %get-tuple-element.19), calls=%async_computation.1 | async-start | bytes 1310720 | tf_op jit(solution)/shard_map/all_to_all | solution.py:478
  58.1 17.3 %collective-permute-start.1 = (bf16[128,1280]{1,0:T(8,128)(2,1)}, bf16[128,1280]{1,0:T(8,128)(2,1)S(1)}, u32[]{:S(2)}, u32[]{:S(2)}) collective-permute-start(bf16[128,1280]{1,0:T(8,128)(2,1)} %get-tuple-element.33), channel_id=1, source_target_pairs={{1,0},{2,1},{3,2},{4,3},{5,4},{6,5},{7,6},{8,7},{9,8},{10,9},{11,1... | collective-permute-start | bytes 983048 | tf_op jit(solution)/shard_map/ppermute | solution.py:494
  60.8 14.5 %collective-permute-start = (bf16[128,1280]{1,0:T(8,128)(2,1)S(1)}, bf16[128,1280]{1,0:T(8,128)(2,1)S(1)}, u32[]{:S(2)}, u32[]{:S(2)}) collective-permute-start(bf16[128,1280]{1,0:T(8,128)(2,1)S(1)} %get-tuple-element.34), channel_id=1, source_target_pairs={{0,1},{1,2},{2,3},{3,4},{4,5},{5,6},{6,7},{7,8},{8,9},{9,10},{10,1... | collective-permute-start | bytes 983048 | tf_op jit(solution)/shard_map/ppermute | solution.py:493

commit v7 on v5

--- a/solution.py
+++ b/solution.py
@@ -24,20 +24,20 @@
 SM = pltpu.SMEM
 
 
-def _pack_kernel(rank_ref, owner_ref, slot_ref, frames_ref, gpos_ref, out_ref):
-    frames = frames_ref[...]
+def _pack_kernel(rank_ref, owner_ref, slot_ref, gpos_ref, frames_hbm, out_hbm, frames_ref, more_ref, sem):
+    load = pltpu.make_async_copy(frames_hbm, frames_ref, sem.at[0])
+    load.start()
+    copies = []
     for blk in range(2):
         for c in range(LT):
-            piece = frames_ref[blk * BLOCK : (blk + 1) * BLOCK, c * 128 : (c + 1) * 128]
-            out_ref[:, blk * LT + c] = piece.reshape(SHARDS, SUB, 128)
+            src = frames_hbm.at[blk, :, :, c * 128 : (c + 1) * 128]
+            k = blk * LT + c
+            copies.append(pltpu.make_async_copy(src, out_hbm.at[:, k], sem.at[1 + k]))
+            copies[-1].start()
     local = (gpos_ref[...] - rank_ref[0] * ROWS).astype(jnp.float32)
     local = jnp.broadcast_to(local, (8, BLOCK)).T[:, :1]
     cols = lax.broadcasted_iota(jnp.int32, (BLOCK, ROWS), 1).astype(jnp.float32)
     onehot = jnp.where(cols == local, 1.0, 0.0).astype(jnp.bfloat16)
-    picked = jnp.dot(onehot, frames, preferred_element_type=jnp.float32)
-    for c in range(LT):
-        piece = picked[:, c * 128 : (c + 1) * 128].reshape(SHARDS, SUB, 128)
-        out_ref[:, 2 * LT + c] = piece.astype(jnp.bfloat16)
     lane = lax.broadcasted_iota(jnp.int32, (SUB, 128), 1)
     codes = jnp.zeros((SUB, 128), jnp.int32)
     for q in range(2):
@@ -47,17 +47,34 @@
     codes = codes + lax.broadcasted_iota(jnp.int32, (SUB, 128), 0)
     codes = codes.astype(jnp.float32).astype(jnp.bfloat16)
     for s in range(SHARDS):
-        out_ref[s, 3 * LT] = codes
+        more_ref[s, LT] = codes
+    load.wait()
+    frames = frames_ref[...].astype(jnp.float32).reshape(ROWS, D).astype(jnp.bfloat16)
+    picked = jnp.dot(onehot, frames, preferred_element_type=jnp.float32)
+    for c in range(LT):
+        piece = picked[:, c * 128 : (c + 1) * 128].reshape(SHARDS, SUB, 128)
+        more_ref[:, c] = piece.astype(jnp.bfloat16)
+    last = pltpu.make_async_copy(more_ref, out_hbm.at[:, 2 * LT : 3 * LT + 1], sem.at[1 + 2 * LT])
+    last.start()
+    for copy in copies:
+        copy.wait()
+    last.wait()
 
 
 def pack(rank, owner, slot, frames, gpos):
     return pl.pallas_call(
         _pack_kernel,
-        out_shape=VM((SHARDS, 3 * LT + 1, SUB, 128), jnp.bfloat16),
-        in_specs=[pl.BlockSpec(memory_space=SM)] * 3 + [pl.BlockSpec(memory_space=VM)] * 2,
-        out_specs=pl.BlockSpec(memory_space=VM),
+        out_shape=jax.ShapeDtypeStruct((SHARDS, 3 * LT + 1, SUB, 128), jnp.bfloat16),
+        in_specs=[pl.BlockSpec(memory_space=SM)] * 3
+        + [pl.BlockSpec(memory_space=VM), pl.BlockSpec(memory_space=pl.ANY)],
+        out_specs=pl.BlockSpec(memory_space=pl.ANY),
+        scratch_shapes=[
+            VM((2, SHARDS, SUB, D), jnp.bfloat16),
+            VM((SHARDS, LT + 1, SUB, 128), jnp.bfloat16),
+            pltpu.SemaphoreType.DMA((2 * LT + 2,)),
+        ],
         name="pack",
-    )(rank, owner, slot, frames, gpos)
+    )(rank, owner, slot, gpos, frames.reshape(2, SHARDS, SUB, D))
 
 
 def _select_kernel(held_ref, out_ref, buf, sem):

time: 94.2 us -> 115 us (1.22)
  Pallas kernels: 38.4 us -> 58.7 us
    pallas_call x1, Pallas kernels: 1.49 us -> 21.9 us  [pack(): pl.pallas_call(_pack_kernel, out_shape=jax.ShapeDtypeStruct((SHARDS, 3 *...]
  transfers between devices with their start and end apart: 3 -> 3, of which waited for: 2 -> 2; matrix products, arithmetic and copies ran while one was open for 1% -> 1% of each run, Pallas kernels for 20% -> 17%
where the time goes in v7:
time: 115 us; the launch traced here: 114 us
  Pallas kernels  58.7 us (51%)
  blocking collectives  22.9 us (20%)
  waiting for transfers between devices  18.9 us (16%)
  starting transfers between devices  11 us (10%)
  local copies, waits for them, and re-layouts  1.37 us (1%)
    all_to_all x1, blocking collectives, exchange(): return lax.all_to_all(value, 'tm', split_axis=0, concat_axis=0, tiled=True)  22.9 us
    pallas_call x1, Pallas kernels, pack(): pl.pallas_call(_pack_kernel, out_shape=jax.ShapeDtypeStruct((SHARDS, 3 *...  21.9 us
    ppermute x1, waiting for transfers between devices, program(): lo = lax.ppermute(frames[BLOCK:], 'tm', up)  18.2 us
    pallas_call x1, Pallas kernels, late(): pl.pallas_call(_late_kernel, out_shape=jax.ShapeDtypeStruct((64, D), jnp....  16.4 us
    pallas_call x1, Pallas kernels, halo_part(): pl.pallas_call(_halo_kernel, grid=(STEPS,), out_shape=(f32, f32, f32), in...  10.6 us
    pallas_call x1, Pallas kernels, own_part(): pl.pallas_call(_own_kernel, grid=(STEPS,), out_shape=(half, half, half, j...  8.25 us
    all_to_all x1, starting transfers between devices, exchange(): return lax.all_to_all(value, 'tm', split_axis=0, concat_axis=0, tiled=True)  5.12 us
    ppermute x1, starting transfers between devices, program(): lo = lax.ppermute(frames[BLOCK:], 'tm', up)  3.37 us
  transfers between devices with their start and end apart: 3, of which 2 were waited for; matrix products, arithmetic and copies ran while one was open for 1% of the time, Pallas kernels for 17%

profile of v7, /device:TPU:2, one launch (start us, length us, event | category | flops | bytes accessed | tf_op | source)
XLA Modules:
  0.0 113.5 jit_solution(14511940144466043616)
XLA Ops:
  0.0 21.9 %pack.1 = bf16[16,31,8,128]{3,2,1,0:T(8,128)(2,1)} custom-call(s32[1]{0:T(128)} %bitcast.rank_ref, s32[2,3]{1,0:T(2,128)} %owner_ref.3, s32[2,3]{1,0:T(2,128)} %slot_ref.3, s32[1,128]{1,0:T(1,128)} %bitcast.6, bf16[2,16,8,1280]{3,2,1,0:T(8,128)(2,1)} %bitcast.5), custom_call_target="tpu_custom_call" | custom-call | tf_op jit(solution)/shard_map/pack/pallas_call | solution.py:65
  21.9 22.9 %all_to_all.10.held_ref = bf16[16,31,8,128]{3,2,1,0:T(8,128)(2,1)S(1)} all-to-all(bf16[16,31,8,128]{3,2,1,0:T(8,128)(2,1)} %pack.1), channel_id=1, replica_groups=mesh['rec'=16,'tm'=16] {'tm'}, dimensions={0} | all-to-all | bytes 2031616 | tf_op jit(solution)/shard_map/all_to_all | solution.py:422
  44.8 1.7 %select.1 = bf16[16,7,8,1280]{3,2,1,0:T(8,128)(2,1)} custom-call(bf16[16,31,8,128]{3,2,1,0:T(8,128)(2,1)S(1)} %all_to_all.10.held_ref), custom_call_target="tpu_custom_call" | custom-call | tf_op jit(solution)/shard_map/select/pallas_call | solution.py:116
  46.5 0.0 copy-start
  46.5 0.0 copy-start.1
  46.5 5.1 %all-to-all-start.1 = ((bf16[16,7,8,1280]{3,2,1,0:T(8,128)(2,1)}), bf16[16,7,8,1280]{3,2,1,0:T(8,128)(2,1)S(1)}, u32[]{:S(2)}, u32[]{:S(2)}) async-start(bf16[16,7,8,1280]{3,2,1,0:T(8,128)(2,1)} %select.1), calls=%async_computation.1 | async-start | bytes 4587520 | tf_op jit(solution)/shard_map/all_to_all | solution.py:422
  51.6 0.0 copy-done
  51.6 0.8 fusion
  52.4 3.4 %collective-permute-start = (bf16[128,1280]{1,0:T(8,128)(2,1)}, bf16[128,1280]{1,0:T(8,128)(2,1)S(1)}, u32[]{:S(2)}, u32[]{:S(2)}) collective-permute-start(bf16[128,1280]{1,0:T(8,128)(2,1)} %get-tuple-element.20), channel_id=1, source_target_pairs={{0,1},{1,2},{2,3},{3,4},{4,5},{5,6},{6,7},{7,8},{8,9},{9,10},{10,1... | collective-permute-start | bytes 983048 | tf_op jit(solution)/shard_map/ppermute | solution.py:435
  55.8 2.5 %collective-permute-start.1 = (bf16[128,1280]{1,0:T(8,128)(2,1)S(1)}, bf16[128,1280]{1,0:T(8,128)(2,1)S(1)}, u32[]{:S(2)}, u32[]{:S(2)}) collective-permute-start(bf16[128,1280]{1,0:T(8,128)(2,1)S(1)} %get-tuple-element.19), channel_id=1, source_target_pairs={{1,0},{2,1},{3,2},{4,3},{5,4},{6,5},{7,6},{8,7},{9,8},{10,9},{11,1... | collective-permute-start | bytes 983048 | tf_op jit(solution)/shard_map/ppermute | solution.py:436
  58.9 0.0 copy-done.1
  58.9 0.6 reshape.19.gain_ref
  59.5 8.3 %own.1 = (bf16[256,1280]{1,0:T(8,128)(2,1)}, bf16[256,1280]{1,0:T(8,128)(2,1)}, bf16[256,1280]{1,0:T(8,128)(2,1)}, f32[8,512]{1,0:T(8,128)}) custom-call(s32[1]{0:T(128)} %bitcast.rank_ref, s32[1]{0:T(128)S(6)} %copy.10.len_ref, s32[2,3]{1,0:T(2,128)} %owner_ref.3, s32[2,3]{1,0:T(2,128)} %slot_ref.3, s32[1,128]{1,0:T(1,128)} %bitcast.7, ...), custom_call_target="tpu_custom_call" | custom-call | tf_op jit(solution)/shard_map/own/pallas_call | solution.py:238
  67.8 18.2 %collective-permute-done.lo_ref = bf16[128,1280]{1,0:T(8,128)(2,1)S(1)} collective-permute-done((bf16[128,1280]{1,0:T(8,128)(2,1)}, bf16[128,1280]{1,0:T(8,128)(2,1)S(1)}, u32[]{:S(2)}, u32[]{:S(2)}) %collective-permute-start) | collective-permute-done | bytes 327712 | tf_op jit(solution)/shard_map/ppermute | solution.py:435
  85.9 0.7 collective-permute-done.1.hi_ref
  86.6 10.6 %halo.1 = (f32[256,1280]{1,0:T(8,128)}, f32[256,1280]{1,0:T(8,128)}, f32[256,1280]{1,0:T(8,128)}) custom-call(bf16[128,1280]{1,0:T(8,128)(2,1)S(1)} %collective-permute-done.lo_ref, bf16[128,1280]{1,0:T(8,128)(2,1)S(1)} %collective-permute-done.1.hi_ref, f32[8,512]{1,0:T(8,128)} %get-tuple-element.12.bias_ref, ...), custom_call_target="tpu_custom_call" | custom-call | tf_op jit(solution)/shard_map/halo/pallas_call | solution.py:253
  97.2 0.0 all-to-all-done.1
  97.2 16.4 %late.1 = bf16[64,1280]{1,0:T(8,128)(2,1)} custom-call(s32[1]{0:T(128)} %bitcast.rank_ref, s32[1]{0:T(128)S(6)} %copy.10.len_ref, bf16[896,1280]{1,0:T(8,128)(2,1)S(1)} %bitcast.4, f32[8,512]{1,0:T(8,128)} %get-tuple-element.12.bias_ref, bf16[256,1280]{1,0:T(8,128)(2,1)} %get-tuple-element.13.q_ref.q_hbm, f32[256,1280]{1,0:T(8,128)} %get-tuple-element.16.o_hbm, ...), custom_call_target="tpu_custom_call" | custom-call | tf_op jit(solution)/shard_map/late/pallas_call | solution.py:394
Async XLA Ops:
  46.5 5.1 %copy-start = (bf16[256,1280]{1,0:T(8,128)(2,1)S(1)}, bf16[256,1280]{1,0:T(8,128)(2,1)}, u32[]{:S(2)}) copy-start(bf16[256,1280]{1,0:T(8,128)(2,1)} %own_ref.1) | copy-start | bytes 1966084
  46.5 12.4 %copy-start.1 = (f32[1280]{0:T(1024)S(1)}, f32[1280]{0:T(1024)}, u32[]{:S(2)}) copy-start(f32[1280]{0:T(1024)} %param.13) | copy-start | bytes 15364
  46.5 50.7 %all-to-all-start.1 = ((bf16[16,7,8,1280]{3,2,1,0:T(8,128)(2,1)}), bf16[16,7,8,1280]{3,2,1,0:T(8,128)(2,1)S(1)}, u32[]{:S(2)}, u32[]{:S(2)}) async-start(bf16[16,7,8,1280]{3,2,1,0:T(8,128)(2,1)} %select.1), calls=%async_computation.1 | async-start | bytes 4587520 | tf_op jit(solution)/shard_map/all_to_all | solution.py:422
  52.4 33.5 %collective-permute-start = (bf16[128,1280]{1,0:T(8,128)(2,1)}, bf16[128,1280]{1,0:T(8,128)(2,1)S(1)}, u32[]{:S(2)}, u32[]{:S(2)}) collective-permute-start(bf16[128,1280]{1,0:T(8,128)(2,1)} %get-tuple-element.20), channel_id=1, source_target_pairs={{0,1},{1,2},{2,3},{3,4},{4,5},{5,6},{6,7},{7,8},{8,9},{9,10},{10,1... | collective-permute-start | bytes 983048 | tf_op jit(solution)/shard_map/ppermute | solution.py:435
  55.8 30.8 %collective-permute-start.1 = (bf16[128,1280]{1,0:T(8,128)(2,1)S(1)}, bf16[128,1280]{1,0:T(8,128)(2,1)S(1)}, u32[]{:S(2)}, u32[]{:S(2)}) collective-permute-start(bf16[128,1280]{1,0:T(8,128)(2,1)S(1)} %get-tuple-element.19), channel_id=1, source_target_pairs={{1,0},{2,1},{3,2},{4,3},{5,4},{6,5},{7,6},{8,7},{9,8},{10,9},{11,1... | collective-permute-start | bytes 983048 | tf_op jit(solution)/shard_map/ppermute | solution.py:436

commit v8 on v5

--- a/solution.py
+++ b/solution.py
@@ -16,7 +16,7 @@
 SHARDS = 16
 SUB = BLOCK // SHARDS
 ROWS = 256
-SUBS = 2 * PICKS + 1
+SUBS = 2 * PICKS
 LT = D // 128
 NEG = -1e30
 
@@ -24,7 +24,7 @@
 SM = pltpu.SMEM
 
 
-def _pack_kernel(rank_ref, owner_ref, slot_ref, frames_ref, gpos_ref, out_ref):
+def _pack_kernel(rank_ref, owner_ref, slot_ref, frames_ref, gpos_ref, out_ref, picked_ref):
     frames = frames_ref[...]
     for blk in range(2):
         for c in range(LT):
@@ -35,9 +35,7 @@
     cols = lax.broadcasted_iota(jnp.int32, (BLOCK, ROWS), 1).astype(jnp.float32)
     onehot = jnp.where(cols == local, 1.0, 0.0).astype(jnp.bfloat16)
     picked = jnp.dot(onehot, frames, preferred_element_type=jnp.float32)
-    for c in range(LT):
-        piece = picked[:, c * 128 : (c + 1) * 128].reshape(SHARDS, SUB, 128)
-        out_ref[:, 2 * LT + c] = piece.astype(jnp.bfloat16)
+    picked_ref[...] = picked.astype(jnp.bfloat16)
     lane = lax.broadcasted_iota(jnp.int32, (SUB, 128), 1)
     codes = jnp.zeros((SUB, 128), jnp.int32)
     for q in range(2):
@@ -47,15 +45,18 @@
     codes = codes + lax.broadcasted_iota(jnp.int32, (SUB, 128), 0)
     codes = codes.astype(jnp.float32).astype(jnp.bfloat16)
     for s in range(SHARDS):
-        out_ref[s, 3 * LT] = codes
+        out_ref[s, 2 * LT] = codes
 
 
 def pack(rank, owner, slot, frames, gpos):
     return pl.pallas_call(
         _pack_kernel,
-        out_shape=VM((SHARDS, 3 * LT + 1, SUB, 128), jnp.bfloat16),
+        out_shape=(
+            jax.ShapeDtypeStruct((SHARDS, 2 * LT + 1, SUB, 128), jnp.bfloat16),
+            jax.ShapeDtypeStruct((BLOCK, D), jnp.bfloat16),
+        ),
         in_specs=[pl.BlockSpec(memory_space=SM)] * 3 + [pl.BlockSpec(memory_space=VM)] * 2,
-        out_specs=pl.BlockSpec(memory_space=VM),
+        out_specs=(pl.BlockSpec(memory_space=VM),) * 2,
         name="pack",
     )(rank, owner, slot, frames, gpos)
 
@@ -68,7 +69,7 @@
         copy.start()
         copies.append(copy)
 
-    codes = held_ref[:, 3 * LT].astype(jnp.float32).reshape(BLOCK, 128)
+    codes = held_ref[:, 2 * LT].astype(jnp.float32).reshape(BLOCK, 128)
     blocks = []
     for slot in range(2):
         tiles = [
@@ -78,14 +79,6 @@
         blocks.append(jnp.concatenate(tiles, axis=1))
     rows = jnp.concatenate(blocks, axis=0)
     cols = lax.broadcasted_iota(jnp.int32, (BLOCK, ROWS), 1).astype(jnp.float32)
-    for c in range(LT):
-        total = held_ref[0, 2 * LT + c].astype(jnp.float32)
-        for i in range(1, SHARDS):
-            total = total + held_ref[i, 2 * LT + c].astype(jnp.float32)
-        total = total.astype(jnp.bfloat16)
-        for r in range(SHARDS):
-            buf[2 * PICKS, r, :, c * 128 : (c + 1) * 128] = total
-    send(2 * PICKS, out_ref.at[:, 2 * PICKS])
     for k in range(2 * PICKS):
         onehot = jnp.where(cols == codes[:, k : k + 1], 1.0, 0.0).astype(jnp.bfloat16)
         got = jnp.dot(onehot, rows, preferred_element_type=jnp.float32)
@@ -103,7 +96,7 @@
         out_specs=pl.BlockSpec(memory_space=pl.ANY),
         scratch_shapes=[
             pltpu.VMEM((2 * PICKS + 1, SHARDS, SUB, D), jnp.bfloat16),
-            pltpu.SemaphoreType.DMA((2 * PICKS + 1,)),
+            pltpu.SemaphoreType.DMA((SUBS,)),
         ],
         name="select",
     )(pltpu.with_memory_space_constraint(held, VM))
@@ -178,31 +171,32 @@
         def picked(q, j):
             return owner_ref[q, j] * 2 + slot_ref[q, j]
 
-        for q in range(2):
-            near = [(lane // BLOCK == i, rank_ref[0] * 2 + q - 1 + i) for i in range(3)]
-            bias_ref[q : q + 1, :] = row(near)
         glob = jnp.where(gpos_ref[...] < live * BLOCK, 0.0, NEG)
         rows = lane // SUB
         for q in range(2):
-            far = row([((rows % PICKS == j), picked(q, j)) for j in range(PICKS)])
-            parts = [far[:, : PICKS * BLOCK], glob]
-            bias_ref[2 + q : 3 + q, :] = jnp.concatenate(parts if q == 0 else parts[::-1], axis=1)
+            near = row([(lane // BLOCK == i, rank_ref[0] * 2 + q - 1 + i) for i in range(3)])
+            bias_ref[q : q + 1, :] = jnp.concatenate([near[:, : 3 * BLOCK], glob], axis=1)
+            far = row([(rows % PICKS == j, picked(q, j)) for j in range(PICKS)])
+            bias_ref[2 + q : 3 + q, :] = far
         bias_ref[4:8, :] = jnp.zeros((4, 4 * BLOCK), jnp.float32)
 
 
-def _halo_kernel(lo_ref, hi_ref, bias_ref, q_ref, k_ref, v_ref, wk_ref, wv_ref, o_ref, l_ref, m_ref):
-    rim = jnp.concatenate([lo_ref[...], hi_ref[...]], axis=0)
+def _halo_kernel(
+    lo_ref, hi_ref, glob_ref, bias_ref, q_ref, k_ref, v_ref, wk_ref, wv_ref, o_ref, l_ref, m_ref
+):
+    rim = jnp.concatenate([lo_ref[...], hi_ref[...], glob_ref[...]], axis=0)
 
     def widen(own_ref, w_ref):
         far = _dot(rim, w_ref[...]).astype(jnp.bfloat16)
-        return jnp.concatenate([far[:BLOCK], own_ref[...], far[BLOCK:]], axis=0)
+        lo, hi, glob = (far[i * BLOCK : (i + 1) * BLOCK] for i in range(3))
+        own = own_ref[...]
+        return [jnp.concatenate([lo, own, glob], axis=0), jnp.concatenate([own, hi, glob], axis=0)]
 
     keys = widen(k_ref, wk_ref)
     values = widen(v_ref, wv_ref)
     for b in range(2):
-        at = slice(b * BLOCK, b * BLOCK + 3 * BLOCK)
         res = _attend(
-            q_ref[b * BLOCK : (b + 1) * BLOCK], keys[at], values[at], bias_ref[b : b + 1, : 3 * BLOCK]
+            q_ref[b * BLOCK : (b + 1) * BLOCK], keys[b], values[b], bias_ref[b : b + 1, :]
         )
         for ref, val in zip((o_ref, l_ref, m_ref), res):
             ref[b * BLOCK : (b + 1) * BLOCK, :] = val
@@ -229,7 +223,7 @@
     )(rank, length, owner, slot, gpos, own, w_query, w_kv, w_kv)
 
 
-def halo_part(lo, hi, bias, q, k, v, w_kv):
+def halo_part(lo, hi, glob, bias, q, k, v, w_kv):
     f32 = jax.ShapeDtypeStruct((ROWS, D), jnp.float32)
     lo = pltpu.with_memory_space_constraint(lo, VM)
     hi = pltpu.with_memory_space_constraint(hi, VM)
@@ -240,6 +234,7 @@
         in_specs=[
             pl.BlockSpec(memory_space=VM),
             pl.BlockSpec(memory_space=VM),
+            _whole((BLOCK, D)),
             _whole((8, 4 * BLOCK)),
             *[_cols(ROWS)] * 3,
             _cols(D),
@@ -247,7 +242,7 @@
         ],
         out_specs=(_cols(ROWS),) * 3,
         name="halo",
-    )(lo, hi, bias, q, k, v, w_kv, w_kv)
+    )(lo, hi, glob, bias, q, k, v, w_kv, w_kv)
 
 
 def _finish(projected, acc, gain_ref, live):
@@ -344,8 +339,7 @@
         for full, ref in zip(both, (keys_ref, values_ref)):
             full = full.reshape(SHARDS, SUBS, SUB, TILE)
             ref[p % 2, :near] = full[:, :PICKS].reshape(near, TILE).astype(jnp.bfloat16)
-            ref[p % 2, near : near + BLOCK] = full[:, 2 * PICKS].reshape(BLOCK, TILE).astype(jnp.bfloat16)
-            ref[p % 2, near + BLOCK :] = full[:, PICKS : 2 * PICKS].reshape(near, TILE).astype(jnp.bfloat16)
+            ref[p % 2, near:] = full[:, PICKS:].reshape(near, TILE).astype(jnp.bfloat16)
 
     project(0)
     fetch.wait("q")
@@ -357,10 +351,10 @@
             fetch.wait("o", "l", "m")
         for b in range(2):
             rows = slice(b * BLOCK, (b + 1) * BLOCK)
-            used = pl.ds(b * near, near + BLOCK)
+            used = pl.ds(b * near, near)
             far = _stage(
                 q_ref[rows, at], keys_ref.at[p % 2, used], values_ref.at[p % 2, used],
-                scores_ref.at[b], weight_ref.at[b], bias_ref[2 + b : 3 + b, :],
+                scores_ref.at[b], weight_ref.at[b], bias_ref[2 + b : 3 + b, :near],
             )
             out, total, _ = _join((o_ref[rows, at], l_ref[rows, at], m_ref[rows, at]), far)
             context_ref[rows, at] = (out / total).astype(jnp.bfloat16)
@@ -393,8 +387,8 @@
             pltpu.SemaphoreType.DMA((2 * STEPS + 5,)),
             VM((2, SUBS * BLOCK, TILE), jnp.bfloat16),
             VM((2, SUBS * BLOCK, TILE), jnp.bfloat16),
-            VM((2, 4 * BLOCK, 4 * BLOCK), jnp.float32),
-            VM((2, 4 * BLOCK, 4 * BLOCK), jnp.bfloat16),
+            VM((2, 4 * BLOCK, PICKS * BLOCK), jnp.float32),
+            VM((2, 4 * BLOCK, PICKS * BLOCK), jnp.bfloat16),
             VM((ROWS, D), jnp.bfloat16),
         ],
         name="late",
@@ -412,14 +406,17 @@
     gain = norm_gain.reshape(1, D)
     up = [(i, i + 1) for i in range(shards - 1)]
     down = [(j, i) for i, j in up]
-    packed = pack(rank, rand_owner, rand_slot, frames, gpos)
+    packed, glob = pack(rank, rand_owner, rand_slot, frames, gpos)
     held = exchange(packed)
     q, k, v, bias = own_part(rank, length, rand_owner, rand_slot, gpos, frames, w_query, w_kv)
     lo = lax.ppermute(frames[BLOCK:], "tm", up)
     hi = lax.ppermute(frames[:BLOCK], "tm", down)
+    for k_step in range(4):
+        other = lax.ppermute(glob, "tm", [(i, i ^ (1 << k_step)) for i in range(shards)])
+        glob = glob + other
     reply = select(held)
     got = exchange(reply).reshape(SUBS * BLOCK, D)
-    o, l, m = halo_part(lo, hi, bias, q, k, v, w_kv)
+    o, l, m = halo_part(lo, hi, glob, bias, q, k, v, w_kv)
     return late(rank, length, got, bias, q, o, l, m, w_kv, w_out, gain)
 
 

time: 94.2 us -> 124 us (1.32)
  the two profiles are of different devices: /device:TPU:2 before, /device:TPU:72 now
where the time goes in v8:
time: 124 us
  waiting for transfers between devices  40.6 us (33%)
  Pallas kernels  39.4 us (32%)
  starting transfers between devices  21.6 us (17%)
  blocking collectives  18.8 us (15%)
  local copies, waits for them, and re-layouts  1.5 us (1%)
    ppermute x4, waiting for transfers between devices, program(): lax.ppermute(glob, 'tm', [(i, i ^ 1 << k_step) for i in range(shards)])  40.6 us
    all_to_all x1, blocking collectives, exchange(): return lax.all_to_all(value, 'tm', split_axis=0, concat_axis=0, tiled=True)  18.8 us
    pallas_call x1, Pallas kernels, late(): pl.pallas_call(_late_kernel, out_shape=jax.ShapeDtypeStruct((64, D), jnp....  15.4 us
    pallas_call x1, Pallas kernels, halo_part(): pl.pallas_call(_halo_kernel, grid=(STEPS,), out_shape=(f32, f32, f32), in...  11.7 us
    pallas_call x1, Pallas kernels, own_part(): pl.pallas_call(_own_kernel, grid=(STEPS,), out_shape=(half, half, half, j...  8.25 us
    ppermute x4, starting transfers between devices, program(): lax.ppermute(glob, 'tm', [(i, i ^ 1 << k_step) for i in range(shards)])  7.93 us
    ppermute x1, starting transfers between devices, program(): hi = lax.ppermute(frames[:BLOCK], 'tm', down)  6.21 us
    all_to_all x1, starting transfers between devices, exchange(): return lax.all_to_all(value, 'tm', split_axis=0, concat_axis=0, tiled=True)  5.6 us
  transfers between devices with their start and end apart: 7, of which 3 were waited for; matrix products, arithmetic and copies ran while one was open for 2% of the time, Pallas kernels for 16%

profile of v8, /device:TPU:72, one launch (start us, length us, event | category | flops | bytes accessed | tf_op | source)
XLA Modules:
  0.0 124.0 jit_solution(14188018181063667203)
XLA Ops:
  0.0 2.4 %pack.1 = (bf16[16,21,8,128]{3,2,1,0:T(8,128)(2,1)}, bf16[128,1280]{1,0:T(8,128)(2,1)}) custom-call(s32[1]{0:T(128)} %bitcast.rank_ref, s32[2,3]{1,0:T(2,128)} %owner_ref.3, s32[2,3]{1,0:T(2,128)} %slot_ref.3, bf16[256,1280]{1,0:T(8,128)(2,1)} %own_ref.1, s32[1,128]{1,0:T(1,128)} %bitcast.4), custom_call_target="tpu_custom_call" | custom-call | tf_op jit(solution)/shard_map/pack/pallas_call | solution.py:52
  2.4 18.8 %all_to_all.10.held_ref = bf16[16,21,8,128]{3,2,1,0:T(8,128)(2,1)S(1)} all-to-all(bf16[16,21,8,128]{3,2,1,0:T(8,128)(2,1)} %get-tuple-element.14), channel_id=1, replica_groups=mesh['rec'=16,'tm'=16] {'tm'}, dimensions={0} | all-to-all | bytes 1376256 | tf_op jit(solution)/shard_map/all_to_all | solution.py:399
  21.2 1.7 %select.1 = bf16[16,6,8,1280]{3,2,1,0:T(8,128)(2,1)} custom-call(bf16[16,21,8,128]{3,2,1,0:T(8,128)(2,1)S(1)} %all_to_all.10.held_ref), custom_call_target="tpu_custom_call" | custom-call | tf_op jit(solution)/shard_map/select/pallas_call | solution.py:92
  22.9 0.0 copy-start.1
  22.9 5.6 %all-to-all-start.1 = ((bf16[16,6,8,1280]{3,2,1,0:T(8,128)(2,1)}), bf16[16,6,8,1280]{3,2,1,0:T(8,128)(2,1)S(1)}, u32[]{:S(2)}, u32[]{:S(2)}) async-start(bf16[16,6,8,1280]{3,2,1,0:T(8,128)(2,1)} %select.1), calls=%async_computation.1 | async-start | bytes 3932160 | tf_op jit(solution)/shard_map/all_to_all | solution.py:399
  28.5 0.0 copy-start
  28.5 0.0 copy-done.1
  28.5 0.0 copy-start.2
  28.5 1.6 %collective-permute-start.2 = (bf16[128,1280]{1,0:T(8,128)(2,1)S(1)}, bf16[128,1280]{1,0:T(8,128)(2,1)S(1)}, u32[]{:S(2)}, u32[]{:S(2)}) collective-permute-start(bf16[128,1280]{1,0:T(8,128)(2,1)S(1)} %copy-done.1), channel_id=1, source_target_pairs={{0,1},{1,0},{2,3},{3,2},{4,5},{5,4},{6,7},{7,6},{8,9},{9,8},{10,11... | collective-permute-start | bytes 983048 | tf_op jit(solution)/shard_map/ppermute | solution.py:415
  30.1 28.3 %collective-permute-done.2 = bf16[128,1280]{1,0:T(8,128)(2,1)S(1)} collective-permute-done((bf16[128,1280]{1,0:T(8,128)(2,1)S(1)}, bf16[128,1280]{1,0:T(8,128)(2,1)S(1)}, u32[]{:S(2)}, u32[]{:S(2)}) %collective-permute-start.2) | collective-permute-done | bytes 327712 | tf_op jit(solution)/shard_map/ppermute | solution.py:415
  58.4 0.1 add.12
  58.4 1.8 %collective-permute-start.3 = (bf16[128,1280]{1,0:T(8,128)(2,1)S(1)}, bf16[128,1280]{1,0:T(8,128)(2,1)S(1)}, u32[]{:S(2)}, u32[]{:S(2)}) collective-permute-start(bf16[128,1280]{1,0:T(8,128)(2,1)S(1)} %add.12), channel_id=1, source_target_pairs={{0,2},{1,3},{2,0},{3,1},{4,6},{5,7},{6,4},{7,5},{8,10},{9,11},{10,... | collective-permute-start | bytes 983048 | tf_op jit(solution)/shard_map/ppermute | solution.py:415
  60.2 7.1 %collective-permute-done.3 = bf16[128,1280]{1,0:T(8,128)(2,1)S(1)} collective-permute-done((bf16[128,1280]{1,0:T(8,128)(2,1)S(1)}, bf16[128,1280]{1,0:T(8,128)(2,1)S(1)}, u32[]{:S(2)}, u32[]{:S(2)}) %collective-permute-start.3) | collective-permute-done | bytes 327712 | tf_op jit(solution)/shard_map/ppermute | solution.py:415
  67.3 0.1 add.13
  67.4 1.1 collective-permute-start.4
  68.4 0.0 copy-done
  68.5 0.9 fusion
  69.3 5.2 %collective-permute-done.4 = bf16[128,1280]{1,0:T(8,128)(2,1)S(1)} collective-permute-done((bf16[128,1280]{1,0:T(8,128)(2,1)S(1)}, bf16[128,1280]{1,0:T(8,128)(2,1)S(1)}, u32[]{:S(2)}, u32[]{:S(2)}) %collective-permute-start.4) | collective-permute-done | bytes 327712 | tf_op jit(solution)/shard_map/ppermute | solution.py:415
  74.5 0.1 add.14
  74.6 3.6 %collective-permute-start.5 = (bf16[128,1280]{1,0:T(8,128)(2,1)S(1)}, bf16[128,1280]{1,0:T(8,128)(2,1)S(1)}, u32[]{:S(2)}, u32[]{:S(2)}) collective-permute-start(bf16[128,1280]{1,0:T(8,128)(2,1)S(1)} %add.14), channel_id=1, source_target_pairs={{0,8},{1,9},{2,10},{3,11},{4,12},{5,13},{6,14},{7,15},{8,0},{9,1},... | collective-permute-start | bytes 983048 | tf_op jit(solution)/shard_map/ppermute | solution.py:415
  78.2 1.9 %collective-permute-start = (bf16[128,1280]{1,0:T(8,128)(2,1)}, bf16[128,1280]{1,0:T(8,128)(2,1)S(1)}, u32[]{:S(2)}, u32[]{:S(2)}) collective-permute-start(bf16[128,1280]{1,0:T(8,128)(2,1)} %get-tuple-element.24), channel_id=1, source_target_pairs={{0,1},{1,2},{2,3},{3,4},{4,5},{5,6},{6,7},{7,8},{8,9},{9,10},{10,1... | collective-permute-start | bytes 983048 | tf_op jit(solution)/shard_map/ppermute | solution.py:412
  80.1 6.2 %collective-permute-start.1 = (bf16[128,1280]{1,0:T(8,128)(2,1)}, bf16[128,1280]{1,0:T(8,128)(2,1)S(1)}, u32[]{:S(2)}, u32[]{:S(2)}) collective-permute-start(bf16[128,1280]{1,0:T(8,128)(2,1)} %get-tuple-element.23), channel_id=1, source_target_pairs={{1,0},{2,1},{3,2},{4,3},{5,4},{6,5},{7,6},{8,7},{9,8},{10,9},{11,1... | collective-permute-start | bytes 983048 | tf_op jit(solution)/shard_map/ppermute | solution.py:413
  87.0 0.0 copy-done.2
  87.0 0.6 reshape.15.gain_ref
  87.6 8.2 %own.1 = (bf16[256,1280]{1,0:T(8,128)(2,1)}, bf16[256,1280]{1,0:T(8,128)(2,1)}, bf16[256,1280]{1,0:T(8,128)(2,1)}, f32[8,512]{1,0:T(8,128)}) custom-call(s32[1]{0:T(128)} %bitcast.rank_ref, s32[1]{0:T(128)S(6)} %copy.10.len_ref, s32[2,3]{1,0:T(2,128)} %owner_ref.3, s32[2,3]{1,0:T(2,128)} %slot_ref.3, s32[1,128]{1,0:T(1,128)} %bitcast.5, ...), custom_call_target="tpu_custom_call" | custom-call | tf_op jit(solution)/shard_map/own/pallas_call | solution.py:215
  95.8 0.0 collective-permute-done.5
  95.8 0.8 add.15.glob_ref
  96.7 0.0 collective-permute-done.lo_ref
  96.7 0.0 collective-permute-done.1.hi_ref
  96.7 11.7 %halo.1 = (f32[256,1280]{1,0:T(8,128)}, f32[256,1280]{1,0:T(8,128)}, f32[256,1280]{1,0:T(8,128)}) custom-call(bf16[128,1280]{1,0:T(8,128)(2,1)S(1)} %collective-permute-done.lo_ref, bf16[128,1280]{1,0:T(8,128)(2,1)S(1)} %collective-permute-done.1.hi_ref, bf16[128,1280]{1,0:T(8,128)(2,1)} %add.15.glob_ref, f32[8,512]{1,0:T(8,128)} %get-tuple-element.15.bias_ref, ...), custom_call_target="tpu_custom_call" | custom-call | tf_op jit(solution)/shard_map/halo/pallas_call | solution.py:230
  108.4 0.0 all-to-all-done.1
  108.4 15.4 %late.1 = bf16[64,1280]{1,0:T(8,128)(2,1)} custom-call(s32[1]{0:T(128)} %bitcast.rank_ref, s32[1]{0:T(128)S(6)} %copy.10.len_ref, bf16[768,1280]{1,0:T(8,128)(2,1)S(1)} %bitcast.3, f32[8,512]{1,0:T(8,128)} %get-tuple-element.15.bias_ref, bf16[256,1280]{1,0:T(8,128)(2,1)} %get-tuple-element.16.q_ref.q_hbm, f32[256,1280]{1,0:T(8,128)} %get-tuple-element.20.o_hbm, ...), custom_call_target="tpu_custom_call" | custom-call | tf_op jit(solution)/shard_map/late/pallas_call | solution.py:371
Async XLA Ops:
  22.9 5.6 %copy-start.1 = (bf16[128,1280]{1,0:T(8,128)(2,1)S(1)}, bf16[128,1280]{1,0:T(8,128)(2,1)}, u32[]{:S(2)}) copy-start(bf16[128,1280]{1,0:T(8,128)(2,1)} %get-tuple-element.17) | copy-start | bytes 983044
  22.9 85.5 %all-to-all-start.1 = ((bf16[16,6,8,1280]{3,2,1,0:T(8,128)(2,1)}), bf16[16,6,8,1280]{3,2,1,0:T(8,128)(2,1)S(1)}, u32[]{:S(2)}, u32[]{:S(2)}) async-start(bf16[16,6,8,1280]{3,2,1,0:T(8,128)(2,1)} %select.1), calls=%async_computation.1 | async-start | bytes 3932160 | tf_op jit(solution)/shard_map/all_to_all | solution.py:399
  28.5 39.9 %copy-start = (bf16[256,1280]{1,0:T(8,128)(2,1)S(1)}, bf16[256,1280]{1,0:T(8,128)(2,1)}, u32[]{:S(2)}) copy-start(bf16[256,1280]{1,0:T(8,128)(2,1)} %own_ref.1) | copy-start | bytes 1966084
  28.5 58.4 %copy-start.2 = (f32[1280]{0:T(1024)S(1)}, f32[1280]{0:T(1024)}, u32[]{:S(2)}) copy-start(f32[1280]{0:T(1024)} %param.13) | copy-start | bytes 15364
  28.5 29.8 %collective-permute-start.2 = (bf16[128,1280]{1,0:T(8,128)(2,1)S(1)}, bf16[128,1280]{1,0:T(8,128)(2,1)S(1)}, u32[]{:S(2)}, u32[]{:S(2)}) collective-permute-start(bf16[128,1280]{1,0:T(8,128)(2,1)S(1)} %copy-done.1), channel_id=1, source_target_pairs={{0,1},{1,0},{2,3},{3,2},{4,5},{5,4},{6,7},{7,6},{8,9},{9,8},{10,11... | collective-permute-start | bytes 983048 | tf_op jit(solution)/shard_map/ppermute | solution.py:415
  58.4 8.9 %collective-permute-start.3 = (bf16[128,1280]{1,0:T(8,128)(2,1)S(1)}, bf16[128,1280]{1,0:T(8,128)(2,1)S(1)}, u32[]{:S(2)}, u32[]{:S(2)}) collective-permute-start(bf16[128,1280]{1,0:T(8,128)(2,1)S(1)} %add.12), channel_id=1, source_target_pairs={{0,2},{1,3},{2,0},{3,1},{4,6},{5,7},{6,4},{7,5},{8,10},{9,11},{10,... | collective-permute-start | bytes 983048 | tf_op jit(solution)/shard_map/ppermute | solution.py:415
  67.4 7.2 %collective-permute-start.4 = (bf16[128,1280]{1,0:T(8,128)(2,1)S(1)}, bf16[128,1280]{1,0:T(8,128)(2,1)S(1)}, u32[]{:S(2)}, u32[]{:S(2)}) collective-permute-start(bf16[128,1280]{1,0:T(8,128)(2,1)S(1)} %add.13), channel_id=1, source_target_pairs={{0,4},{1,5},{2,6},{3,7},{4,0},{5,1},{6,2},{7,3},{8,12},{9,13},{10,... | collective-permute-start | bytes 983048 | tf_op jit(solution)/shard_map/ppermute | solution.py:415
  74.6 21.2 %collective-permute-start.5 = (bf16[128,1280]{1,0:T(8,128)(2,1)S(1)}, bf16[128,1280]{1,0:T(8,128)(2,1)S(1)}, u32[]{:S(2)}, u32[]{:S(2)}) collective-permute-start(bf16[128,1280]{1,0:T(8,128)(2,1)S(1)} %add.14), channel_id=1, source_target_pairs={{0,8},{1,9},{2,10},{3,11},{4,12},{5,13},{6,14},{7,15},{8,0},{9,1},... | collective-permute-start | bytes 983048 | tf_op jit(solution)/shard_map/ppermute | solution.py:415
  78.2 18.5 %collective-permute-start = (bf16[128,1280]{1,0:T(8,128)(2,1)}, bf16[128,1280]{1,0:T(8,128)(2,1)S(1)}, u32[]{:S(2)}, u32[]{:S(2)}) collective-permute-start(bf16[128,1280]{1,0:T(8,128)(2,1)} %get-tuple-element.24), channel_id=1, source_target_pairs={{0,1},{1,2},{2,3},{3,4},{4,5},{5,6},{6,7},{7,8},{8,9},{9,10},{10,1... | collective-permute-start | bytes 983048 | tf_op jit(solution)/shard_map/ppermute | solution.py:412
  80.1 16.6 %collective-permute-start.1 = (bf16[128,1280]{1,0:T(8,128)(2,1)}, bf16[128,1280]{1,0:T(8,128)(2,1)S(1)}, u32[]{:S(2)}, u32[]{:S(2)}) collective-permute-start(bf16[128,1280]{1,0:T(8,128)(2,1)} %get-tuple-element.23), channel_id=1, source_target_pairs={{1,0},{2,1},{3,2},{4,3},{5,4},{6,5},{7,6},{8,7},{9,8},{10,9},{11,1... | collective-permute-start | bytes 983048 | tf_op jit(solution)/shard_map/ppermute | solution.py:413

commit v9 on v5

--- a/solution.py
+++ b/solution.py
@@ -24,20 +24,18 @@
 SM = pltpu.SMEM
 
 
-def _pack_kernel(rank_ref, owner_ref, slot_ref, frames_ref, gpos_ref, out_ref):
-    frames = frames_ref[...]
+def _pack_kernel(rank_ref, owner_ref, slot_ref, gpos_ref, frames_hbm, out_hbm, frames_ref, buf, sem):
+    loads, stores = [], []
     for blk in range(2):
-        for c in range(LT):
-            piece = frames_ref[blk * BLOCK : (blk + 1) * BLOCK, c * 128 : (c + 1) * 128]
-            out_ref[:, blk * LT + c] = piece.reshape(SHARDS, SUB, 128)
-    local = (gpos_ref[...] - rank_ref[0] * ROWS).astype(jnp.float32)
-    local = jnp.broadcast_to(local, (8, BLOCK)).T[:, :1]
-    cols = lax.broadcasted_iota(jnp.int32, (BLOCK, ROWS), 1).astype(jnp.float32)
-    onehot = jnp.where(cols == local, 1.0, 0.0).astype(jnp.bfloat16)
-    picked = jnp.dot(onehot, frames, preferred_element_type=jnp.float32)
-    for c in range(LT):
-        piece = picked[:, c * 128 : (c + 1) * 128].reshape(SHARDS, SUB, 128)
-        out_ref[:, 2 * LT + c] = piece.astype(jnp.bfloat16)
+        at = pl.ds(blk * BLOCK, BLOCK)
+        loads.append(pltpu.make_async_copy(frames_hbm.at[at], frames_ref.at[at], sem.at[blk]))
+        loads[-1].start()
+
+    def send(k, start, count):
+        at = pl.ds(start, count)
+        stores.append(pltpu.make_async_copy(buf.at[:, at], out_hbm.at[:, at], sem.at[k]))
+        stores[-1].start()
+
     lane = lax.broadcasted_iota(jnp.int32, (SUB, 128), 1)
     codes = jnp.zeros((SUB, 128), jnp.int32)
     for q in range(2):
@@ -47,17 +45,41 @@
     codes = codes + lax.broadcasted_iota(jnp.int32, (SUB, 128), 0)
     codes = codes.astype(jnp.float32).astype(jnp.bfloat16)
     for s in range(SHARDS):
-        out_ref[s, 3 * LT] = codes
+        buf[s, 3 * LT] = codes
+    local = (gpos_ref[...] - rank_ref[0] * ROWS).astype(jnp.float32)
+    local = jnp.broadcast_to(local, (8, BLOCK)).T[:, :1]
+    cols = lax.broadcasted_iota(jnp.int32, (BLOCK, ROWS), 1).astype(jnp.float32)
+    onehot = jnp.where(cols == local, 1.0, 0.0).astype(jnp.bfloat16)
+    for blk in range(2):
+        loads[blk].wait()
+        for c in range(LT):
+            piece = frames_ref[blk * BLOCK : (blk + 1) * BLOCK, c * 128 : (c + 1) * 128]
+            buf[:, blk * LT + c] = piece.reshape(SHARDS, SUB, 128)
+        send(2 + blk, blk * LT, LT)
+    picked = jnp.dot(onehot, frames_ref[...], preferred_element_type=jnp.float32)
+    for c in range(LT):
+        piece = picked[:, c * 128 : (c + 1) * 128].reshape(SHARDS, SUB, 128)
+        buf[:, 2 * LT + c] = piece.astype(jnp.bfloat16)
+    send(4, 2 * LT, LT + 1)
+    for copy in stores:
+        copy.wait()
 
 
 def pack(rank, owner, slot, frames, gpos):
+    shape = (SHARDS, 3 * LT + 1, SUB, 128)
     return pl.pallas_call(
         _pack_kernel,
-        out_shape=VM((SHARDS, 3 * LT + 1, SUB, 128), jnp.bfloat16),
-        in_specs=[pl.BlockSpec(memory_space=SM)] * 3 + [pl.BlockSpec(memory_space=VM)] * 2,
-        out_specs=pl.BlockSpec(memory_space=VM),
+        out_shape=jax.ShapeDtypeStruct(shape, jnp.bfloat16),
+        in_specs=[pl.BlockSpec(memory_space=SM)] * 3
+        + [pl.BlockSpec(memory_space=VM), pl.BlockSpec(memory_space=pl.ANY)],
+        out_specs=pl.BlockSpec(memory_space=pl.ANY),
+        scratch_shapes=[
+            VM((ROWS, D), jnp.bfloat16),
+            VM(shape, jnp.bfloat16),
+            pltpu.SemaphoreType.DMA((5,)),
+        ],
         name="pack",
-    )(rank, owner, slot, frames, gpos)
+    )(rank, owner, slot, gpos, frames)
 
 
 def _select_kernel(held_ref, out_ref, buf, sem):
@@ -271,23 +293,24 @@
     return slice(base + p * TILE, base + (p + 1) * TILE)
 
 
-def _stage(query, keys_ref, values_ref, scores_ref, weight_ref, bias):
-    width = keys_ref.shape[0]
-    scores_ref[:, :width] = _scores(query, keys_ref[...])
+def _soften(scores_ref, weight_ref, bias):
     tops = []
     for r in range(0, 4 * BLOCK, 64):
-        piece = scores_ref[r : r + 64, :width] + bias
+        piece = scores_ref[r : r + 64, :] + bias
         top = jnp.max(piece, axis=1, keepdims=True)
-        weight_ref[r : r + 64, :width] = jnp.exp(piece - top).astype(jnp.bfloat16)
+        weight_ref[r : r + 64, :] = jnp.exp(piece - top).astype(jnp.bfloat16)
         tops.append(top)
-    top = jnp.concatenate(tops, axis=0)
-    ones = jnp.ones((width, 128), jnp.bfloat16)
+    return jnp.concatenate(tops, axis=0)
+
+
+def _mix(weight_ref, values_ref, top):
+    ones = jnp.ones((weight_ref.shape[1], 128), jnp.bfloat16)
     low = lax.broadcasted_iota(jnp.int32, (BLOCK, 128), 1) < HD
     outs, sums, maxes = [], [], []
     for pair in range(2):
         base = pair * 256
         ext = jnp.concatenate([values_ref[:, pair * 128 : (pair + 1) * 128], ones], axis=1)
-        res = _dot(weight_ref[base : base + 256, :width], ext)
+        res = _dot(weight_ref[base : base + 256, :], ext)
         outs.append(jnp.where(low, res[:BLOCK, :128], res[BLOCK:, :128]))
         sums.append(jnp.where(low, res[:BLOCK, 128:], res[BLOCK:, 128:]))
         maxes.append(jnp.where(low, top[base : base + BLOCK], top[base + BLOCK : base + 256]))
@@ -338,30 +361,37 @@
     )
     near = PICKS * BLOCK
 
-    def project(p):
-        fetch.wait(("w", 0, p), ("w", D, p))
-        both = [_dot(rows_ref[...], wkv_ref[:, _tile(p, base)]) for base in (0, D)]
-        for full, ref in zip(both, (keys_ref, values_ref)):
-            full = full.reshape(SHARDS, SUBS, SUB, TILE)
-            ref[p % 2, :near] = full[:, :PICKS].reshape(near, TILE).astype(jnp.bfloat16)
-            ref[p % 2, near : near + BLOCK] = full[:, 2 * PICKS].reshape(BLOCK, TILE).astype(jnp.bfloat16)
-            ref[p % 2, near + BLOCK :] = full[:, PICKS : 2 * PICKS].reshape(near, TILE).astype(jnp.bfloat16)
-
-    project(0)
-    fetch.wait("q")
+    def keep(full, ref, p):
+        full = full.reshape(SHARDS, SUBS, SUB, TILE)
+        ref[p % 2, :near] = full[:, :PICKS].reshape(near, TILE).astype(jnp.bfloat16)
+        ref[p % 2, near : near + BLOCK] = full[:, 2 * PICKS].reshape(BLOCK, TILE).astype(jnp.bfloat16)
+        ref[p % 2, near + BLOCK :] = full[:, PICKS : 2 * PICKS].reshape(near, TILE).astype(jnp.bfloat16)
+
+    def project(p, base):
+        return _dot(rows_ref[...], wkv_ref[:, _tile(p, base)])
+
+    fetch.wait(("w", 0, 0), ("w", D, 0))
+    both = [project(0, 0), project(0, D)]
+    keep(both[0], keys_ref, 0)
+    keep(both[1], values_ref, 0)
+    fetch.wait("q", "o", "l", "m")
+    halves = [(slice(b * BLOCK, (b + 1) * BLOCK), pl.ds(b * near, near + BLOCK)) for b in range(2)]
     for p in range(STEPS):
         at = _tile(p)
-        if p + 1 < STEPS:
-            project(p + 1)
-        if p == 0:
-            fetch.wait("o", "l", "m")
+        more = p + 1 < STEPS
+        if more:
+            fetch.wait(("w", 0, p + 1), ("w", D, p + 1))
+        for b, (rows, used) in enumerate(halves):
+            scores_ref[b] = _scores(q_ref[rows, at], keys_ref[p % 2, used])
+        if more:
+            both = [project(p + 1, 0), project(p + 1, D)]
+            keep(both[0], keys_ref, p + 1)
+            keep(both[1], values_ref, p + 1)
+        tops = []
         for b in range(2):
-            rows = slice(b * BLOCK, (b + 1) * BLOCK)
-            used = pl.ds(b * near, near + BLOCK)
-            far = _stage(
-                q_ref[rows, at], keys_ref.at[p % 2, used], values_ref.at[p % 2, used],
-                scores_ref.at[b], weight_ref.at[b], bias_ref[2 + b : 3 + b, :],
-            )
+            tops.append(_soften(scores_ref.at[b], weight_ref.at[b], bias_ref[2 + b : 3 + b, :]))
+        for b, (rows, used) in enumerate(halves):
+            far = _mix(weight_ref.at[b], values_ref.at[p % 2, used], tops[b])
             out, total, _ = _join((o_ref[rows, at], l_ref[rows, at], m_ref[rows, at]), far)
             context_ref[rows, at] = (out / total).astype(jnp.bfloat16)
     fetch.wait("wo")

time: 94.2 us -> 94.2 us (level)
    pallas_call x1, Pallas kernels: 16.4 us -> 14.7 us  [late(): pl.pallas_call(_late_kernel, out_shape=jax.ShapeDtypeStruct((64, D), jnp....]
    pallas_call x1, Pallas kernels: 1.49 us -> 2.9 us  [pack(): pl.pallas_call(_pack_kernel, out_shape=jax.ShapeDtypeStruct(shape, jnp.bf...]
where the time goes in v9:
time: 94.2 us; the launch traced here: 92.9 us
  Pallas kernels  38.1 us (40%)
  blocking collectives  22.9 us (24%)
  waiting for transfers between devices  18.8 us (20%)
  starting transfers between devices  11 us (12%)
  local copies, waits for them, and re-layouts  1.37 us (1%)
    all_to_all x1, blocking collectives, exchange(): return lax.all_to_all(value, 'tm', split_axis=0, concat_axis=0, tiled=True)  22.9 us
    ppermute x1, waiting for transfers between devices, program(): lo = lax.ppermute(frames[BLOCK:], 'tm', up)  18.1 us
    pallas_call x1, Pallas kernels, late(): pl.pallas_call(_late_kernel, out_shape=jax.ShapeDtypeStruct((64, D), jnp....  14.7 us
    pallas_call x1, Pallas kernels, halo_part(): pl.pallas_call(_halo_kernel, grid=(STEPS,), out_shape=(f32, f32, f32), in...  10.6 us
    pallas_call x1, Pallas kernels, own_part(): pl.pallas_call(_own_kernel, grid=(STEPS,), out_shape=(half, half, half, j...  8.27 us
    all_to_all x1, starting transfers between devices, exchange(): return lax.all_to_all(value, 'tm', split_axis=0, concat_axis=0, tiled=True)  5.12 us
    ppermute x1, starting transfers between devices, program(): lo = lax.ppermute(frames[BLOCK:], 'tm', up)  3.37 us
    pallas_call x1, Pallas kernels, pack(): pl.pallas_call(_pack_kernel, out_shape=jax.ShapeDtypeStruct(shape, jnp.bf...  2.9 us
  transfers between devices with their start and end apart: 3, of which 2 were waited for; matrix products, arithmetic and copies ran while one was open for 1% of the time, Pallas kernels for 20%

profile of v9, /device:TPU:2, one launch (start us, length us, event | category | flops | bytes accessed | tf_op | source)
XLA Modules:
  0.0 92.9 jit_solution(8392468558494800596)
XLA Ops:
  0.0 2.9 %pack.1 = bf16[16,31,8,128]{3,2,1,0:T(8,128)(2,1)} custom-call(s32[1]{0:T(128)} %bitcast.rank_ref, s32[2,3]{1,0:T(2,128)} %owner_ref.3, s32[2,3]{1,0:T(2,128)} %slot_ref.3, s32[1,128]{1,0:T(1,128)} %bitcast.4, bf16[256,1280]{1,0:T(8,128)(2,1)} %own_ref.1), custom_call_target="tpu_custom_call" | custom-call | tf_op jit(solution)/shard_map/pack/pallas_call | solution.py:70
  2.9 22.9 %all_to_all.10.held_ref = bf16[16,31,8,128]{3,2,1,0:T(8,128)(2,1)S(1)} all-to-all(bf16[16,31,8,128]{3,2,1,0:T(8,128)(2,1)} %pack.1), channel_id=1, replica_groups=mesh['rec'=16,'tm'=16] {'tm'}, dimensions={0} | all-to-all | bytes 2031616 | tf_op jit(solution)/shard_map/all_to_all | solution.py:435
  25.8 1.7 %select.1 = bf16[16,7,8,1280]{3,2,1,0:T(8,128)(2,1)} custom-call(bf16[16,31,8,128]{3,2,1,0:T(8,128)(2,1)S(1)} %all_to_all.10.held_ref), custom_call_target="tpu_custom_call" | custom-call | tf_op jit(solution)/shard_map/select/pallas_call | solution.py:121
  27.5 0.0 copy-start
  27.5 0.0 copy-start.1
  27.5 5.1 %all-to-all-start.1 = ((bf16[16,7,8,1280]{3,2,1,0:T(8,128)(2,1)}), bf16[16,7,8,1280]{3,2,1,0:T(8,128)(2,1)S(1)}, u32[]{:S(2)}, u32[]{:S(2)}) async-start(bf16[16,7,8,1280]{3,2,1,0:T(8,128)(2,1)} %select.1), calls=%async_computation.1 | async-start | bytes 4587520 | tf_op jit(solution)/shard_map/all_to_all | solution.py:435
  32.7 0.0 copy-done
  32.7 0.8 fusion
  33.4 3.4 %collective-permute-start = (bf16[128,1280]{1,0:T(8,128)(2,1)}, bf16[128,1280]{1,0:T(8,128)(2,1)S(1)}, u32[]{:S(2)}, u32[]{:S(2)}) collective-permute-start(bf16[128,1280]{1,0:T(8,128)(2,1)} %get-tuple-element.20), channel_id=1, source_target_pairs={{0,1},{1,2},{2,3},{3,4},{4,5},{5,6},{6,7},{7,8},{8,9},{9,10},{10,1... | collective-permute-start | bytes 983048 | tf_op jit(solution)/shard_map/ppermute | solution.py:448
  36.8 2.5 %collective-permute-start.1 = (bf16[128,1280]{1,0:T(8,128)(2,1)S(1)}, bf16[128,1280]{1,0:T(8,128)(2,1)S(1)}, u32[]{:S(2)}, u32[]{:S(2)}) collective-permute-start(bf16[128,1280]{1,0:T(8,128)(2,1)S(1)} %get-tuple-element.19), channel_id=1, source_target_pairs={{1,0},{2,1},{3,2},{4,3},{5,4},{6,5},{7,6},{8,7},{9,8},{10,9},{11,1... | collective-permute-start | bytes 983048 | tf_op jit(solution)/shard_map/ppermute | solution.py:449
  39.9 0.0 copy-done.1
  40.0 0.6 reshape.15.gain_ref
  40.5 8.3 %own.1 = (bf16[256,1280]{1,0:T(8,128)(2,1)}, bf16[256,1280]{1,0:T(8,128)(2,1)}, bf16[256,1280]{1,0:T(8,128)(2,1)}, f32[8,512]{1,0:T(8,128)}) custom-call(s32[1]{0:T(128)} %bitcast.rank_ref, s32[1]{0:T(128)S(6)} %copy.10.len_ref, s32[2,3]{1,0:T(2,128)} %owner_ref.3, s32[2,3]{1,0:T(2,128)} %slot_ref.3, s32[1,128]{1,0:T(1,128)} %bitcast.5, ...), custom_call_target="tpu_custom_call" | custom-call | tf_op jit(solution)/shard_map/own/pallas_call | solution.py:243
  48.8 18.1 %collective-permute-done.lo_ref = bf16[128,1280]{1,0:T(8,128)(2,1)S(1)} collective-permute-done((bf16[128,1280]{1,0:T(8,128)(2,1)}, bf16[128,1280]{1,0:T(8,128)(2,1)S(1)}, u32[]{:S(2)}, u32[]{:S(2)}) %collective-permute-start) | collective-permute-done | bytes 327712 | tf_op jit(solution)/shard_map/ppermute | solution.py:448
  67.0 0.7 collective-permute-done.1.hi_ref
  67.6 10.6 %halo.1 = (f32[256,1280]{1,0:T(8,128)}, f32[256,1280]{1,0:T(8,128)}, f32[256,1280]{1,0:T(8,128)}) custom-call(bf16[128,1280]{1,0:T(8,128)(2,1)S(1)} %collective-permute-done.lo_ref, bf16[128,1280]{1,0:T(8,128)(2,1)S(1)} %collective-permute-done.1.hi_ref, f32[8,512]{1,0:T(8,128)} %get-tuple-element.12.bias_ref, ...), custom_call_target="tpu_custom_call" | custom-call | tf_op jit(solution)/shard_map/halo/pallas_call | solution.py:258
  78.2 0.0 all-to-all-done.1
  78.2 14.7 %late.1 = bf16[64,1280]{1,0:T(8,128)(2,1)} custom-call(s32[1]{0:T(128)} %bitcast.rank_ref, s32[1]{0:T(128)S(6)} %copy.10.len_ref, bf16[896,1280]{1,0:T(8,128)(2,1)S(1)} %bitcast.3, f32[8,512]{1,0:T(8,128)} %get-tuple-element.12.bias_ref, bf16[256,1280]{1,0:T(8,128)(2,1)} %get-tuple-element.13.q_ref.q_hbm, f32[256,1280]{1,0:T(8,128)} %get-tuple-element.16.o_hbm, ...), custom_call_target="tpu_custom_call" | custom-call | tf_op jit(solution)/shard_map/late/pallas_call | solution.py:407
Async XLA Ops:
  27.5 5.1 %copy-start = (bf16[256,1280]{1,0:T(8,128)(2,1)S(1)}, bf16[256,1280]{1,0:T(8,128)(2,1)}, u32[]{:S(2)}) copy-start(bf16[256,1280]{1,0:T(8,128)(2,1)} %own_ref.1) | copy-start | bytes 1966084
  27.5 12.4 %copy-start.1 = (f32[1280]{0:T(1024)S(1)}, f32[1280]{0:T(1024)}, u32[]{:S(2)}) copy-start(f32[1280]{0:T(1024)} %param.13) | copy-start | bytes 15364
  27.5 50.7 %all-to-all-start.1 = ((bf16[16,7,8,1280]{3,2,1,0:T(8,128)(2,1)}), bf16[16,7,8,1280]{3,2,1,0:T(8,128)(2,1)S(1)}, u32[]{:S(2)}, u32[]{:S(2)}) async-start(bf16[16,7,8,1280]{3,2,1,0:T(8,128)(2,1)} %select.1), calls=%async_computation.1 | async-start | bytes 4587520 | tf_op jit(solution)/shard_map/all_to_all | solution.py:435
  33.4 33.5 %collective-permute-start = (bf16[128,1280]{1,0:T(8,128)(2,1)}, bf16[128,1280]{1,0:T(8,128)(2,1)S(1)}, u32[]{:S(2)}, u32[]{:S(2)}) collective-permute-start(bf16[128,1280]{1,0:T(8,128)(2,1)} %get-tuple-element.20), channel_id=1, source_target_pairs={{0,1},{1,2},{2,3},{3,4},{4,5},{5,6},{6,7},{7,8},{8,9},{9,10},{10,1... | collective-permute-start | bytes 983048 | tf_op jit(solution)/shard_map/ppermute | solution.py:448
  36.8 30.8 %collective-permute-start.1 = (bf16[128,1280]{1,0:T(8,128)(2,1)S(1)}, bf16[128,1280]{1,0:T(8,128)(2,1)S(1)}, u32[]{:S(2)}, u32[]{:S(2)}) collective-permute-start(bf16[128,1280]{1,0:T(8,128)(2,1)S(1)} %get-tuple-element.19), channel_id=1, source_target_pairs={{1,0},{2,1},{3,2},{4,3},{5,4},{6,5},{7,6},{8,7},{9,8},{10,9},{11,1... | collective-permute-start | bytes 983048 | tf_op jit(solution)/shard_map/ppermute | solution.py:449
